TPU v7x, 32 devices: a whole 2x2x4 slice. The times are simulated.
32 devices in a mesh: twin: 2 (over x), dp: 16 (over z, y, core).
Axes of the slice: x: 2, y: 2, z: 4, core: 2. Of those that a mesh axis runs over, the one named last changes fastest.
Arguments:
- hidden: bfloat16 [64, 512, 768], P(('twin', 'dp')), may hold values from -6 to 6
- segment_ids: int32 [64, 512], P(('twin', 'dp')), may hold values from 0 to 7, never falling along the last dimension, each value on 1 to 128 neighbouring positions
- targets: int32 [256], replicated, may hold values from 0 to 255, each once
- w_qkv: bfloat16 [768, 2304], replicated, may hold values from -0.21875 to 0.21875
- b_query: bfloat16 [768], replicated, may hold values from -3 to 3
- b_value: bfloat16 [768], replicated, may hold values from -3 to 3
- w_out: bfloat16 [768, 768], replicated, may hold values from -1.25 to 1.25
- b_out: bfloat16 [768], replicated, may hold values from -3 to 3
- ln1_gain: bfloat16 [768], replicated, may hold values from 0.5 to 1.5
- ln1_bias: bfloat16 [768], replicated, may hold values from -2 to 2
- w_in: bfloat16 [768, 3072], replicated, may hold values from -0.21875 to 0.21875
- b_in: bfloat16 [3072], replicated, may hold values from -3 to 3
- w_down: bfloat16 [3072, 768], replicated, may hold values from -0.109375 to 0.109375
- b_down: bfloat16 [768], replicated, may hold values from -3 to 3
- ln2_gain: bfloat16 [768], replicated, may hold values from 0.5 to 1.5
- ln2_bias: bfloat16 [768], replicated, may hold values from -0.29882812 to 0.29882812
Outputs:
- losses: float32 [256], P(('twin', 'dp'))
- hidden_grad: bfloat16 [64, 512, 768], P(('twin', 'dp'))
- grad_w_qkv: float32 [768, 2304], P('dp')
- grad_b_query: float32 [768], P('dp')
- grad_b_value: float32 [768], P('dp')
- grad_w_out: float32 [768, 768], P('dp')
- grad_b_out: float32 [768], P('dp')
- grad_ln1_gain: float32 [768], P('dp')
- grad_ln1_bias: float32 [768], P('dp')
- grad_w_in: float32 [768, 3072], P('dp')
- grad_b_in: float32 [3072], P('dp')
- grad_w_down: float32 [3072, 768], P('dp')
- grad_b_down: float32 [768], P('dp')
- grad_ln2_gain: float32 [768], P('dp')
- grad_ln2_bias: float32 [768], P('dp')
Inputs may be any that keep to these rules, and one draw needn't show every extreme that they name: `segment_ids`: in each row the ids never fall; every id of 0 to 7 occurs, on 1 to 128 tokens. `targets`: every positive is the target of exactly one anchor.
All inputs are finite; a program needn't handle non-finite values.
Results may differ from a plain program's by a relative error of at most 0.012.
Values may be sent and summed in bfloat16 or wider, within the bound.
No kernel may reach another device: no remote copies, remote signals or barrier semaphores. Data moves between devices by JAX's collectives and lax.ppermute only.
A program may use at most 192 MiB of HBM per device.

v0:
```python
import jax
import jax.numpy as jnp
from jax import lax
from jax.sharding import PartitionSpec as P

D = 768
HEADS = 12
HEAD_DIM = 64
SEG = 8


cosine_scale = 64.0
loss_scale = 32.0
norm_epsilon = 1e-12
unit_epsilon = 1e-06
masked_score = -1e30


def layer_norm(inputs, norm_gain, norm_shift):
    middle = jnp.mean(inputs, axis=-1, keepdims=True)
    centered = inputs - middle
    spread = jnp.mean(centered * centered, axis=-1, keepdims=True)
    return centered * lax.rsqrt(spread + norm_epsilon) * norm_gain + norm_shift


def gelu_exact(inputs):
    return 0.5 * inputs * (1.0 + lax.erf(inputs * 0.5**0.5))


def contract_rows(left, right):
    return lax.dot_general(
        left, right, (((0,), (0,)), ((), ())), preferred_element_type=jnp.float32
    )


def contract_cols(left, right):
    return lax.dot_general(
        left, right, (((1,), (1,)), ((), ())), preferred_element_type=jnp.float32
    )


def split_heads(row_qkv):
    length = row_qkv.shape[0]
    query_heads = row_qkv[:, :D].reshape(length, HEADS, HEAD_DIM)
    key_heads = row_qkv[:, D : 2 * D].reshape(length, HEADS, HEAD_DIM)
    value_heads = row_qkv[:, 2 * D :].reshape(length, HEADS, HEAD_DIM)
    return (query_heads, key_heads, value_heads)


def masked_scores(query_heads, key_heads, row_seg):
    scores = jnp.einsum(
        "qhd,khd->hqk", query_heads, key_heads, preferred_element_type=jnp.float32
    ) * HEAD_DIM ** (-0.5)
    same_doc = (row_seg[:, None] == row_seg[None, :])[None]
    return (jnp.where(same_doc, scores, masked_score), same_doc)


def rank_loss(sims, wanted):
    row_top = jnp.max(sims, axis=1, keepdims=True)
    weights = jnp.exp(sims - row_top)
    row_total = jnp.sum(weights, axis=1, keepdims=True)
    column = lax.broadcasted_iota(jnp.int32, sims.shape, 1)
    target_hit = column == wanted[:, None]
    picked = jnp.sum(jnp.where(target_hit, sims, 0.0), axis=1)
    losses = row_top[:, 0] + jnp.log(row_total[:, 0]) - picked
    slope = (loss_scale * (weights / row_total - target_hit.astype(jnp.float32))).astype(
        jnp.bfloat16
    )
    return (losses, slope)


def body(
    hidden,
    segment_ids,
    targets,
    w_qkv,
    b_query,
    b_value,
    w_out,
    b_out,
    ln1_gain,
    ln1_bias,
    w_in,
    b_in,
    w_down,
    b_down,
    ln2_gain,
    ln2_bias,
):
    row_count, length, width = hidden.shape
    token_count = row_count * length
    tokens = hidden.reshape(token_count, width)
    bias_qkv = jnp.concatenate(
        [b_query.astype(jnp.float32), jnp.zeros((width,), jnp.float32), b_value.astype(jnp.float32)]
    )
    qkv_all = (jnp.dot(tokens, w_qkv, preferred_element_type=jnp.float32) + bias_qkv).astype(
        jnp.bfloat16
    )
    qkv_rows = qkv_all.reshape(row_count, length, 3 * width)

    def attend_forward(row_pack):
        row_qkv, row_seg = row_pack
        query_heads, key_heads, value_heads = split_heads(row_qkv)
        scores, same_doc = masked_scores(query_heads, key_heads, row_seg)
        row_top = jnp.max(scores, axis=-1, keepdims=True)
        weights = jnp.exp(scores - row_top)
        row_total = jnp.sum(weights, axis=-1, keepdims=True)
        prob_rows = (weights / row_total).astype(jnp.bfloat16)
        context = jnp.einsum(
            "hqk,khd->qhd", prob_rows, value_heads, preferred_element_type=jnp.float32
        )
        return (context.reshape(length, width).astype(jnp.bfloat16), row_top + jnp.log(row_total))

    context, log_total = lax.map(attend_forward, (qkv_rows, segment_ids))
    context_flat = context.reshape(token_count, width)
    attended = jnp.dot(context_flat, w_out, preferred_element_type=jnp.float32) + b_out.astype(
        jnp.float32
    )
    normed_one, norm_one_back = jax.vjp(
        layer_norm,
        tokens.astype(jnp.float32) + attended,
        ln1_gain.astype(jnp.float32),
        ln1_bias.astype(jnp.float32),
    )
    normed_low = normed_one.astype(jnp.bfloat16)
    hidden_pre = jnp.dot(normed_low, w_in, preferred_element_type=jnp.float32) + b_in.astype(
        jnp.float32
    )
    active, gelu_back = jax.vjp(gelu_exact, hidden_pre)
    active_low = active.astype(jnp.bfloat16)
    branch = jnp.dot(active_low, w_down, preferred_element_type=jnp.float32) + b_down.astype(
        jnp.float32
    )
    output, norm_two_back = jax.vjp(
        layer_norm, normed_one + branch, ln2_gain.astype(jnp.float32), ln2_bias.astype(jnp.float32)
    )
    member = (segment_ids[:, None, :] == jnp.arange(SEG, dtype=jnp.int32)[None, :, None]).astype(
        jnp.float32
    )
    counts = jnp.sum(member, axis=2, keepdims=True)

    def pool_units(out_rows):
        pooled = (
            jnp.einsum("rsl,rld->rsd", member, out_rows, precision=lax.Precision.HIGHEST) / counts
        )
        unit_rows = pooled * lax.rsqrt(
            jnp.mean(pooled * pooled, axis=-1, keepdims=True) + unit_epsilon
        )
        return unit_rows.reshape(row_count * SEG, width)

    unit_rows, pool_back = jax.vjp(pool_units, output.reshape(row_count, length, width))
    unit_low = unit_rows.astype(jnp.bfloat16)
    gathered = lax.all_gather(unit_low, ("twin", "dp"), axis=0, tiled=True)
    anchor_count = gathered.shape[0] // 2
    anchors = gathered[:anchor_count]
    positives = gathered[anchor_count:]
    factor = cosine_scale / width
    devices = lax.axis_size(("twin", "dp"))
    loss_share = anchor_count // devices
    loss_start = lax.axis_index(("twin", "dp")) * loss_share
    all_losses, slope = rank_loss(contract_cols(anchors, positives) * factor, targets)
    losses = lax.dynamic_slice_in_dim(all_losses, loss_start, loss_share, 0)
    sentences = unit_low.shape[0]
    offset = lax.axis_index("dp") * sentences
    anchor_rows = (
        jnp.dot(
            lax.dynamic_slice_in_dim(slope, offset, sentences, 0),
            positives,
            preferred_element_type=jnp.float32,
        )
        * factor
    )
    positive_rows = (
        contract_rows(lax.dynamic_slice_in_dim(slope, offset, sentences, 1), anchors) * factor
    )
    unit_grad = jnp.where(lax.axis_index("twin") == 0, anchor_rows, positive_rows)
    grad_output = pool_back(unit_grad)[0].reshape(token_count, width)
    grad_sum_two, grad_ln2_gain, grad_ln2_bias = norm_two_back(grad_output)
    grad_branch = grad_sum_two.astype(jnp.bfloat16)
    grad_w_down = contract_rows(active_low, grad_branch)
    grad_b_down = jnp.sum(grad_branch, axis=0, dtype=jnp.float32)
    grad_active = contract_cols(grad_branch, w_down)
    grad_pre = gelu_back(grad_active)[0].astype(jnp.bfloat16)
    grad_w_in = contract_rows(normed_low, grad_pre)
    grad_b_in = jnp.sum(grad_pre, axis=0, dtype=jnp.float32)
    grad_normed = contract_cols(grad_pre, w_in) + grad_sum_two
    grad_sum_one, grad_ln1_gain, grad_ln1_bias = norm_one_back(grad_normed)
    grad_attended = grad_sum_one.astype(jnp.bfloat16)
    grad_w_out = contract_rows(context_flat, grad_attended)
    grad_b_out = jnp.sum(grad_attended, axis=0, dtype=jnp.float32)
    grad_context = (
        contract_cols(grad_attended, w_out).astype(jnp.bfloat16).reshape(row_count, length, width)
    )

    def attend_backward(row_pack):
        row_qkv, row_seg, row_lse, row_grad = row_pack
        query_heads, key_heads, value_heads = split_heads(row_qkv)
        scores, same_doc = masked_scores(query_heads, key_heads, row_seg)
        prob_rows = jnp.where(same_doc, jnp.exp(scores - row_lse), 0.0)
        grad_heads = row_grad.reshape(length, HEADS, HEAD_DIM)
        grad_value = jnp.einsum(
            "hqk,qhd->khd",
            prob_rows.astype(jnp.bfloat16),
            grad_heads,
            preferred_element_type=jnp.float32,
        )
        grad_prob = jnp.einsum(
            "qhd,khd->hqk", grad_heads, value_heads, preferred_element_type=jnp.float32
        )
        inner = jnp.sum(prob_rows * grad_prob, axis=-1, keepdims=True)
        grad_scores = (prob_rows * (grad_prob - inner)).astype(jnp.bfloat16)
        grad_query = jnp.einsum(
            "hqk,khd->qhd", grad_scores, key_heads, preferred_element_type=jnp.float32
        ) * HEAD_DIM ** (-0.5)
        grad_key = jnp.einsum(
            "hqk,qhd->khd", grad_scores, query_heads, preferred_element_type=jnp.float32
        ) * HEAD_DIM ** (-0.5)
        return jnp.concatenate(
            [
                grad_query.reshape(length, width),
                grad_key.reshape(length, width),
                grad_value.reshape(length, width),
            ],
            axis=1,
        ).astype(jnp.bfloat16)

    grad_qkv = lax.map(attend_backward, (qkv_rows, segment_ids, log_total, grad_context))
    grad_qkv = grad_qkv.reshape(token_count, 3 * width)
    grad_w_qkv = contract_rows(tokens, grad_qkv)
    grad_b_query = jnp.sum(grad_qkv[:, :width], axis=0, dtype=jnp.float32)
    grad_b_value = jnp.sum(grad_qkv[:, 2 * width :], axis=0, dtype=jnp.float32)
    hidden_grad = (
        (contract_cols(grad_qkv, w_qkv) + grad_sum_one)
        .astype(jnp.bfloat16)
        .reshape(row_count, length, width)
    )
    (
        grad_w_qkv,
        grad_b_query,
        grad_b_value,
        grad_w_out,
        grad_b_out,
        grad_ln1_gain,
        grad_ln1_bias,
        grad_w_in,
        grad_b_in,
        grad_w_down,
        grad_b_down,
        grad_ln2_gain,
        grad_ln2_bias,
    ) = (
        lax.psum_scatter(grad_w_qkv, "dp", scatter_dimension=0, tiled=True),
        lax.psum_scatter(grad_b_query, "dp", scatter_dimension=0, tiled=True),
        lax.psum_scatter(grad_b_value, "dp", scatter_dimension=0, tiled=True),
        lax.psum_scatter(grad_w_out, "dp", scatter_dimension=0, tiled=True),
        lax.psum_scatter(grad_b_out, "dp", scatter_dimension=0, tiled=True),
        lax.psum_scatter(grad_ln1_gain, "dp", scatter_dimension=0, tiled=True),
        lax.psum_scatter(grad_ln1_bias, "dp", scatter_dimension=0, tiled=True),
        lax.psum_scatter(grad_w_in, "dp", scatter_dimension=0, tiled=True),
        lax.psum_scatter(grad_b_in, "dp", scatter_dimension=0, tiled=True),
        lax.psum_scatter(grad_w_down, "dp", scatter_dimension=0, tiled=True),
        lax.psum_scatter(grad_b_down, "dp", scatter_dimension=0, tiled=True),
        lax.psum_scatter(grad_ln2_gain, "dp", scatter_dimension=0, tiled=True),
        lax.psum_scatter(grad_ln2_bias, "dp", scatter_dimension=0, tiled=True),
    )
    (
        grad_w_qkv,
        grad_b_query,
        grad_b_value,
        grad_w_out,
        grad_b_out,
        grad_ln1_gain,
        grad_ln1_bias,
        grad_w_in,
        grad_b_in,
        grad_w_down,
        grad_b_down,
        grad_ln2_gain,
        grad_ln2_bias,
    ) = (
        lax.psum(grad_w_qkv.astype(jnp.bfloat16), "twin").astype(jnp.float32),
        lax.psum(grad_b_query.astype(jnp.bfloat16), "twin").astype(jnp.float32),
        lax.psum(grad_b_value.astype(jnp.bfloat16), "twin").astype(jnp.float32),
        lax.psum(grad_w_out.astype(jnp.bfloat16), "twin").astype(jnp.float32),
        lax.psum(grad_b_out.astype(jnp.bfloat16), "twin").astype(jnp.float32),
        lax.psum(grad_ln1_gain.astype(jnp.bfloat16), "twin").astype(jnp.float32),
        lax.psum(grad_ln1_bias.astype(jnp.bfloat16), "twin").astype(jnp.float32),
        lax.psum(grad_w_in.astype(jnp.bfloat16), "twin").astype(jnp.float32),
        lax.psum(grad_b_in.astype(jnp.bfloat16), "twin").astype(jnp.float32),
        lax.psum(grad_w_down.astype(jnp.bfloat16), "twin").astype(jnp.float32),
        lax.psum(grad_b_down.astype(jnp.bfloat16), "twin").astype(jnp.float32),
        lax.psum(grad_ln2_gain.astype(jnp.bfloat16), "twin").astype(jnp.float32),
        lax.psum(grad_ln2_bias.astype(jnp.bfloat16), "twin").astype(jnp.float32),
    )
    return (
        losses,
        hidden_grad,
        grad_w_qkv,
        grad_b_query,
        grad_b_value,
        grad_w_out,
        grad_b_out,
        grad_ln1_gain,
        grad_ln1_bias,
        grad_w_in,
        grad_b_in,
        grad_w_down,
        grad_b_down,
        grad_ln2_gain,
        grad_ln2_bias,
    )


def solution(mesh):
    placed = (
        P(("twin", "dp"), None, None),
        P(("twin", "dp"), None),
        P(),
        P(),
        P(),
        P(),
        P(),
        P(),
        P(),
        P(),
        P(),
        P(),
        P(),
        P(),
        P(),
        P(),
    )
    return jax.shard_map(
        body,
        mesh=mesh,
        in_specs=placed,
        out_specs=(
            P(("twin", "dp")),
            P(("twin", "dp"), None, None),
            P("dp", None),
            P("dp"),
            P("dp"),
            P("dp", None),
            P("dp"),
            P("dp"),
            P("dp"),
            P("dp", None),
            P("dp"),
            P("dp", None),
            P("dp"),
            P("dp"),
            P("dp"),
        ),
        check_vma=False,
    )
```

profile of v0, /device:TPU:0, one launch (start us, length us, event | category | flops | bytes accessed | tf_op | source)
XLA Modules:
  0.0 668.2 jit_solution(16013698214673223419)
XLA Ops:
  9.2 7.3 %add_convert_fusion.1 = bf16[1024,2304]{1,0:T(8,128)(2,1)} fusion(bf16[1024,768]{1,0:T(8,128)(2,1)} %bitcast.178, bf16[768,2304]{1,0:T(8,128)(2,1)S(1)} %copy-done, f32[2304]{0:T(1024)S(1)} %pad_maximum_fusion), kind=kOutput, calls=%fused_computation.35 | convolution fusion | flops 3628597248 | bytes 9839616 | tf_op jit(solution)/shard_map/dot_general | solution.py:96
  16.5 6.7 copy.53
  23.8 38.7 %while.22 = (s32[]{:T(128)}, bf16[2,512,768]{2,1,0:T(8,128)(2,1)}, f32[2,12,512,1]{2,1,3,0:T(8,128)}, bf16[2,512,2304]{1,2,0:T(8,128)(2,1)}, s32[2,512]{1,0:T(2,128)S(1)}, /*index=5*/s32[]{:T(128)}) while((s32[]{:T(128)}, bf16[2,512,768]{2,1,0:T(8,128)(2,1)}, f32[2,12,512,1]{2,1,3,0:T(8,128)}, bf16[2,512,2304]{1,2,0:T(8,128)(2,1)}, ...), condition=%wide.region_3.4_spmd, body=%wide.region_0.3_spmd.sunk | while | flops 843704320 | bytes 55786600 | solution.py:114
  23.8 1.8 dynamic-slice_bitcast_fusion.6
  27.0 2.1 fusion.115
  29.1 3.5 fusion.116
  33.3 5.5 fusion.117
  38.8 2.3 copy.70
  41.1 2.1 constant_dynamic-update-slice_fusion.2
  43.2 1.8 dynamic-slice_bitcast_fusion.6
  46.3 2.1 fusion.115
  48.5 3.5 fusion.116
  52.6 5.5 fusion.117
  58.2 2.3 copy.70
  60.5 2.1 constant_dynamic-update-slice_fusion.2
  62.6 3.9 fusion.49
  67.8 9.7 %multiply_convert_fusion.3 = (bf16[1024,3072]{1,0:T(8,128)(2,1)S(1)}, f32[1024,3072]{1,0:T(8,128)}) fusion(f32[3072]{0:T(1024)S(1)} %convert_element_type.203, bf16[768,3072]{1,0:T(8,128)(2,1)S(1)} %bitcast.177, f32[1024,768]{1,0:T(8,128)S(1)} %get-tuple-element.228, f32[768]{0:T(1024)S(1)} %convert_element_type.201, f32[768]{0:T(1024)S(1)} %convert_element_type.200, ...), kind=kOutput, calls=%fused_computation.33 | convolution fusion | flops 4854644736 | bytes 26765312 | tf_op jit(solution)/shard_map/dot_general | solution.py:126
  77.6 5.5 fusion.50
  86.9 45.3 %all_gather.3 = bf16[512,768]{1,0:T(8,128)(2,1)S(1)} all-gather(bf16[16,768]{1,0:T(8,128)(2,1)S(1)} %fusion.29), channel_id=1, replica_groups=mesh['twin'=2,'dp'=16] {'twin','dp'}, dimensions={0}, use_global_device_ids=true | all-gather | bytes 811008 | tf_op jit(solution)/shard_map/all_gather | solution.py:153
  138.8 2.9 fusion.52
  143.3 1.8 fusion.46
  146.0 15.0 %convert_reduce_fusion = (f32[3072]{0:T(1024)}, bf16[1024,3072]{1,0:T(8,128)(2,1)S(1)}) fusion(bf16[1024,768]{1,0:T(8,128)(2,1)S(1)} %get-tuple-element.210, bf16[3072,768]{1,0:T(8,128)(2,1)S(1)} %bitcast.175, f32[1024,3072]{1,0:T(8,128)} %get-tuple-element.230, f32[3072]{0:T(1024)S(1)} %copy-done.46), kind=kOutput, calls=%fused_computation.31 | convolution fusion | flops 4882166784 | bytes 25190400 | tf_op jit(solution)/shard_map/dot_general | solution.py:37
  161.1 11.3 %multiply_reduce_fusion.1 = (f32[768]{0:T(1024)}, f32[1024]{0:T(1024)S(1)}, f32[768]{0:T(1024)}, f32[1024,768]{1,0:T(8,128)S(1)}) fusion(f32[1024,768]{1,0:T(8,128)S(1)} %copy-done.9, f32[1024]{0:T(1024)S(1)} %fusion.36, f32[1024]{0:T(1024)S(1)} %broadcast_multiply_fusion.1, f32[768]{0:T(1024)S(1)} %convert_element_type.200, ...), kind=kOutput, calls=%fused_computation.43 | convolution fusion | flops 4839699456 | bytes 20472832 | tf_op jit(solution)/shard_map/dot_general | solution.py:37
  173.9 1.6 copy-done.12
  177.5 2.9 fusion.54
  180.4 4.3 convolution_convert_fusion
  184.8 85.4 %while.23 = (s32[]{:T(128)}, bf16[2,512,2304]{1,2,0:T(8,128)(2,1)}, bf16[2,512,2304]{1,2,0:T(8,128)(2,1)}, s32[2,512]{1,0:T(2,128)S(1)}, f32[2,12,512,1]{2,1,3,0...) while((s32[]{:T(128)}, bf16[2,512,2304]{1,2,0:T(8,128)(2,1)}, bf16[2,512,2304]{1,2,0:T(8,128)(2,1)}, ...), condition=%wide.region_20.21_spmd, body=%wide.region_18.20_spmd.sunk | while | flops 2079188992 | bytes 181877680 | solution.py:227
  185.0 1.9 dynamic-slice_bitcast_fusion.8
  187.9 6.4 fusion.129
  196.9 2.3 copy.71
  199.2 11.5 %multiply_reduce_fusion.9 = (f32[12,512]{1,0:T(8,128)S(1)}, f32[12,512,512]{1,2,0:T(8,128)}) fusion(f32[12,512]{1,0:T(8,128)} %dynamic-slice_bitcast_fusion.7, f32[12,512,512]{1,2,0:T(8,128)} %fusion.129, pred[512,512]{0,1:T(8,128)(4,1)} %broadcast_compare_fusion.5, bf16[512,12,64]{0,2,1:T(8,128)(2,1)} %bitcast.162, bf16[512,12,64]{0,2,1:T(8,128)(2,1)} %bitcast.160), kind=kOutput, calls=%fused_computation.15.clone.1 | convolution fusion | flops 421521408 | bytes 27049984 | tf_op jit(solution)/shard_map/while/body/eval_jaxpr/qhd,khd->hqk/dot_general | solution.py:207
  210.8 1.8 slice-done.2
  212.6 7.1 %multiply_convert_fusion.9 = bf16[12,512,512]{1,2,0:T(8,128)(2,1)S(1)} fusion(f32[12,512,512]{1,2,0:T(8,128)} %get-tuple-element.330, f32[12,512]{1,0:T(8,128)S(1)} %get-tuple-element.331, f32[12,512]{1,0:T(8,128)S(1)} %copy-done.15, f32[12,512,512]{1,2,0:T(8,128)S(1)} %bitcast.150, pred[512,512]{0,1:T(8,128)(4,1)S(1)} %copy-done.10), kind=kLoop, calls=%fused_computation.14.clone.1 | loop fusion | flops 22020096 | bytes 31768576 | tf_op jit(solution)/shard_map/while/body/eval_jaxpr/convert_element_type | solution.py:211
  220.9 2.0 multiply_convert_fusion.10
  222.9 3.2 fusion.130
  227.6 1.8 dynamic-slice_bitcast_fusion.8
  230.5 6.4 fusion.129
  239.4 2.3 copy.71
  241.8 11.5 %multiply_reduce_fusion.9 = (f32[12,512]{1,0:T(8,128)S(1)}, f32[12,512,512]{1,2,0:T(8,128)}) fusion(f32[12,512]{1,0:T(8,128)} %dynamic-slice_bitcast_fusion.7, f32[12,512,512]{1,2,0:T(8,128)} %fusion.129, pred[512,512]{0,1:T(8,128)(4,1)} %broadcast_compare_fusion.5, bf16[512,12,64]{0,2,1:T(8,128)(2,1)} %bitcast.162, bf16[512,12,64]{0,2,1:T(8,128)(2,1)} %bitcast.160), kind=kOutput, calls=%fused_computation.15.clone.1 | convolution fusion | flops 421521408 | bytes 27049984 | tf_op jit(solution)/shard_map/while/body/eval_jaxpr/qhd,khd->hqk/dot_general | solution.py:207
  253.3 1.6 slice-done.2
  254.9 7.1 %multiply_convert_fusion.9 = bf16[12,512,512]{1,2,0:T(8,128)(2,1)S(1)} fusion(f32[12,512,512]{1,2,0:T(8,128)} %get-tuple-element.330, f32[12,512]{1,0:T(8,128)S(1)} %get-tuple-element.331, f32[12,512]{1,0:T(8,128)S(1)} %copy-done.15, f32[12,512,512]{1,2,0:T(8,128)S(1)} %bitcast.150, pred[512,512]{0,1:T(8,128)(4,1)S(1)} %copy-done.10), kind=kLoop, calls=%fused_computation.14.clone.1 | loop fusion | flops 22020096 | bytes 31768576 | tf_op jit(solution)/shard_map/while/body/eval_jaxpr/convert_element_type | solution.py:211
  263.2 2.0 multiply_convert_fusion.10
  265.2 3.2 fusion.130
  268.4 1.6 maximum_dynamic-update-slice_fusion.2
  270.2 9.5 %convolution_bitcast_fusion = f32[768,2304]{0,1:T(8,128)} fusion(bf16[2,512,2304]{1,2,0:T(8,128)(2,1)} %get-tuple-element.77, bf16[2,512,768]{2,1,0:T(8,128)(2,1)} %param.20), kind=kOutput, calls=%fused_computation.36 | convolution fusion | flops 3623878656 | bytes 13369344 | tf_op jit(solution)/shard_map/dot_general | solution.py:31
  279.7 8.0 %copy.63 = f32[768,2304]{1,0:T(8,128)} copy(f32[768,2304]{0,1:T(8,128)} %convolution_bitcast_fusion) | data formatting | bytes 14155776
  288.5 11.4 %fusion.41 = f32[768,3072]{1,0:T(8,128)} fusion(bf16[1024,3072]{1,0:T(8,128)(2,1)} %copy-done.14, f32[1024,768]{1,0:T(8,128)} %copy-done.8, f32[768]{0:T(1024)S(1)} %copy-done.31, f32[768]{0:T(1024)S(1)} %copy-done.27, f32[1024]{0:T(1024)S(1)} %copy-done.24, f32[1024]{0:T(1024)S(1)} %copy-done.22), kind=kOutput, calls=%fused_computation.120 | convolution fusion | flops 4835770368 | bytes 18888704 | tf_op jit(solution)/shard_map/dot_general | solution.py:31
  299.9 10.2 %fusion.55 = f32[3072,768]{1,0:T(8,128)} fusion(bf16[1024,3072]{1,0:T(8,128)(2,1)} %copy-done.62, bf16[1024,768]{1,0:T(8,128)(2,1)} %copy-done.17), kind=kOutput, calls=%fused_computation.132 | convolution fusion | flops 4831838208 | bytes 17301504 | tf_op jit(solution)/shard_map/dot_general | solution.py:31
  310.2 7.0 %copy.57 = bf16[2,512,2304]{2,1,0:T(8,128)(2,1)} copy(bf16[2,512,2304]{1,2,0:T(8,128)(2,1)} %get-tuple-element.77) | data formatting | bytes 9437184 | tf_op jit(solution)/shard_map/while | solution.py:227
  319.1 3.0 convert_reduce_fusion.3
  322.1 61.8 %all-reduce.9 = (bf16[768]{0:T(1024)(128)(2,1)}, bf16[768]{0:T(1024)(128)(2,1)}, bf16[768]{0:T(1024)(128)(2,1)}, bf16[768]{0:T(1024)(128)(2,1)}, bf16[768]{0:T(1...) all-reduce(f32[768]{0:T(1024)} %get-tuple-element.161, ...), channel_id=3, replica_groups=mesh['twin'=2,'dp'=16] {'dp'}, use_global_device_ids=true, to_apply=%region_24.25.clone | all-reduce | flops 9216 | bytes 55296
  393.7 5.6 all-reduce.10
  411.1 1.6 convert_element_type.226
  412.7 2.1 copy.64
  414.8 75.2 %reduce-scatter.9.cloned.1.call-done = f32[48,3072]{1,0:T(8,128)} async-done(((f32[768,3072]{1,0:T(8,128)}), f32[48,3072]{1,0:T(8,128)}) %reduce-scatter.9.cloned.1.call-update) | async-done | bytes 589840 | tf_op jit(solution)/shard_map/reduce_scatter | solution.py:259
  490.0 1.8 convert_element_type.235
  491.8 113.9 %reduce-scatter.11.cloned.1.call-done = f32[192,768]{1,0:T(8,128)} async-done(((f32[3072,768]{1,0:T(8,128)}), f32[192,768]{1,0:T(8,128)}) %reduce-scatter.11.cloned.1.call-update) | async-done | bytes 589840 | tf_op jit(solution)/shard_map/reduce_scatter | solution.py:261
  605.7 1.8 convert_element_type.240
  607.5 7.8 %add_convert_fusion.2 = bf16[1024,768]{1,0:T(8,128)(2,1)} fusion(f32[1024,768]{1,0:T(8,128)} %copy-done.12, bf16[1024,2304]{1,0:T(8,128)(2,1)} %bitcast.166, bf16[768,2304]{1,0:T(8,128)(2,1)S(1)} %copy-done, f32[1024]{0:T(1024)S(1)} %copy-done.41), kind=kOutput, calls=%fused_computation.47 | convolution fusion | flops 3626237952 | bytes 12980224 | tf_op jit(solution)/shard_map/dot_general | solution.py:37
  615.3 38.7 %all-reduce.14.cloned.1.call-done = (bf16[48,2304]{0,1:T(8,128)(2,1)}, bf16[48,768]{1,0:T(8,128)(2,1)}, bf16[48,3072]{1,0:T(8,128)(2,1)}, bf16[192,768]{1,0:T(8,128)(2,1)}) async-done(((bf16[48,2304]{0,1:T(8,128)(2,1)}, bf16[48,768]{1,0:T(8,128)(2,1)}, bf16[48,3072]{1,0:T(8,128)(2,1)}, bf16[192,768]{1,0:T(8,128)(2,1)}), (bf16[48,2304]{0,1:T(8,128)(2,1)}, bf16[48,768]{1,0:T(8,128)(2,1)}, ...) | async-done | bytes 884752 | tf_op jit(solution)/shard_map/psum | solution.py:281
  654.0 1.8 convert_element_type.236
  655.8 1.8 convert_element_type.241
  657.6 2.0 copy.58
  659.7 1.6 convert_element_type.227
  (265 shorter events, 58.1 us)
Async XLA Ops:
  7.2 2.0 copy-start
  7.2 403.9 %reduce-scatter.7.cloned.1.call-start = ((), (), s32[]{:S(2)}) async-start(), calls=%async_computation.4 | async-start | bytes 2506752 | tf_op jit(solution)/shard_map/reduce_scatter | solution.py:255
  16.5 6.7 copy-start.25
  23.8 38.7 %copy-start.54 = (bf16[768]{0:T(1024)(128)(2,1)S(1)}, bf16[768]{0:T(1024)(128)(2,1)}, u32[]{:S(2)}) copy-start(bf16[768]{0:T(1024)(128)(2,1)} %param.27) | copy-start | bytes 4612
  27.0 2.1 copy-start.5
  46.3 2.1 copy-start.5
  62.6 5.3 slice-start.7
  62.6 5.3 slice-start.8
  66.5 11.1 %copy-start.8 = (f32[1024,768]{1,0:T(8,128)}, f32[1024,768]{1,0:T(8,128)S(1)}, u32[]{:S(2)}) copy-start(f32[1024,768]{1,0:T(8,128)S(1)} %get-tuple-element.228) | copy-start | bytes 9437188
  66.6 105.8 %copy-start.21 = (f32[1024]{0:T(1024)}, f32[1024]{0:T(1024)S(1)}, u32[]{:S(2)}) copy-start(f32[1024]{0:T(1024)S(1)} %broadcast_multiply_fusion.1) | copy-start | bytes 12292
  66.6 11.0 %slice-start.3 = ((s8[4718592]{0:T(1024)(128)(4,1)}), s8[4194304]{0:T(1024)(128)(4,1)S(1)}, s32[]{:S(2)}) async-start(s8[4718592]{0:T(1024)(128)(4,1)} %bitcast.172), calls=%async_computation.12 | async-start | bytes 8388608
  67.7 104.6 %copy-start.23 = (f32[1024]{0:T(1024)}, f32[1024]{0:T(1024)S(1)}, u32[]{:S(2)}) copy-start(f32[1024]{0:T(1024)S(1)} %fusion.36) | copy-start | bytes 12292
  67.7 104.6 %copy-start.26 = (f32[768]{0:T(1024)}, f32[768]{0:T(1024)S(1)}, u32[]{:S(2)}) copy-start(f32[768]{0:T(1024)S(1)} %convert_element_type.200) | copy-start | bytes 9220
  67.8 9.8 %copy-start.30 = (f32[768]{0:T(1024)}, f32[768]{0:T(1024)S(1)}, u32[]{:S(2)}) copy-start(f32[768]{0:T(1024)S(1)} %convert_element_type.201) | copy-start | bytes 9220
  67.8 9.8 %copy-start.45 = (f32[3072]{0:T(1024)}, f32[3072]{0:T(1024)S(1)}, u32[]{:S(2)}) copy-start(f32[3072]{0:T(1024)S(1)} %convert_element_type.203) | copy-start | bytes 36868
  67.8 9.8 %slice-start.4 = ((s8[4718592]{0:T(1024)(128)(4,1)}), s8[524288]{0:T(1024)(128)(4,1)S(1)}, s32[]{:S(2)}) async-start(s8[4718592]{0:T(1024)(128)(4,1)} %bitcast.172), calls=%async_computation.13 | async-start | bytes 1048576
  77.6 5.5 copy-start.62
  83.1 1.8 copy-start.6
  84.9 48.5 %copy-start.53 = (s32[256]{0:T(256)S(1)}, s32[256]{0:T(256)}, u32[]{:S(2)}) copy-start(s32[256]{0:T(256)} %param.22) | copy-start | bytes 3076
  86.3 47.1 %copy-start.19 = (f32[2,8,768]{2,1,0:T(8,128)}, f32[2,8,768]{2,1,0:T(8,128)S(1)}, u32[]{:S(2)}) copy-start(f32[2,8,768]{2,1,0:T(8,128)S(1)} %get-tuple-element.234) | copy-start | bytes 147460
  86.3 47.1 %copy-start.51 = (f32[2,8]{1,0:T(2,128)}, f32[2,8]{1,0:T(2,128)S(1)}, u32[]{:S(2)}) copy-start(f32[2,8]{1,0:T(2,128)S(1)} %get-tuple-element.233) | copy-start | bytes 196
  135.4 6.3 copy-start.7
  135.4 6.3 copy-start.29
  135.4 6.3 copy-start.33
  135.4 6.3 copy-start.35
  143.2 2.8 slice-start.5
  143.2 2.8 slice-start.6
  146.0 15.1 %copy-start.17 = (bf16[1024,768]{1,0:T(8,128)(2,1)}, bf16[1024,768]{1,0:T(8,128)(2,1)S(1)}, u32[]{:S(2)}) copy-start(bf16[1024,768]{1,0:T(8,128)(2,1)S(1)} %get-tuple-element.210) | copy-start | bytes 4718596
  146.0 15.0 %copy-start.9 = (f32[1024,768]{1,0:T(8,128)S(1)}, f32[1024,768]{1,0:T(8,128)}, u32[]{:S(2)}) copy-start(f32[1024,768]{1,0:T(8,128)} %copy-done.8) | copy-start | bytes 9437188
  161.0 11.3 %copy-start.14 = (bf16[1024,3072]{1,0:T(8,128)(2,1)}, bf16[1024,3072]{1,0:T(8,128)(2,1)S(1)}, u32[]{:S(2)}) copy-start(bf16[1024,3072]{1,0:T(8,128)(2,1)S(1)} %get-tuple-element.241) | copy-start | bytes 18874372
  161.1 11.3 %copy-start.37 = (f32[1024]{0:T(1024)S(1)}, f32[1024]{0:T(1024)}, u32[]{:S(2)}) copy-start(f32[1024]{0:T(1024)} %copy-done.36) | copy-start | bytes 12292
  173.8 3.7 copy-start.60
  173.9 2.5 copy-start.40
  180.4 232.3 %reduce-scatter.13.cloned.1.call-start = ((), (), s32[]{:S(2)}) async-start(), calls=%async_computation.7 | async-start | bytes 7520256
  187.9 6.4 copy-start.1
  187.9 6.4 copy-start.3
  187.9 7.4 %copy-start.20 = (f32[2,12,512,1]{2,1,3,0:T(8,128)S(1)}, f32[2,12,512,1]{2,1,3,0:T(8,128)}, u32[]{:S(2)}) copy-start(f32[2,12,512,1]{2,1,3,0:T(8,128)} %get-tuple-element.368) | copy-start | bytes 147460 | tf_op jit(solution)/shard_map/while
  187.9 8.0 %copy-start.13 = (bf16[2,512,768]{2,1,0:T(8,128)(2,1)S(1)}, bf16[2,512,768]{2,1,0:T(8,128)(2,1)}, u32[]{:S(2)}) copy-start(bf16[2,512,768]{2,1,0:T(8,128)(2,1)} %get-tuple-element.369) | copy-start | bytes 4718596 | tf_op jit(solution)/shard_map/while
  199.2 11.6 %slice-start = ((s8[12582912]{0:T(1024)(128)(4,1)}), s8[4194304]{0:T(1024)(128)(4,1)S(1)}, s32[]{:S(2)}) async-start(s8[12582912]{0:T(1024)(128)(4,1)} %bitcast.149), calls=%async_computation.9 | async-start | bytes 8388608 | tf_op jit(solution)/shard_map/while
  199.2 11.6 %slice-start.1 = ((s8[12582912]{0:T(1024)(128)(4,1)}), s8[4194304]{0:T(1024)(128)(4,1)S(1)}, s32[]{:S(2)}) async-start(s8[12582912]{0:T(1024)(128)(4,1)} %bitcast.149), calls=%async_computation.10 | async-start | bytes 8388608 | tf_op jit(solution)/shard_map/while
  199.2 13.4 %slice-start.2 = ((s8[12582912]{0:T(1024)(128)(4,1)}), s8[4194304]{0:T(1024)(128)(4,1)S(1)}, s32[]{:S(2)}) async-start(s8[12582912]{0:T(1024)(128)(4,1)} %bitcast.149), calls=%async_computation.11 | async-start | bytes 8388608 | tf_op jit(solution)/shard_map/while
  199.2 13.4 %copy-start.10 = (pred[512,512]{0,1:T(8,128)(4,1)S(1)}, pred[512,512]{0,1:T(8,128)(4,1)}, u32[]{:S(2)}) copy-start(pred[512,512]{0,1:T(8,128)(4,1)} %broadcast_compare_fusion.5) | copy-start | bytes 786436 | tf_op jit(solution)/shard_map/while
  199.2 13.4 %copy-start.15 = (f32[12,512]{1,0:T(8,128)S(1)}, f32[12,512]{1,0:T(8,128)}, u32[]{:S(2)}) copy-start(f32[12,512]{1,0:T(8,128)} %dynamic-slice_bitcast_fusion.7) | copy-start | bytes 73732 | tf_op jit(solution)/shard_map/while
  212.6 7.1 %copy-start.2 = (bf16[512,768]{0,1:T(8,128)(2,1)S(1)}, bf16[512,768]{0,1:T(8,128)(2,1)}, u32[]{:S(2)}) copy-start(bf16[512,768]{0,1:T(8,128)(2,1)} %copy-done.1) | copy-start | bytes 2359300 | tf_op jit(solution)/shard_map/while
  220.9 2.0 copy-start.11
  230.5 6.4 copy-start.1
  230.5 6.4 copy-start.3
  230.5 7.3 %copy-start.20 = (f32[2,12,512,1]{2,1,3,0:T(8,128)S(1)}, f32[2,12,512,1]{2,1,3,0:T(8,128)}, u32[]{:S(2)}) copy-start(f32[2,12,512,1]{2,1,3,0:T(8,128)} %get-tuple-element.368) | copy-start | bytes 147460 | tf_op jit(solution)/shard_map/while
  230.5 7.9 %copy-start.13 = (bf16[2,512,768]{2,1,0:T(8,128)(2,1)S(1)}, bf16[2,512,768]{2,1,0:T(8,128)(2,1)}, u32[]{:S(2)}) copy-start(bf16[2,512,768]{2,1,0:T(8,128)(2,1)} %get-tuple-element.369) | copy-start | bytes 4718596 | tf_op jit(solution)/shard_map/while
  241.7 11.5 %slice-start = ((s8[12582912]{0:T(1024)(128)(4,1)}), s8[4194304]{0:T(1024)(128)(4,1)S(1)}, s32[]{:S(2)}) async-start(s8[12582912]{0:T(1024)(128)(4,1)} %bitcast.149), calls=%async_computation.9 | async-start | bytes 8388608 | tf_op jit(solution)/shard_map/while
  241.8 11.5 %slice-start.1 = ((s8[12582912]{0:T(1024)(128)(4,1)}), s8[4194304]{0:T(1024)(128)(4,1)S(1)}, s32[]{:S(2)}) async-start(s8[12582912]{0:T(1024)(128)(4,1)} %bitcast.149), calls=%async_computation.10 | async-start | bytes 8388608 | tf_op jit(solution)/shard_map/while
  241.8 13.2 %slice-start.2 = ((s8[12582912]{0:T(1024)(128)(4,1)}), s8[4194304]{0:T(1024)(128)(4,1)S(1)}, s32[]{:S(2)}) async-start(s8[12582912]{0:T(1024)(128)(4,1)} %bitcast.149), calls=%async_computation.11 | async-start | bytes 8388608 | tf_op jit(solution)/shard_map/while
  241.8 13.2 %copy-start.10 = (pred[512,512]{0,1:T(8,128)(4,1)S(1)}, pred[512,512]{0,1:T(8,128)(4,1)}, u32[]{:S(2)}) copy-start(pred[512,512]{0,1:T(8,128)(4,1)} %broadcast_compare_fusion.5) | copy-start | bytes 786436 | tf_op jit(solution)/shard_map/while
  241.8 13.2 %copy-start.15 = (f32[12,512]{1,0:T(8,128)S(1)}, f32[12,512]{1,0:T(8,128)}, u32[]{:S(2)}) copy-start(f32[12,512]{1,0:T(8,128)} %dynamic-slice_bitcast_fusion.7) | copy-start | bytes 73732 | tf_op jit(solution)/shard_map/while
  254.9 7.1 %copy-start.2 = (bf16[512,768]{0,1:T(8,128)(2,1)S(1)}, bf16[512,768]{0,1:T(8,128)(2,1)}, u32[]{:S(2)}) copy-start(bf16[512,768]{0,1:T(8,128)(2,1)} %copy-done.1) | copy-start | bytes 2359300 | tf_op jit(solution)/shard_map/while
  263.2 2.0 copy-start.11
  287.8 202.2 %reduce-scatter.9.cloned.1.call-start = ((), (), s32[]{:S(2)}) async-start(), calls=%async_computation.5 | async-start | bytes 10027008 | tf_op jit(solution)/shard_map/reduce_scatter | solution.py:259
  299.9 305.8 %reduce-scatter.11.cloned.1.call-start = ((), (), s32[]{:S(2)}) async-start(), calls=%async_computation.6 | async-start | bytes 10027008 | tf_op jit(solution)/shard_map/reduce_scatter | solution.py:261
  310.2 7.0 %copy-start.61 = (u32[32]{0:T(128)S(1)}, u32[32]{0:T(128)}, u32[]{:S(2)}) copy-start(u32[32]{0:T(128)} %constant.104) | copy-start | bytes 388
  310.2 343.8 %all-reduce.14.cloned.1.call-start = ((), (), s32[]{:S(2)}) async-start(), calls=%async_computation.8 | async-start | bytes 2506752 | tf_op jit(solution)/shard_map/psum | solution.py:281
  317.2 4.9 copy-start.42
  317.2 4.9 copy-start.43
  317.2 4.9 copy-start.44
  319.1 288.4 %copy-start.41 = (f32[1024]{0:T(1024)S(1)}, f32[1024]{0:T(1024)}, u32[]{:S(2)}) copy-start(f32[1024]{0:T(1024)} %copy-done.40) | copy-start | bytes 12292
  (26 other events, 25.1 us)
Sparse Core Ops, SparseCore 0:
  180.5 59.4 reduce-scatter.6
  287.9 86.8 reduce-scatter.12
  378.9 111.0 reduce-scatter.8
  494.5 111.1 reduce-scatter.10
  609.1 44.7 all-reduce.13
where the time goes:
time: 678 us; the launch traced here: 668 us
  waiting for transfers between devices  228 us (34%)
  matrix products  170 us (25%)
  blocking collectives  113 us (17%)
  local copies, waits for them, and re-layouts  75.5 us (11%)
  other arithmetic  65.2 us (10%)
  between operations  16.2 us (2%)
    reduce_scatter x1, waiting for transfers between devices, body(): lax.psum_scatter(grad_w_down, 'dp', scatter_dimension=0, tiled=True)  114 us
    reduce_scatter x1, waiting for transfers between devices, body(): lax.psum_scatter(grad_w_in, 'dp', scatter_dimension=0, tiled=True)  75.2 us
    unnamed x1, blocking collectives  61.8 us
    all_gather x1, blocking collectives, body(): gathered = lax.all_gather(unit_low, ('twin', 'dp'), axis=0, tiled=True)  45.3 us
    psum x1, waiting for transfers between devices, body(): lax.psum(grad_w_qkv.astype(jnp.bfloat16), 'twin').astype(jnp.float32)  38.7 us
    dot_general x5, matrix products, contract_cols(): lax.dot_general(left, right, (((1,), (1,)), ((), ())), preferred_element_...  38.7 us
    dot_general x5, matrix products, contract_rows(): lax.dot_general(left, right, (((0,), (0,)), ((), ())), preferred_element_...  35.3 us
    unnamed x131, local copies, waits for them, and re-layouts  29.5 us
  transfers between devices with their start and end apart: 5, of which 3 were waited for; matrix products, arithmetic and copies ran while one was open for 25% of the time, Pallas kernels for 0%

commit v1 on v0

v1 whole, which is shorter than its diff:
```python
import functools
import math

import jax
import jax.numpy as jnp
from jax import lax
from jax.experimental import pallas as pl
from jax.experimental.pallas import tpu as pltpu
from jax.sharding import PartitionSpec as P

D = 768
HEADS = 12
HEAD_DIM = 64
SEG = 8
QB = 128
MOST = 128

cosine_scale = 64.0
loss_scale = 32.0
norm_epsilon = 1e-12
unit_epsilon = 1e-06
masked_score = -1e30


def layer_norm(inputs, norm_gain, norm_shift):
    middle = jnp.mean(inputs, axis=-1, keepdims=True)
    centered = inputs - middle
    spread = jnp.mean(centered * centered, axis=-1, keepdims=True)
    return centered * lax.rsqrt(spread + norm_epsilon) * norm_gain + norm_shift


def gelu_exact(inputs):
    return 0.5 * inputs * (1.0 + lax.erf(inputs * 0.5**0.5))


def contract_rows(left, right):
    return lax.dot_general(
        left, right, (((0,), (0,)), ((), ())), preferred_element_type=jnp.float32
    )


def contract_cols(left, right):
    return lax.dot_general(
        left, right, (((1,), (1,)), ((), ())), preferred_element_type=jnp.float32
    )


def rank_loss(sims, wanted):
    row_top = jnp.max(sims, axis=1, keepdims=True)
    weights = jnp.exp(sims - row_top)
    row_total = jnp.sum(weights, axis=1, keepdims=True)
    column = lax.broadcasted_iota(jnp.int32, sims.shape, 1)
    target_hit = column == wanted[:, None]
    picked = jnp.sum(jnp.where(target_hit, sims, 0.0), axis=1)
    losses = row_top[:, 0] + jnp.log(row_total[:, 0]) - picked
    slope = (loss_scale * (weights / row_total - target_hit.astype(jnp.float32))).astype(
        jnp.bfloat16
    )
    return (losses, slope)


def windows(length):
    out = []
    for start in range(0, length, QB):
        out.append((start, max(0, start - MOST), min(length, start + QB + MOST)))
    return out


def pair_masks(shape):
    lane = lax.broadcasted_iota(jnp.int32, shape, 1)
    return lane < HEAD_DIM


def block_probs(q, k_pair, bias):
    scores = contract_cols(q, k_pair) + bias
    top = jnp.max(scores, axis=-1, keepdims=True)
    weights = jnp.exp(scores - top)
    return weights * (1.0 / jnp.sum(weights, axis=-1, keepdims=True))


def attend_fwd_kernel(q_ref, k_ref, v_ref, segc_ref, segr_ref, out_ref):
    length = q_ref.shape[0]
    zero = jnp.zeros((), jnp.bfloat16)
    for start, low, high in windows(length):
        rows = slice(start, start + QB)
        cols = slice(low, high)
        q_pair = q_ref[rows, :] * jnp.asarray(HEAD_DIM**-0.5, jnp.bfloat16)
        k_pair = k_ref[cols, :]
        v_pair = v_ref[cols, :]
        bias = jnp.where(segc_ref[rows, :] == segr_ref[:, cols], 0.0, masked_score)
        first_q = pair_masks(q_pair.shape)
        first_v = pair_masks(v_pair.shape)
        p0 = block_probs(jnp.where(first_q, q_pair, zero), k_pair, bias).astype(jnp.bfloat16)
        p1 = block_probs(jnp.where(first_q, zero, q_pair), k_pair, bias).astype(jnp.bfloat16)
        out = jnp.dot(
            p0, jnp.where(first_v, v_pair, zero), preferred_element_type=jnp.float32
        ) + jnp.dot(p1, jnp.where(first_v, zero, v_pair), preferred_element_type=jnp.float32)
        out_ref[rows, :] = out.astype(jnp.bfloat16)


def attend_forward(qkv, seg_col, seg_row):
    rows, length = seg_row.shape[0], seg_row.shape[2]
    pairs = HEADS // 2
    width = 2 * HEAD_DIM

    def block(part):
        return pl.BlockSpec((None, length, width), lambda r, h: (r, 0, part * pairs + h))

    return pl.pallas_call(
        attend_fwd_kernel,
        name="attend_fwd",
        grid=(rows, pairs),
        in_specs=[
            block(0),
            block(1),
            block(2),
            pl.BlockSpec((None, length, 1), lambda r, h: (r, 0, 0)),
            pl.BlockSpec((None, 1, length), lambda r, h: (r, 0, 0)),
        ],
        out_specs=pl.BlockSpec((None, length, width), lambda r, h: (r, 0, h)),
        out_shape=jax.ShapeDtypeStruct((rows, length, D), jnp.bfloat16),
        cost_estimate=pl.CostEstimate(
            flops=rows * HEADS * 4 * length * length * HEAD_DIM,
            bytes_accessed=rows * length * D * 8,
            transcendentals=rows * HEADS * length * length // 2,
        ),
        compiler_params=pltpu.CompilerParams(vmem_limit_bytes=24 << 20),
    )(qkv, qkv, qkv, seg_col, seg_row)


def attend_bwd_kernel(q_ref, k_ref, v_ref, g_ref, segc_ref, segr_ref, out_ref, dk_acc, dv_acc):
    length = q_ref.shape[0]
    zero = jnp.zeros((), jnp.bfloat16)
    scale = jnp.asarray(HEAD_DIM**-0.5, jnp.bfloat16)
    dk_acc[...] = jnp.zeros_like(dk_acc)
    dv_acc[...] = jnp.zeros_like(dv_acc)
    for start, low, high in windows(length):
        rows = slice(start, start + QB)
        cols = slice(low, high)
        q_pair = q_ref[rows, :] * scale
        k_pair = k_ref[cols, :]
        v_pair = v_ref[cols, :]
        g_pair = g_ref[rows, :]
        bias = jnp.where(segc_ref[rows, :] == segr_ref[:, cols], 0.0, masked_score)
        first_q = pair_masks(q_pair.shape)
        first_k = pair_masks(k_pair.shape)
        dq = None
        for head in range(2):
            pick = (lambda m, a: jnp.where(m, a, zero)) if head == 0 else (
                lambda m, a: jnp.where(m, zero, a)
            )
            q_one = pick(first_q, q_pair)
            g_one = pick(first_q, g_pair)
            k_one = pick(first_k, k_pair)
            p = block_probs(q_one, k_pair, bias)
            gp = contract_cols(g_one, v_pair)
            inner = jnp.sum(p * gp, axis=-1, keepdims=True)
            ds = (p * (gp - inner)).astype(jnp.bfloat16)
            p_low = p.astype(jnp.bfloat16)
            part = jnp.dot(ds, k_one, preferred_element_type=jnp.float32)
            dq = part if dq is None else dq + part
            dk_acc[cols, :] += contract_rows(ds, q_one)
            dv_acc[cols, :] += contract_rows(p_low, g_one)
        out_ref[0, rows, :] = (dq * HEAD_DIM**-0.5).astype(jnp.bfloat16)
    out_ref[1] = dk_acc[...].astype(jnp.bfloat16)
    out_ref[2] = dv_acc[...].astype(jnp.bfloat16)


def attend_backward(qkv, grad_context, seg_col, seg_row):
    rows, length = seg_row.shape[0], seg_row.shape[2]
    pairs = HEADS // 2
    width = 2 * HEAD_DIM

    def block(part):
        return pl.BlockSpec((None, length, width), lambda r, h: (r, 0, part * pairs + h))

    return pl.pallas_call(
        attend_bwd_kernel,
        name="attend_bwd",
        grid=(rows, pairs),
        in_specs=[
            block(0),
            block(1),
            block(2),
            pl.BlockSpec((None, length, width), lambda r, h: (r, 0, h)),
            pl.BlockSpec((None, length, 1), lambda r, h: (r, 0, 0)),
            pl.BlockSpec((None, 1, length), lambda r, h: (r, 0, 0)),
        ],
        out_specs=pl.BlockSpec((3, None, length, width), lambda r, h: (0, r, 0, h)),
        out_shape=jax.ShapeDtypeStruct((3, rows, length, D), jnp.bfloat16),
        scratch_shapes=[
            pltpu.VMEM((length, width), jnp.float32),
            pltpu.VMEM((length, width), jnp.float32),
        ],
        cost_estimate=pl.CostEstimate(
            flops=rows * HEADS * 10 * length * length * HEAD_DIM,
            bytes_accessed=rows * length * D * 14,
            transcendentals=rows * HEADS * length * length // 2,
        ),
        compiler_params=pltpu.CompilerParams(vmem_limit_bytes=24 << 20),
    )(qkv, qkv, qkv, grad_context, seg_col, seg_row)


def add_low(*parts):
    total = parts[0].astype(jnp.float32)
    for part in parts[1:]:
        total = total + part.astype(jnp.float32)
    return lax.optimization_barrier(total.astype(jnp.bfloat16))


def digits_of(devices):
    out, rest = [], devices // 2
    if rest > 1:
        out.append(2)
        rest //= 2
    while rest > 1:
        size = 4 if rest % 4 == 0 else 2
        out.append(size)
        rest //= size
    return out


def swap_dp(value, flip):
    devices = lax.axis_size("dp")
    return lax.ppermute(value, "dp", [(i, i ^ flip) for i in range(devices)])


def swap_twin(value):
    return lax.ppermute(value, "twin", [(0, 1), (1, 0)])


def digit_step(value, size, unit):
    mine = (lax.axis_index("dp") // unit) % size
    rest = value.shape[0] // size
    view = value.reshape((rest, size) + value.shape[1:])
    parts = [lax.dynamic_index_in_dim(view, mine, 1, keepdims=False)]
    for flip in range(1, size):
        send = lax.dynamic_index_in_dim(view, mine ^ flip, 1, keepdims=False)
        parts.append(swap_dp(send, flip * unit))
    return add_low(*parts)


def reduce_pair(left, right):
    twin = lax.axis_index("twin")
    devices = lax.axis_size("dp")
    digits = digits_of(devices)
    keep = lax.dynamic_index_in_dim(left, twin, 0, keepdims=False)
    send = lax.dynamic_index_in_dim(left, 1 - twin, 0, keepdims=False)
    a = add_low(keep, swap_twin(send))
    b = right
    unit = 2
    for size in digits:
        a = digit_step(a, size, unit)
        b = digit_step(b, size, unit)
        unit *= size
    a, b = a[0], b[0]
    other = swap_twin(a)
    low = jnp.where(twin == 0, a, other).astype(jnp.float32)
    high = jnp.where(twin == 0, other, a).astype(jnp.float32)
    return (low, high, b.astype(jnp.float32) + swap_twin(b).astype(jnp.float32))


def core_sum(value):
    core = lax.axis_index("dp") % 2
    view = value.reshape((value.shape[0] // 2, 2) + value.shape[1:])
    keep = lax.dynamic_index_in_dim(view, core, 1, keepdims=False)
    send = lax.dynamic_index_in_dim(view, 1 - core, 1, keepdims=False)
    return add_low(keep, swap_dp(send, 1))


def scatter_columns(grad, extra=None):
    devices = lax.axis_size("dp")
    total = core_sum(grad.reshape(devices, grad.shape[0] // devices, grad.shape[1]))
    quarter = grad.shape[1] // 4 // 128 * 128
    left = jnp.stack([total[:, :, :quarter], total[:, :, quarter : 2 * quarter]])
    low, high, rest = reduce_pair(left, total[:, :, 2 * quarter :])
    return jnp.concatenate([low, high, rest], axis=1)


def scatter_rows(grad):
    devices = lax.axis_size("dp")
    r = grad.shape[0] // devices
    total = core_sum(grad.reshape(devices, r, grad.shape[1]))
    quarter = r // 4
    left = jnp.stack([total[:, :quarter], total[:, quarter : 2 * quarter]])
    low, high, rest = reduce_pair(left, total[:, 2 * quarter :])
    return jnp.concatenate([low, high, rest], axis=0)


def body(
    hidden,
    segment_ids,
    targets,
    w_qkv,
    b_query,
    b_value,
    w_out,
    b_out,
    ln1_gain,
    ln1_bias,
    w_in,
    b_in,
    w_down,
    b_down,
    ln2_gain,
    ln2_bias,
):
    row_count, length, width = hidden.shape
    token_count = row_count * length
    devices = lax.axis_size("dp")
    tokens = hidden.reshape(token_count, width)
    bias_qkv = jnp.concatenate(
        [b_query.astype(jnp.float32), jnp.zeros((width,), jnp.float32), b_value.astype(jnp.float32)]
    )
    qkv_all = (jnp.dot(tokens, w_qkv, preferred_element_type=jnp.float32) + bias_qkv).astype(
        jnp.bfloat16
    )
    qkv_rows = qkv_all.reshape(row_count, length, 3 * width)
    seg_col = segment_ids.reshape(row_count, length, 1)
    seg_row = segment_ids.reshape(row_count, 1, length)
    context_flat = attend_forward(qkv_rows, seg_col, seg_row).reshape(token_count, width)
    attended = jnp.dot(context_flat, w_out, preferred_element_type=jnp.float32) + b_out.astype(
        jnp.float32
    )
    normed_one, norm_one_back = jax.vjp(
        layer_norm,
        tokens.astype(jnp.float32) + attended,
        ln1_gain.astype(jnp.float32),
        ln1_bias.astype(jnp.float32),
    )
    normed_low = normed_one.astype(jnp.bfloat16)
    hidden_pre = jnp.dot(normed_low, w_in, preferred_element_type=jnp.float32) + b_in.astype(
        jnp.float32
    )
    active, gelu_back = jax.vjp(gelu_exact, hidden_pre)
    active_low = active.astype(jnp.bfloat16)
    branch = jnp.dot(active_low, w_down, preferred_element_type=jnp.float32) + b_down.astype(
        jnp.float32
    )
    output, norm_two_back = jax.vjp(
        layer_norm, normed_one + branch, ln2_gain.astype(jnp.float32), ln2_bias.astype(jnp.float32)
    )
    member = (segment_ids[:, None, :] == jnp.arange(SEG, dtype=jnp.int32)[None, :, None]).astype(
        jnp.float32
    )
    counts = jnp.sum(member, axis=2, keepdims=True)

    def pool_units(out_rows):
        pooled = (
            jnp.einsum("rsl,rld->rsd", member, out_rows, precision=lax.Precision.HIGHEST) / counts
        )
        unit_rows = pooled * lax.rsqrt(
            jnp.mean(pooled * pooled, axis=-1, keepdims=True) + unit_epsilon
        )
        return unit_rows.reshape(row_count * SEG, width)

    unit_rows, pool_back = jax.vjp(pool_units, output.reshape(row_count, length, width))
    unit_low = unit_rows.astype(jnp.bfloat16)
    gathered = lax.all_gather(unit_low, ("twin", "dp"), axis=0, tiled=True)
    anchor_count = gathered.shape[0] // 2
    anchors = gathered[:anchor_count]
    positives = gathered[anchor_count:]
    factor = cosine_scale / width
    everyone = lax.axis_size(("twin", "dp"))
    loss_share = anchor_count // everyone
    loss_start = lax.axis_index(("twin", "dp")) * loss_share
    all_losses, slope = rank_loss(contract_cols(anchors, positives) * factor, targets)
    losses = lax.dynamic_slice_in_dim(all_losses, loss_start, loss_share, 0)
    sentences = unit_low.shape[0]
    offset = lax.axis_index("dp") * sentences
    anchor_rows = (
        jnp.dot(
            lax.dynamic_slice_in_dim(slope, offset, sentences, 0),
            positives,
            preferred_element_type=jnp.float32,
        )
        * factor
    )
    positive_rows = (
        contract_rows(lax.dynamic_slice_in_dim(slope, offset, sentences, 1), anchors) * factor
    )
    unit_grad = jnp.where(lax.axis_index("twin") == 0, anchor_rows, positive_rows)
    grad_output = pool_back(unit_grad)[0].reshape(token_count, width)
    grad_sum_two, grad_ln2_gain, grad_ln2_bias = norm_two_back(grad_output)
    grad_branch = grad_sum_two.astype(jnp.bfloat16)
    grad_w_down = contract_rows(active_low, grad_branch).astype(jnp.bfloat16)
    grad_w_down = scatter_rows(grad_w_down)
    grad_b_down = jnp.sum(grad_branch, axis=0, dtype=jnp.float32)
    grad_active = contract_cols(grad_branch, w_down)
    grad_pre = gelu_back(grad_active)[0].astype(jnp.bfloat16)
    grad_w_in = contract_rows(normed_low, grad_pre).astype(jnp.bfloat16)
    grad_w_in = scatter_columns(grad_w_in)
    grad_b_in = jnp.sum(grad_pre, axis=0, dtype=jnp.float32)
    grad_normed = contract_cols(grad_pre, w_in) + grad_sum_two
    grad_sum_one, grad_ln1_gain, grad_ln1_bias = norm_one_back(grad_normed)
    grad_attended = grad_sum_one.astype(jnp.bfloat16)
    grad_w_out = contract_rows(context_flat, grad_attended).astype(jnp.bfloat16)
    grad_b_out = jnp.sum(grad_attended, axis=0, dtype=jnp.float32)
    grad_context = (
        contract_cols(grad_attended, w_out).astype(jnp.bfloat16).reshape(row_count, length, width)
    )
    grad_parts = attend_backward(qkv_rows, grad_context, seg_col, seg_row).reshape(
        3, token_count, width
    )
    grad_qkv = jnp.concatenate([grad_parts[0], grad_parts[1], grad_parts[2]], axis=1)
    grad_w_qkv = contract_rows(tokens, grad_qkv).astype(jnp.bfloat16)
    sums = jnp.sum(grad_parts, axis=1, dtype=jnp.float32)
    hidden_grad = (
        (contract_cols(grad_qkv, w_qkv) + grad_sum_one)
        .astype(jnp.bfloat16)
        .reshape(row_count, length, width)
    )
    vectors = jnp.stack(
        [sums[0], sums[2], grad_b_out, grad_ln1_gain, grad_ln1_bias]
        + [grad_b_down, grad_ln2_gain, grad_ln2_bias]
    )
    share = width // devices
    wide = grad_b_in.reshape(devices, -1, share).transpose(1, 0, 2).reshape(-1, width)
    vectors = jnp.concatenate([vectors, wide])
    vectors = jnp.pad(vectors, ((0, 128 - vectors.shape[0]), (0, 0))).T.astype(jnp.bfloat16)
    last = scatter_columns(jnp.concatenate([grad_w_qkv, grad_w_out, vectors], axis=1))
    grad_w_qkv = last[:, : 3 * width]
    grad_w_out = last[:, 3 * width : 4 * width]
    small = last[:, 4 * width :].T
    return (
        losses,
        hidden_grad,
        grad_w_qkv,
        small[0],
        small[1],
        grad_w_out,
        small[2],
        small[3],
        small[4],
        grad_w_in,
        small[8 : 8 + wide.shape[0]].reshape(-1),
        grad_w_down,
        small[5],
        small[6],
        small[7],
    )


def solution(mesh):
    whole = (P(),) * 14
    placed = (P(("twin", "dp"), None, None), P(("twin", "dp"), None)) + whole
    return jax.shard_map(
        body,
        mesh=mesh,
        in_specs=placed,
        out_specs=(
            P(("twin", "dp")),
            P(("twin", "dp"), None, None),
            P("dp", None),
            P("dp"),
            P("dp"),
            P("dp", None),
            P("dp"),
            P("dp"),
            P("dp"),
            P("dp", None),
            P("dp"),
            P("dp", None),
            P("dp"),
            P("dp"),
            P("dp"),
        ),
        check_vma=False,
    )
```

time: 678 us -> 403 us (0.59)
  waiting for transfers between devices: 228 us -> 56.1 us
  matrix products: 170 us -> 87.5 us
  Pallas kernels: 0 us -> 72.2 us
  blocking collectives: 113 us -> 45.3 us
  starting transfers between devices: 0.2 us -> 35.1 us
  local copies, waits for them, and re-layouts: 75.5 us -> 53.3 us
  other arithmetic: 65.2 us -> 45.2 us
  between operations: 16.2 us -> 1.93 us
    reduce_scatter x3 -> x0, waiting for transfers between devices: 189 us -> none  [the longest x1 114 us: body(): lax.psum_scatter(grad_w_down, 'dp', scatter_dimension=0, tiled=True)]
    pallas_call x0 -> x2, Pallas kernels: none -> 72.2 us  [the longest x1 50.5 us: attend_backward(): pl.pallas_call(attend_bwd_kernel, name='attend_bwd', grid=(rows, pairs),...]
    dot_general x14 -> x0, matrix products: 63.7 us -> none  [the longest x2 23.1 us: attend_backward(): jnp.einsum('qhd,khd->hqk', grad_heads, value_heads, preferred_element_typ...]
    unnamed x1 -> x0, blocking collectives: 61.8 us -> none
    ppermute x0 -> x36, waiting for transfers between devices: none -> 56.1 us  [the longest x9 32.8 us: swap_twin(): return lax.ppermute(value, 'twin', [(0, 1), (1, 0)])]
    psum x1 -> x0, waiting for transfers between devices: 38.7 us -> none  [body(): lax.psum(grad_w_qkv.astype(jnp.bfloat16), 'twin').astype(jnp.float32)]
    ppermute x0 -> x36, starting transfers between devices: none -> 35.1 us  [the longest x27 27.3 us: swap_dp(): return lax.ppermute(value, 'dp', [(i, i ^ flip) for i in range(devices)])]
    convert_element_type x17 -> x20, other arithmetic: 35.1 us -> 12.3 us  [the longest x17 11.3 us: add_low(): return lax.optimization_barrier(total.astype(jnp.bfloat16))]
  transfers between devices with their start and end apart: 5 -> 36, of which waited for: 3 -> 13; matrix products, arithmetic and copies ran while one was open for 25% -> 22% of each run, Pallas kernels for 0% -> 13%
where the time goes in v1:
time: 403 us; the launch traced here: 397 us
  matrix products  87.5 us (22%)
  Pallas kernels  72.2 us (18%)
  waiting for transfers between devices  56.1 us (14%)
  local copies, waits for them, and re-layouts  53.3 us (13%)
  blocking collectives  45.3 us (11%)
  other arithmetic  45.2 us (11%)
  starting transfers between devices  35.1 us (9%)
    pallas_call x1, Pallas kernels, attend_backward(): pl.pallas_call(attend_bwd_kernel, name='attend_bwd', grid=(rows, pairs),...  50.5 us
    all_gather x1, blocking collectives, body(): gathered = lax.all_gather(unit_low, ('twin', 'dp'), axis=0, tiled=True)  45.3 us
    ppermute x9, waiting for transfers between devices, swap_twin(): return lax.ppermute(value, 'twin', [(0, 1), (1, 0)])  32.8 us
    dot_general x5, matrix products, contract_cols(): lax.dot_general(left, right, (((1,), (1,)), ((), ())), preferred_element_...  31.3 us
    dot_general x5, matrix products, contract_rows(): lax.dot_general(left, right, (((0,), (0,)), ((), ())), preferred_element_...  28.2 us
    ppermute x27, starting transfers between devices, swap_dp(): return lax.ppermute(value, 'dp', [(i, i ^ flip) for i in range(devices)])  27.3 us
    ppermute x27, waiting for transfers between devices, swap_dp(): return lax.ppermute(value, 'dp', [(i, i ^ flip) for i in range(devices)])  23.3 us
    pallas_call x1, Pallas kernels, attend_forward(): pl.pallas_call(attend_fwd_kernel, name='attend_fwd', grid=(rows, pairs),...  21.7 us
  transfers between devices with their start and end apart: 36, of which 13 were waited for; matrix products, arithmetic and copies ran while one was open for 22% of the time, Pallas kernels for 13%

profile of v1, /device:TPU:0, one launch (start us, length us, event | category | flops | bytes accessed | tf_op | source)
XLA Modules:
  0.0 396.6 jit_solution(5378662232987494661)
XLA Ops:
  0.7 1.5 convert_reduce_fusion
  4.1 1.3 convert_element_type.393
  8.1 1.7 copy.31.segc_ref
  11.2 5.9 %add_convert_fusion.1 = bf16[1024,2304]{1,0:T(8,128)(2,1)S(1)} fusion(bf16[1024,768]{1,0:T(8,128)(2,1)} %bitcast.213, bf16[768,2304]{1,0:T(8,128)(2,1)S(1)} %copy-done, f32[2304]{0:T(1024)S(1)} %pad_maximum_fusion.10), kind=kOutput, calls=%fused_computation.3 | convolution fusion | flops 3628597248 | bytes 9839616 | tf_op jit(solution)/shard_map/dot_general | solution.py:315
  17.2 21.7 %attend_fwd.1 = bf16[2,512,768]{2,1,0:T(8,128)(2,1)S(1)} custom-call(bf16[2,512,2304]{2,1,0:T(8,128)(2,1)S(1)} %bitcast.162, bf16[2,512,2304]{2,1,0:T(8,128)(2,1)S(1)} %bitcast.163, bf16[2,512,2304]{2,1,0:T(8,128)(2,1)S(1)} %bitcast.164, s32[2,512,1]{2,1,0:T(8,128)S(1)} %copy-done.3, s32[2,1,512]{2,1,0:T(1,128)S(1)} %broadcast_in_dim.18.segr_ref), custom_call_target="tpu_custom_call" | custom-call | flops 1610612736 | bytes 6291456 | tf_op jit(solution)/shard_map/attend_fwd/pallas_call | solution.py:109
  38.9 1.6 fusion.62
  42.7 9.6 %multiply_convert_fusion = (bf16[1024,3072]{1,0:T(8,128)(2,1)S(1)}, f32[1024,3072]{1,0:T(8,128)}) fusion(f32[3072]{0:T(1024)S(1)} %copy-done.39, bf16[768,3072]{1,0:T(8,128)(2,1)S(1)} %bitcast.210, f32[1024,768]{1,0:T(8,128)S(1)} %get-tuple-element.74, f32[768]{0:T(1024)S(1)} %convert_element_type.391, f32[768]{0:T(1024)S(1)} %convert_element_type.390, ...), kind=kOutput, calls=%fused_computation.1 | convolution fusion | flops 4854644736 | bytes 26765312 | tf_op jit(solution)/shard_map/dot_general | solution.py:332
  52.4 5.4 %fusion.63 = (f32[1024]{0:T(1024)S(1)}, f32[1024,768]{1,0:T(8,128)S(1)}) fusion(f32[768]{0:T(1024)S(1)} %copy-done.51, bf16[1024,3072]{1,0:T(8,128)(2,1)S(1)} %get-tuple-element.75, bf16[3072,768]{1,0:T(8,128)(2,1)S(1)} %bitcast.208, f32[768]{0:T(1024)S(1)} %convert_element_type.391, f32[768]{0:T(1024)S(1)} %convert_element_type.390, ...), kind=kOutput, calls=%fused_computation.201 | convolution fusion | flops 4837342208 | bytes 17323008 | tf_op jit(solution)/shard_map/dot_general | solution.py:337
  61.9 45.3 %all_gather.3 = bf16[512,768]{1,0:T(8,128)(2,1)S(1)} all-gather(bf16[16,768]{1,0:T(8,128)(2,1)S(1)} %fusion.41), channel_id=1, replica_groups=mesh['twin'=2,'dp'=16] {'twin','dp'}, dimensions={0}, use_global_device_ids=true | all-gather | bytes 811008 | tf_op jit(solution)/shard_map/all_gather | solution.py:359
  108.1 1.6 fusion.64
  109.7 1.6 fusion.34
  111.9 1.7 multiply_convert_fusion.1
  113.7 1.4 convolution_multiply_fusion.2
  117.0 2.9 fusion.65
  119.9 1.5 fusion.4
  121.4 2.9 fusion.59
  124.3 2.8 fusion.56
  127.2 13.3 %fusion.66 = (bf16[3072]{0:T(1024)(128)(2,1)}, bf16[1024,3072]{1,0:T(8,128)(2,1)S(1)}) fusion(bf16[1024,768]{1,0:T(8,128)(2,1)S(1)} %get-tuple-element.31, bf16[3072,768]{1,0:T(8,128)(2,1)} %param.28, f32[1024,3072]{1,0:T(8,128)} %get-tuple-element.76, f32[3072]{0:T(1024)S(1)} %copy-done.40), kind=kOutput, calls=%fused_computation.204 | convolution fusion | flops 4879021056 | bytes 25184256 | tf_op jit(solution)/shard_map/dot_general | solution.py:43
  140.5 2.7 copy-done.58
  143.2 7.9 %convolution_convert_fusion.1 = bf16[768,3072]{1,0:T(8,128)(2,1)} fusion(bf16[1024,3072]{1,0:T(8,128)(2,1)S(1)} %get-tuple-element.89, f32[1024,768]{1,0:T(8,128)S(1)} %copy-done.11, f32[768]{0:T(1024)S(1)} %copy-done.50, f32[768]{0:T(1024)S(1)} %copy-done.34, f32[1024]{0:T(1024)S(1)} %copy-done.36, f32[1024]{0:T(1024)S(1)} %copy-done.26), kind=kOutput, calls=%fused_computation.5 | convolution fusion | flops 4838129664 | bytes 14170112 | tf_op jit(solution)/shard_map/dot_general | solution.py:37
  151.1 3.3 dynamic-slice_bitcast_fusion.2
  154.8 9.7 %convolution_convert_fusion = bf16[3072,768]{1,0:T(8,128)(2,1)S(1)} fusion(bf16[1024,3072]{1,0:T(8,128)(2,1)} %copy-done.59, bf16[1024,768]{1,0:T(8,128)(2,1)S(1)} %copy-done.19), kind=kOutput, calls=%fused_computation.4 | convolution fusion | flops 4834197504 | bytes 12582912 | tf_op jit(solution)/shard_map/dot_general | solution.py:37
  164.6 2.4 copy-done.14
  167.0 1.6 dynamic-slice_bitcast_fusion.1
  168.8 6.6 %multiply_reduce_fusion = (bf16[768]{0:T(1024)(128)(2,1)}, f32[1024]{0:T(1024)S(1)}, bf16[768]{0:T(1024)(128)(2,1)}, f32[1024,768]{1,0:T(8,128)S(1)}) fusion(f32[1024,768]{1,0:T(8,128)S(1)} %copy-done.12, f32[1024]{0:T(1024)S(1)} %copy-done.36, f32[1024]{0:T(1024)S(1)} %copy-done.26, f32[768]{0:T(1024)S(1)} %copy-done.34, f32[1024,768]{1,0:T(8,128)S(1)} %copy-done.13, ...), kind=kOutput, calls=%fused_computation.21 | convolution fusion | flops 4839699456 | bytes 20469760 | tf_op jit(solution)/shard_map/dot_general | solution.py:43
  175.4 1.5 fusion.58
  176.9 1.6 copy-done.9
  179.0 1.4 convolution_convert_fusion.3
  180.6 2.5 convolution_convert_fusion.4
  183.1 50.5 %attend_bwd.1 = bf16[3,2,512,768]{3,2,1,0:T(8,128)(2,1)S(1)} custom-call(bf16[2,512,2304]{2,1,0:T(8,128)(2,1)S(1)} %bitcast.167, bf16[2,512,2304]{2,1,0:T(8,128)(2,1)S(1)} %bitcast.168, bf16[2,512,2304]{2,1,0:T(8,128)(2,1)S(1)} %bitcast.169, bf16[2,512,768]{2,1,0:T(8,128)(2,1)S(1)} %bitcast.172, s32[2,512,1]{2,1,0:T(8,128)S(1)} %copy-done.4, ...), custom_call_target="tpu_custom_call" | custom-call | flops 4026531840 | bytes 11010048 | tf_op jit(solution)/shard_map/attend_bwd/pallas_call | solution.py:177
  233.6 2.2 copy-done.2
  235.8 2.2 fusion.60
  238.0 3.0 reduce.2
  250.0 2.0 concatenate.24
  252.8 6.8 %fusion.3 = bf16[768,2304]{0,1:T(8,128)(2,1)S(1)} fusion(bf16[1024,768]{1,0:T(8,128)(2,1)} %bitcast.214, bf16[1024,768]{1,0:T(8,128)(2,1)} %bitcast.196, bf16[1024,768]{1,0:T(8,128)(2,1)} %bitcast.198, bf16[1024,768]{1,0:T(8,128)(2,1)} %bitcast.194), kind=kOutput, calls=%fused_computation.17 | convolution fusion | flops 3639803904 | bytes 9830400 | tf_op jit(solution)/shard_map/dot_general | solution.py:37
  259.6 2.9 pad_maximum_fusion
  262.5 7.4 %copy.34 = bf16[768,3200]{1,0:T(8,128)(2,1)} copy(bf16[768,3200]{0,1:T(8,128)(2,1)} %pad_maximum_fusion) | data formatting | bytes 9830400 | tf_op jit(solution)/shard_map/concatenate | solution.py:421
  269.9 3.4 dynamic-slice_bitcast_fusion
  273.7 8.3 %add_convert_fusion.2 = bf16[1024,768]{1,0:T(8,128)(2,1)} fusion(f32[1024,768]{1,0:T(8,128)} %copy-done.9, f32[1024]{0:T(1024)S(1)} %copy-done.32, bf16[768,2304]{1,0:T(8,128)(2,1)S(1)} %copy-done, bf16[1024,768]{1,0:T(8,128)(2,1)} %bitcast.197, bf16[1024,768]{1,0:T(8,128)(2,1)} %bitcast.199, bf16[1024,768]{1,0:T(8,128)(2,1)} %bitcast.195), kind=kOutput, calls=%fused_computation.22 | convolution fusion | flops 3640393728 | bytes 12980224 | tf_op jit(solution)/shard_map/dot_general | solution.py:43
  282.6 3.3 fusion.2
  286.1 3.1 fusion.1
  290.7 1.5 collective-permute-start.13
  292.2 2.1 collective-permute-start.31
  294.2 2.3 fusion
  297.1 5.1 %collective-permute-done.19 = bf16[4,48,1536]{2,1,0:T(8,128)(2,1)S(1)} collective-permute-done((bf16[4,48,1536]{2,1,0:T(8,128)(2,1)S(1)}, bf16[4,48,1536]{2,1,0:T(8,128)(2,1)S(1)}, u32[]{:S(2)}, u32[]{:S(2)}) %collective-permute-start.19) | collective-permute-done | bytes 589856 | tf_op jit(solution)/shard_map/ppermute | solution.py:225
  303.1 2.8 collective-permute-done.25
  306.2 12.3 %collective-permute-done.13 = bf16[8,48,768]{2,1,0:T(8,128)(2,1)S(1)} collective-permute-done((bf16[8,48,768]{2,1,0:T(8,128)(2,1)S(1)}, bf16[8,48,768]{2,1,0:T(8,128)(2,1)S(1)}, u32[]{:S(2)}, u32[]{:S(2)}) %collective-permute-start.13) | collective-permute-done | bytes 589856 | tf_op jit(solution)/shard_map/ppermute | solution.py:229
  319.2 11.2 %collective-permute-done.1 = bf16[8,48,768]{2,1,0:T(8,128)(2,1)S(1)} collective-permute-done((bf16[8,48,768]{2,1,0:T(8,128)(2,1)S(1)}, bf16[8,48,768]{2,1,0:T(8,128)(2,1)S(1)}, u32[]{:S(2)}, u32[]{:S(2)}) %collective-permute-start.1) | collective-permute-done | bytes 589856 | tf_op jit(solution)/shard_map/ppermute | solution.py:229
  330.4 1.7 collective-permute-start.26
  333.2 4.3 %collective-permute-start.32 = (bf16[1,96,768]{2,1,0:T(8,128)(2,1)S(1)}, bf16[1,96,768]{2,1,0:T(8,128)(2,1)S(1)}, u32[]{:S(2)}, u32[]{:S(2)}) collective-permute-start(bf16[1,96,768]{2,1,0:T(8,128)(2,1)S(1)} %get-tuple-element.50), channel_id=1, source_target_pairs={{0,4},{1,5},{2,6},{3,7},{4,0},{5,1},{6,2},{7,3},{8,12},{9,13},{10,... | collective-permute-start | bytes 442376 | tf_op jit(solution)/shard_map/ppermute | solution.py:225
  337.6 4.2 %collective-permute-done.34 = bf16[1,96,768]{2,1,0:T(8,128)(2,1)S(1)} collective-permute-done((bf16[1,96,768]{2,1,0:T(8,128)(2,1)S(1)}, bf16[1,96,768]{2,1,0:T(8,128)(2,1)S(1)}, u32[]{:S(2)}, u32[]{:S(2)}) %collective-permute-start.34) | collective-permute-done | bytes 147488 | tf_op jit(solution)/shard_map/ppermute | solution.py:225
  341.8 9.3 %collective-permute-done.33 = bf16[1,96,768]{2,1,0:T(8,128)(2,1)S(1)} collective-permute-done((bf16[1,96,768]{2,1,0:T(8,128)(2,1)S(1)}, bf16[1,96,768]{2,1,0:T(8,128)(2,1)S(1)}, u32[]{:S(2)}, u32[]{:S(2)}) %collective-permute-start.33) | collective-permute-done | bytes 147488 | tf_op jit(solution)/shard_map/ppermute | solution.py:225
  352.9 4.5 %collective-permute-done.23 = bf16[48,1536]{1,0:T(8,128)(2,1)S(1)} collective-permute-done((bf16[48,1536]{1,0:T(8,128)(2,1)S(1)}, bf16[48,1536]{1,0:T(8,128)(2,1)S(1)}, u32[]{:S(2)}, u32[]{:S(2)}) %collective-permute-start.23) | collective-permute-done | bytes 147488 | tf_op jit(solution)/shard_map/ppermute | solution.py:229
  358.2 3.4 collective-permute-start.29
  362.6 1.9 collective-permute-start.28
  364.6 1.6 collective-permute-start.2
  366.1 1.9 collective-permute-start.27
  369.6 2.8 collective-permute-start.15
  373.3 1.6 collective-permute-done.17
  374.9 2.8 collective-permute-done.16
  380.0 1.9 collective-permute-start.5
  382.8 1.6 collective-permute-start.3
  391.7 2.1 slice_reduce_fusion
  394.7 1.7 pad_maximum_fusion.8
  (287 shorter events, 50.2 us)
Async XLA Ops:
  0.6 10.5 %copy-start = (bf16[768,2304]{1,0:T(8,128)(2,1)S(1)}, bf16[768,2304]{1,0:T(8,128)(2,1)}, u32[]{:S(2)}) copy-start(bf16[768,2304]{1,0:T(8,128)(2,1)} %param.19) | copy-start | bytes 10616836
  10.4 41.8 %copy-start.49 = (f32[768]{0:T(1024)}, f32[768]{0:T(1024)S(1)}, u32[]{:S(2)}) copy-start(f32[768]{0:T(1024)S(1)} %convert_element_type.391) | copy-start | bytes 9220
  11.1 41.2 %copy-start.33 = (f32[768]{0:T(1024)}, f32[768]{0:T(1024)S(1)}, u32[]{:S(2)}) copy-start(f32[768]{0:T(1024)S(1)} %convert_element_type.390) | copy-start | bytes 9220
  17.1 21.8 %copy-start.1 = (bf16[1024,2304]{1,0:T(8,128)(2,1)}, bf16[1024,2304]{1,0:T(8,128)(2,1)S(1)}, u32[]{:S(2)}) copy-start(bf16[1024,2304]{1,0:T(8,128)(2,1)S(1)} %add_convert_fusion.1) | copy-start | bytes 14155780
  17.1 21.8 %copy-start.52 = (f32[768]{0:T(1024)S(1)}, f32[768]{0:T(1024)}, u32[]{:S(2)}) copy-start(f32[768]{0:T(1024)} %convert_element_type.389) | copy-start | bytes 9220
  17.1 21.8 %copy-start.55 = (bf16[2,512,768]{2,1,0:T(8,128)(2,1)S(1)}, bf16[2,512,768]{2,1,0:T(8,128)(2,1)}, u32[]{:S(2)}) copy-start(bf16[2,512,768]{2,1,0:T(8,128)(2,1)} %param.16) | copy-start | bytes 4718596
  17.1 21.8 %copy-start.56 = (bf16[768,768]{1,0:T(8,128)(2,1)S(1)}, bf16[768,768]{1,0:T(8,128)(2,1)}, u32[]{:S(2)}) copy-start(bf16[768,768]{1,0:T(8,128)(2,1)} %param.22) | copy-start | bytes 3538948
  40.5 11.8 %copy-start.10 = (f32[1024,768]{1,0:T(8,128)}, f32[1024,768]{1,0:T(8,128)S(1)}, u32[]{:S(2)}) copy-start(f32[1024,768]{1,0:T(8,128)S(1)} %get-tuple-element.74) | copy-start | bytes 9437188
  40.5 11.8 %copy-start.25 = (f32[1024]{0:T(1024)}, f32[1024]{0:T(1024)S(1)}, u32[]{:S(2)}) copy-start(f32[1024]{0:T(1024)S(1)} %broadcast_multiply_fusion.1) | copy-start | bytes 12292
  40.6 11.8 %slice-start.4 = ((s8[4718592]{0:T(1024)(128)(4,1)}), s8[4194304]{0:T(1024)(128)(4,1)S(1)}, s32[]{:S(2)}) async-start(s8[4718592]{0:T(1024)(128)(4,1)} %bitcast.207), calls=%async_computation.4 | async-start | bytes 8388608
  42.5 9.8 %copy-start.35 = (f32[1024]{0:T(1024)}, f32[1024]{0:T(1024)S(1)}, u32[]{:S(2)}) copy-start(f32[1024]{0:T(1024)S(1)} %fusion.48) | copy-start | bytes 12292
  42.7 9.6 %copy-start.51 = (f32[768]{0:T(1024)S(1)}, f32[768]{0:T(1024)}, u32[]{:S(2)}) copy-start(f32[768]{0:T(1024)} %convert_element_type.395) | copy-start | bytes 9220
  42.7 9.7 %slice-start.5 = ((s8[4718592]{0:T(1024)(128)(4,1)}), s8[524288]{0:T(1024)(128)(4,1)S(1)}, s32[]{:S(2)}) async-start(s8[4718592]{0:T(1024)(128)(4,1)} %bitcast.207), calls=%async_computation.5 | async-start | bytes 1048576
  61.2 46.0 %copy-start.46 = (f32[2,8]{1,0:T(2,128)}, f32[2,8]{1,0:T(2,128)S(1)}, u32[]{:S(2)}) copy-start(f32[2,8]{1,0:T(2,128)S(1)} %get-tuple-element.79) | copy-start | bytes 196
  127.1 13.4 %copy-start.18 = (bf16[1024,768]{1,0:T(8,128)(2,1)}, bf16[1024,768]{1,0:T(8,128)(2,1)S(1)}, u32[]{:S(2)}) copy-start(bf16[1024,768]{1,0:T(8,128)(2,1)S(1)} %get-tuple-element.31) | copy-start | bytes 4718596
  127.1 16.1 %copy-start.11 = (f32[1024,768]{1,0:T(8,128)S(1)}, f32[1024,768]{1,0:T(8,128)}, u32[]{:S(2)}) copy-start(f32[1024,768]{1,0:T(8,128)} %copy-done.10) | copy-start | bytes 9437188
  127.1 16.1 %copy-start.26 = (f32[1024]{0:T(1024)S(1)}, f32[1024]{0:T(1024)}, u32[]{:S(2)}) copy-start(f32[1024]{0:T(1024)} %copy-done.25) | copy-start | bytes 12292
  127.1 16.1 %copy-start.34 = (f32[768]{0:T(1024)S(1)}, f32[768]{0:T(1024)}, u32[]{:S(2)}) copy-start(f32[768]{0:T(1024)} %copy-done.33) | copy-start | bytes 9220
  127.1 16.0 %copy-start.36 = (f32[1024]{0:T(1024)S(1)}, f32[1024]{0:T(1024)}, u32[]{:S(2)}) copy-start(f32[1024]{0:T(1024)} %copy-done.35) | copy-start | bytes 12292
  127.2 16.0 %copy-start.50 = (f32[768]{0:T(1024)S(1)}, f32[768]{0:T(1024)}, u32[]{:S(2)}) copy-start(f32[768]{0:T(1024)} %copy-done.49) | copy-start | bytes 9220
  151.1 17.6 %slice-start.8 = ((s8[4718592]{0:T(1024)(128)(4,1)}), s8[4194304]{0:T(1024)(128)(4,1)S(1)}, s32[]{:S(2)}) async-start(s8[4718592]{0:T(1024)(128)(4,1)} %bitcast.211), calls=%async_computation.8 | async-start | bytes 8388608
  151.1 17.6 %slice-start.10 = ((s8[6291456]{0:T(1024)(128)(4,1)}), s8[4194304]{0:T(1024)(128)(4,1)S(1)}, s32[]{:S(2)}) async-start(s8[6291456]{0:T(1024)(128)(4,1)} %bitcast.217), calls=%async_computation.10 | async-start | bytes 8388608
  154.5 14.2 %slice-start.9 = ((s8[4718592]{0:T(1024)(128)(4,1)}), s8[524288]{0:T(1024)(128)(4,1)S(1)}, s32[]{:S(2)}) async-start(s8[4718592]{0:T(1024)(128)(4,1)} %bitcast.211), calls=%async_computation.9 | async-start | bytes 1048576
  154.5 14.2 %slice-start.11 = ((s8[6291456]{0:T(1024)(128)(4,1)}), s8[2097152]{0:T(1024)(128)(4,1)S(1)}, s32[]{:S(2)}) async-start(s8[6291456]{0:T(1024)(128)(4,1)} %bitcast.217), calls=%async_computation.11 | async-start | bytes 4194304
  154.5 128.1 %collective-permute-start.12 = (bf16[8,48,3072]{2,1,0:T(8,128)(2,1)}, bf16[8,48,3072]{2,1,0:T(8,128)(2,1)}, u32[]{:S(2)}, u32[]{:S(2)}) collective-permute-start(bf16[8,48,3072]{2,1,0:T(8,128)(2,1)} %dynamic-slice_bitcast_fusion.2), channel_id=1, source_target_pairs={{0,1},{1,0},{2,3},{3,2},{4,5},{5,4},{6,7},{7,6},{8,9},{9,8},{10,11... | collective-permute-start | bytes 7077896 | tf_op jit(solution)/shard_map/ppermute | solution.py:225
  154.8 13.9 %copy-start.13 = (f32[1024,768]{1,0:T(8,128)S(1)}, f32[1024,768]{1,0:T(8,128)}, u32[]{:S(2)}) copy-start(f32[1024,768]{1,0:T(8,128)} %get-tuple-element.37) | copy-start | bytes 9437188
  168.6 117.5 %collective-permute-start.24 = (bf16[8,192,768]{2,1,0:T(8,128)(2,1)}, bf16[8,192,768]{2,1,0:T(8,128)(2,1)}, u32[]{:S(2)}, u32[]{:S(2)}) collective-permute-start(bf16[8,192,768]{2,1,0:T(8,128)(2,1)} %dynamic-slice_bitcast_fusion.1), channel_id=1, source_target_pairs={{0,1},{1,0},{2,3},{3,2},{4,5},{5,4},{6,7},{7,6},{8,9},{9,8},{10,11... | collective-permute-start | bytes 7077896 | tf_op jit(solution)/shard_map/ppermute | solution.py:225
  273.3 20.9 %collective-permute-start = (bf16[8,48,3200]{2,1,0:T(8,128)(2,1)}, bf16[8,48,3200]{2,1,0:T(8,128)(2,1)}, u32[]{:S(2)}, u32[]{:S(2)}) collective-permute-start(bf16[8,48,3200]{2,1,0:T(8,128)(2,1)} %dynamic-slice_bitcast_fusion), channel_id=1, source_target_pairs={{0,1},{1,0},{2,3},{3,2},{4,5},{5,4},{6,7},{7,6},{8,9},{9,8},{10,11... | collective-permute-start | bytes 7372808 | tf_op jit(solution)/shard_map/ppermute | solution.py:225
  273.7 8.3 %copy-start.43 = (f32[256]{0:T(256)S(1)}, f32[256]{0:T(256)}, u32[]{:S(2)}) copy-start(f32[256]{0:T(256)} %get-tuple-element.81) | copy-start | bytes 3076
  273.7 8.3 %copy-start.45 = (f32[256]{0:T(256)S(1)}, f32[256]{0:T(256)}, u32[]{:S(2)}) copy-start(f32[256]{0:T(256)} %copy-done.44) | copy-start | bytes 3076
  273.7 8.3 %copy-start.48 = (f32[256]{0:T(256)S(1)}, f32[256]{0:T(256)}, u32[]{:S(2)}) copy-start(f32[256]{0:T(256)} %get-tuple-element.21) | copy-start | bytes 3076
  286.0 16.2 %collective-permute-start.19 = (bf16[4,48,1536]{2,1,0:T(8,128)(2,1)S(1)}, bf16[4,48,1536]{2,1,0:T(8,128)(2,1)S(1)}, u32[]{:S(2)}, u32[]{:S(2)}) collective-permute-start(bf16[4,48,1536]{2,1,0:T(8,128)(2,1)S(1)} %dynamic-slice_bitcast_fusion.5), channel_id=1, source_target_pairs={{0,2},{1,3},{2,0},{3,1},{4,6},{5,7},{6,4},{7,5},{8,10},{9,11},{10,... | collective-permute-start | bytes 1769480 | tf_op jit(solution)/shard_map/ppermute | solution.py:225
  289.6 16.2 %collective-permute-start.25 = (bf16[8,48,768]{2,1,0:T(8,128)(2,1)S(1)}, bf16[8,48,768]{2,1,0:T(8,128)(2,1)S(1)}, u32[]{:S(2)}, u32[]{:S(2)}) collective-permute-start(bf16[8,48,768]{2,1,0:T(8,128)(2,1)S(1)} %fusion.16), channel_id=1, source_target_pairs={{0,16},{16,0},{1,17},{17,1},{2,18},{18,2},{3,19},{19,3},{4,20},{20... | collective-permute-start | bytes 1769480 | tf_op jit(solution)/shard_map/ppermute | solution.py:229
  290.7 27.9 %collective-permute-start.13 = (bf16[8,48,768]{2,1,0:T(8,128)(2,1)S(1)}, bf16[8,48,768]{2,1,0:T(8,128)(2,1)S(1)}, u32[]{:S(2)}, u32[]{:S(2)}) collective-permute-start(bf16[8,48,768]{2,1,0:T(8,128)(2,1)S(1)} %fusion.20), channel_id=1, source_target_pairs={{0,16},{16,0},{1,17},{17,1},{2,18},{18,2},{3,19},{19,3},{4,20},{20... | collective-permute-start | bytes 1769480 | tf_op jit(solution)/shard_map/ppermute | solution.py:229
  292.2 26.7 %collective-permute-start.31 = (bf16[4,96,768]{2,1,0:T(8,128)(2,1)S(1)}, bf16[4,96,768]{2,1,0:T(8,128)(2,1)S(1)}, u32[]{:S(2)}, u32[]{:S(2)}) collective-permute-start(bf16[4,96,768]{2,1,0:T(8,128)(2,1)S(1)} %dynamic-slice_bitcast_fusion.4), channel_id=1, source_target_pairs={{0,2},{1,3},{2,0},{3,1},{4,6},{5,7},{6,4},{7,5},{8,10},{9,11},{10,... | collective-permute-start | bytes 1769480 | tf_op jit(solution)/shard_map/ppermute | solution.py:225
  296.7 35.7 %collective-permute-start.7 = (bf16[4,48,1664]{2,1,0:T(8,128)(2,1)S(1)}, bf16[4,48,1664]{2,1,0:T(8,128)(2,1)S(1)}, u32[]{:S(2)}, u32[]{:S(2)}) collective-permute-start(bf16[4,48,1664]{2,1,0:T(8,128)(2,1)S(1)} %dynamic-slice_bitcast_fusion.3), channel_id=1, source_target_pairs={{0,2},{1,3},{2,0},{3,1},{4,6},{5,7},{6,4},{7,5},{8,10},{9,11},{10,... | collective-permute-start | bytes 1916936 | tf_op jit(solution)/shard_map/ppermute | solution.py:225
  302.3 28.1 %collective-permute-start.1 = (bf16[8,48,768]{2,1,0:T(8,128)(2,1)S(1)}, bf16[8,48,768]{2,1,0:T(8,128)(2,1)S(1)}, u32[]{:S(2)}, u32[]{:S(2)}) collective-permute-start(bf16[8,48,768]{2,1,0:T(8,128)(2,1)S(1)} %fusion.24), channel_id=1, source_target_pairs={{0,16},{16,0},{1,17},{17,1},{2,18},{18,2},{3,19},{19,3},{4,20},{20... | collective-permute-start | bytes 1769480 | tf_op jit(solution)/shard_map/ppermute | solution.py:229
  305.9 27.2 %collective-permute-start.22 = (bf16[1,48,1536]{2,1,0:T(8,128)(2,1)S(1)}, bf16[1,48,1536]{2,1,0:T(8,128)(2,1)S(1)}, u32[]{:S(2)}, u32[]{:S(2)}) collective-permute-start(bf16[1,48,1536]{2,1,0:T(8,128)(2,1)S(1)} %get-tuple-element.54), channel_id=1, source_target_pairs={{0,12},{1,13},{2,14},{3,15},{4,8},{5,9},{6,10},{7,11},{8,4},{9,5},... | collective-permute-start | bytes 442376 | tf_op jit(solution)/shard_map/ppermute | solution.py:225
  318.5 14.6 %collective-permute-start.21 = (bf16[1,48,1536]{2,1,0:T(8,128)(2,1)S(1)}, bf16[1,48,1536]{2,1,0:T(8,128)(2,1)S(1)}, u32[]{:S(2)}, u32[]{:S(2)}) collective-permute-start(bf16[1,48,1536]{2,1,0:T(8,128)(2,1)S(1)} %get-tuple-element.55), channel_id=1, source_target_pairs={{0,8},{1,9},{2,10},{3,11},{4,12},{5,13},{6,14},{7,15},{8,0},{9,1},... | collective-permute-start | bytes 442376 | tf_op jit(solution)/shard_map/ppermute | solution.py:225
  318.8 14.4 %collective-permute-start.20 = (bf16[1,48,1536]{2,1,0:T(8,128)(2,1)S(1)}, bf16[1,48,1536]{2,1,0:T(8,128)(2,1)S(1)}, u32[]{:S(2)}, u32[]{:S(2)}) collective-permute-start(bf16[1,48,1536]{2,1,0:T(8,128)(2,1)S(1)} %get-tuple-element.53), channel_id=1, source_target_pairs={{0,4},{1,5},{2,6},{3,7},{4,0},{5,1},{6,2},{7,3},{8,12},{9,13},{10,... | collective-permute-start | bytes 442376 | tf_op jit(solution)/shard_map/ppermute | solution.py:225
  330.4 21.7 %collective-permute-start.26 = (bf16[4,48,768]{2,1,0:T(8,128)(2,1)S(1)}, bf16[4,48,768]{2,1,0:T(8,128)(2,1)S(1)}, u32[]{:S(2)}, u32[]{:S(2)}) collective-permute-start(bf16[4,48,768]{2,1,0:T(8,128)(2,1)S(1)} %dynamic-slice_bitcast_fusion.6), channel_id=1, source_target_pairs={{0,2},{1,3},{2,0},{3,1},{4,6},{5,7},{6,4},{7,5},{8,10},{9,11},{10,... | collective-permute-start | bytes 884744 | tf_op jit(solution)/shard_map/ppermute | solution.py:225
  332.4 25.7 %collective-permute-start.14 = (bf16[4,48,768]{2,1,0:T(8,128)(2,1)S(1)}, bf16[4,48,768]{2,1,0:T(8,128)(2,1)S(1)}, u32[]{:S(2)}, u32[]{:S(2)}) collective-permute-start(bf16[4,48,768]{2,1,0:T(8,128)(2,1)S(1)} %dynamic-slice_bitcast_fusion.7), channel_id=1, source_target_pairs={{0,2},{1,3},{2,0},{3,1},{4,6},{5,7},{6,4},{7,5},{8,10},{9,11},{10,... | collective-permute-start | bytes 884744 | tf_op jit(solution)/shard_map/ppermute | solution.py:225
  333.1 8.7 %collective-permute-start.34 = (bf16[1,96,768]{2,1,0:T(8,128)(2,1)S(1)}, bf16[1,96,768]{2,1,0:T(8,128)(2,1)S(1)}, u32[]{:S(2)}, u32[]{:S(2)}) collective-permute-start(bf16[1,96,768]{2,1,0:T(8,128)(2,1)S(1)} %get-tuple-element.51), channel_id=1, source_target_pairs={{0,12},{1,13},{2,14},{3,15},{4,8},{5,9},{6,10},{7,11},{8,4},{9,5},... | collective-permute-start | bytes 442376 | tf_op jit(solution)/shard_map/ppermute | solution.py:225
  333.2 17.9 %collective-permute-start.33 = (bf16[1,96,768]{2,1,0:T(8,128)(2,1)S(1)}, bf16[1,96,768]{2,1,0:T(8,128)(2,1)S(1)}, u32[]{:S(2)}, u32[]{:S(2)}) collective-permute-start(bf16[1,96,768]{2,1,0:T(8,128)(2,1)S(1)} %get-tuple-element.52), channel_id=1, source_target_pairs={{0,8},{1,9},{2,10},{3,11},{4,12},{5,13},{6,14},{7,15},{8,0},{9,1},... | collective-permute-start | bytes 442376 | tf_op jit(solution)/shard_map/ppermute | solution.py:225
  333.2 17.9 %collective-permute-start.32 = (bf16[1,96,768]{2,1,0:T(8,128)(2,1)S(1)}, bf16[1,96,768]{2,1,0:T(8,128)(2,1)S(1)}, u32[]{:S(2)}, u32[]{:S(2)}) collective-permute-start(bf16[1,96,768]{2,1,0:T(8,128)(2,1)S(1)} %get-tuple-element.50), channel_id=1, source_target_pairs={{0,4},{1,5},{2,6},{3,7},{4,0},{5,1},{6,2},{7,3},{8,12},{9,13},{10,... | collective-permute-start | bytes 442376 | tf_op jit(solution)/shard_map/ppermute | solution.py:225
  341.8 22.8 %collective-permute-start.10 = (bf16[1,48,1664]{2,1,0:T(8,128)(2,1)S(1)}, bf16[1,48,1664]{2,1,0:T(8,128)(2,1)S(1)}, u32[]{:S(2)}, u32[]{:S(2)}) collective-permute-start(bf16[1,48,1664]{2,1,0:T(8,128)(2,1)S(1)} %get-tuple-element.48), channel_id=1, source_target_pairs={{0,12},{1,13},{2,14},{3,15},{4,8},{5,9},{6,10},{7,11},{8,4},{9,5},... | collective-permute-start | bytes 479240 | tf_op jit(solution)/shard_map/ppermute | solution.py:225
  351.1 15.0 %collective-permute-start.9 = (bf16[1,48,1664]{2,1,0:T(8,128)(2,1)S(1)}, bf16[1,48,1664]{2,1,0:T(8,128)(2,1)S(1)}, u32[]{:S(2)}, u32[]{:S(2)}) collective-permute-start(bf16[1,48,1664]{2,1,0:T(8,128)(2,1)S(1)} %get-tuple-element.49), channel_id=1, source_target_pairs={{0,8},{1,9},{2,10},{3,11},{4,12},{5,13},{6,14},{7,15},{8,0},{9,1},... | collective-permute-start | bytes 479240 | tf_op jit(solution)/shard_map/ppermute | solution.py:225
  351.1 17.0 %collective-permute-start.8 = (bf16[1,48,1664]{2,1,0:T(8,128)(2,1)S(1)}, bf16[1,48,1664]{2,1,0:T(8,128)(2,1)S(1)}, u32[]{:S(2)}, u32[]{:S(2)}) collective-permute-start(bf16[1,48,1664]{2,1,0:T(8,128)(2,1)S(1)} %get-tuple-element.47), channel_id=1, source_target_pairs={{0,4},{1,5},{2,6},{3,7},{4,0},{5,1},{6,2},{7,3},{8,12},{9,13},{10,... | collective-permute-start | bytes 479240 | tf_op jit(solution)/shard_map/ppermute | solution.py:225
  352.1 5.3 %collective-permute-start.23 = (bf16[48,1536]{1,0:T(8,128)(2,1)S(1)}, bf16[48,1536]{1,0:T(8,128)(2,1)S(1)}, u32[]{:S(2)}, u32[]{:S(2)}) collective-permute-start(bf16[48,1536]{1,0:T(8,128)(2,1)S(1)} %bitcast.201), channel_id=1, source_target_pairs={{0,16},{16,0},{1,17},{17,1},{2,18},{18,2},{3,19},{19,3},{4,20},{20... | collective-permute-start | bytes 442376 | tf_op jit(solution)/shard_map/ppermute | solution.py:229
  357.4 5.1 %collective-permute-start.35 = (bf16[96,768]{1,0:T(8,128)(2,1)S(1)}, bf16[96,768]{1,0:T(8,128)(2,1)S(1)}, u32[]{:S(2)}, u32[]{:S(2)}) collective-permute-start(bf16[96,768]{1,0:T(8,128)(2,1)S(1)} %bitcast.202), channel_id=1, source_target_pairs={{0,16},{16,0},{1,17},{17,1},{2,18},{18,2},{3,19},{19,3},{4,20},{20... | collective-permute-start | bytes 442376 | tf_op jit(solution)/shard_map/ppermute | solution.py:229
  358.2 10.5 %collective-permute-start.29 = (bf16[1,48,768]{2,1,0:T(8,128)(2,1)S(1)}, bf16[1,48,768]{2,1,0:T(8,128)(2,1)S(1)}, u32[]{:S(2)}, u32[]{:S(2)}) collective-permute-start(bf16[1,48,768]{2,1,0:T(8,128)(2,1)S(1)} %get-tuple-element.57), channel_id=1, source_target_pairs={{0,12},{1,13},{2,14},{3,15},{4,8},{5,9},{6,10},{7,11},{8,4},{9,5},... | collective-permute-start | bytes 221192 | tf_op jit(solution)/shard_map/ppermute | solution.py:225
  362.6 7.1 %collective-permute-start.28 = (bf16[1,48,768]{2,1,0:T(8,128)(2,1)S(1)}, bf16[1,48,768]{2,1,0:T(8,128)(2,1)S(1)}, u32[]{:S(2)}, u32[]{:S(2)}) collective-permute-start(bf16[1,48,768]{2,1,0:T(8,128)(2,1)S(1)} %get-tuple-element.58), channel_id=1, source_target_pairs={{0,8},{1,9},{2,10},{3,11},{4,12},{5,13},{6,14},{7,15},{8,0},{9,1},... | collective-permute-start | bytes 221192 | tf_op jit(solution)/shard_map/ppermute | solution.py:225
  364.6 15.3 %collective-permute-start.2 = (bf16[4,48,768]{2,1,0:T(8,128)(2,1)S(1)}, bf16[4,48,768]{2,1,0:T(8,128)(2,1)S(1)}, u32[]{:S(2)}, u32[]{:S(2)}) collective-permute-start(bf16[4,48,768]{2,1,0:T(8,128)(2,1)S(1)} %dynamic-slice_bitcast_fusion.8), channel_id=1, source_target_pairs={{0,2},{1,3},{2,0},{3,1},{4,6},{5,7},{6,4},{7,5},{8,10},{9,11},{10,... | collective-permute-start | bytes 884744 | tf_op jit(solution)/shard_map/ppermute | solution.py:225
  366.1 6.4 %collective-permute-start.27 = (bf16[1,48,768]{2,1,0:T(8,128)(2,1)S(1)}, bf16[1,48,768]{2,1,0:T(8,128)(2,1)S(1)}, u32[]{:S(2)}, u32[]{:S(2)}) collective-permute-start(bf16[1,48,768]{2,1,0:T(8,128)(2,1)S(1)} %get-tuple-element.56), channel_id=1, source_target_pairs={{0,4},{1,5},{2,6},{3,7},{4,0},{5,1},{6,2},{7,3},{8,12},{9,13},{10,... | collective-permute-start | bytes 221192 | tf_op jit(solution)/shard_map/ppermute | solution.py:225
  368.1 6.8 %collective-permute-start.17 = (bf16[1,48,768]{2,1,0:T(8,128)(2,1)S(1)}, bf16[1,48,768]{2,1,0:T(8,128)(2,1)S(1)}, u32[]{:S(2)}, u32[]{:S(2)}) collective-permute-start(bf16[1,48,768]{2,1,0:T(8,128)(2,1)S(1)} %get-tuple-element.60), channel_id=1, source_target_pairs={{0,12},{1,13},{2,14},{3,15},{4,8},{5,9},{6,10},{7,11},{8,4},{9,5},... | collective-permute-start | bytes 221192 | tf_op jit(solution)/shard_map/ppermute | solution.py:225
  368.7 9.0 %collective-permute-start.16 = (bf16[1,48,768]{2,1,0:T(8,128)(2,1)S(1)}, bf16[1,48,768]{2,1,0:T(8,128)(2,1)S(1)}, u32[]{:S(2)}, u32[]{:S(2)}) collective-permute-start(bf16[1,48,768]{2,1,0:T(8,128)(2,1)S(1)} %get-tuple-element.61), channel_id=1, source_target_pairs={{0,8},{1,9},{2,10},{3,11},{4,12},{5,13},{6,14},{7,15},{8,0},{9,1},... | collective-permute-start | bytes 221192 | tf_op jit(solution)/shard_map/ppermute | solution.py:225
  369.6 8.0 %collective-permute-start.15 = (bf16[1,48,768]{2,1,0:T(8,128)(2,1)S(1)}, bf16[1,48,768]{2,1,0:T(8,128)(2,1)S(1)}, u32[]{:S(2)}, u32[]{:S(2)}) collective-permute-start(bf16[1,48,768]{2,1,0:T(8,128)(2,1)S(1)} %get-tuple-element.59), channel_id=1, source_target_pairs={{0,4},{1,5},{2,6},{3,7},{4,0},{5,1},{6,2},{7,3},{8,12},{9,13},{10,... | collective-permute-start | bytes 221192 | tf_op jit(solution)/shard_map/ppermute | solution.py:225
  372.6 13.6 %collective-permute-start.11 = (bf16[48,1664]{1,0:T(8,128)(2,1)S(1)}, bf16[48,1664]{1,0:T(8,128)(2,1)S(1)}, u32[]{:S(2)}, u32[]{:S(2)}) collective-permute-start(bf16[48,1664]{1,0:T(8,128)(2,1)S(1)} %bitcast.200), channel_id=1, source_target_pairs={{0,16},{16,0},{1,17},{17,1},{2,18},{18,2},{3,19},{19,3},{4,20},{20... | collective-permute-start | bytes 479240 | tf_op jit(solution)/shard_map/ppermute | solution.py:229
  377.7 5.1 %collective-permute-start.18 = (bf16[48,768]{1,0:T(8,128)(2,1)S(1)}, bf16[48,768]{1,0:T(8,128)(2,1)S(1)}, u32[]{:S(2)}, u32[]{:S(2)}) collective-permute-start(bf16[48,768]{1,0:T(8,128)(2,1)S(1)} %bitcast.204), channel_id=1, source_target_pairs={{0,16},{16,0},{1,17},{17,1},{2,18},{18,2},{3,19},{19,3},{4,20},{20... | collective-permute-start | bytes 221192 | tf_op jit(solution)/shard_map/ppermute | solution.py:229
  378.7 6.6 %collective-permute-start.30 = (bf16[48,768]{1,0:T(8,128)(2,1)S(1)}, bf16[48,768]{1,0:T(8,128)(2,1)S(1)}, u32[]{:S(2)}, u32[]{:S(2)}) collective-permute-start(bf16[48,768]{1,0:T(8,128)(2,1)S(1)} %bitcast.203), channel_id=1, source_target_pairs={{0,16},{16,0},{1,17},{17,1},{2,18},{18,2},{3,19},{19,3},{4,20},{20... | collective-permute-start | bytes 221192 | tf_op jit(solution)/shard_map/ppermute | solution.py:229
  380.0 7.7 %collective-permute-start.5 = (bf16[1,48,768]{2,1,0:T(8,128)(2,1)S(1)}, bf16[1,48,768]{2,1,0:T(8,128)(2,1)S(1)}, u32[]{:S(2)}, u32[]{:S(2)}) collective-permute-start(bf16[1,48,768]{2,1,0:T(8,128)(2,1)S(1)} %get-tuple-element.63), channel_id=1, source_target_pairs={{0,12},{1,13},{2,14},{3,15},{4,8},{5,9},{6,10},{7,11},{8,4},{9,5},... | collective-permute-start | bytes 221192 | tf_op jit(solution)/shard_map/ppermute | solution.py:225
  381.8 6.0 %collective-permute-start.4 = (bf16[1,48,768]{2,1,0:T(8,128)(2,1)S(1)}, bf16[1,48,768]{2,1,0:T(8,128)(2,1)S(1)}, u32[]{:S(2)}, u32[]{:S(2)}) collective-permute-start(bf16[1,48,768]{2,1,0:T(8,128)(2,1)S(1)} %get-tuple-element.64), channel_id=1, source_target_pairs={{0,8},{1,9},{2,10},{3,11},{4,12},{5,13},{6,14},{7,15},{8,0},{9,1},... | collective-permute-start | bytes 221192 | tf_op jit(solution)/shard_map/ppermute | solution.py:225
  382.8 5.1 %collective-permute-start.3 = (bf16[1,48,768]{2,1,0:T(8,128)(2,1)S(1)}, bf16[1,48,768]{2,1,0:T(8,128)(2,1)S(1)}, u32[]{:S(2)}, u32[]{:S(2)}) collective-permute-start(bf16[1,48,768]{2,1,0:T(8,128)(2,1)S(1)} %get-tuple-element.62), channel_id=1, source_target_pairs={{0,4},{1,5},{2,6},{3,7},{4,0},{5,1},{6,2},{7,3},{8,12},{9,13},{10,... | collective-permute-start | bytes 221192 | tf_op jit(solution)/shard_map/ppermute | solution.py:225
  388.7 5.1 %collective-permute-start.6 = (bf16[48,768]{1,0:T(8,128)(2,1)}, bf16[48,768]{1,0:T(8,128)(2,1)}, u32[]{:S(2)}, u32[]{:S(2)}) collective-permute-start(bf16[48,768]{1,0:T(8,128)(2,1)} %bitcast.26), channel_id=1, source_target_pairs={{0,16},{16,0},{1,17},{17,1},{2,18},{18,2},{3,19},{19,3},{4,20},{20... | collective-permute-start | bytes 221192 | tf_op jit(solution)/shard_map/ppermute | solution.py:229
  (44 other events, 132.0 us)

commit v2 on v0

v2 whole, which is shorter than its diff:
```python
import functools

import jax
import jax.numpy as jnp
from jax import lax
from jax.experimental import pallas as pl
from jax.experimental.pallas import tpu as pltpu
from jax.sharding import PartitionSpec as P

D = 768
HEADS = 12
HEAD_DIM = 64
FF = 3072
SEG = 8
QB = 128
MOST = 128
PAIRS = HEADS // 2
PW = 2 * HEAD_DIM

cosine_scale = 64.0
loss_scale = 32.0
norm_epsilon = 1e-12
unit_epsilon = 1e-06
masked_score = -1e30

F32 = jnp.float32
BF16 = jnp.bfloat16
VMEM = pltpu.VMEM
ANY = pl.ANY
MIB = 1 << 20


def nn(left, right):
    return lax.dot_general(left, right, (((1,), (0,)), ((), ())), preferred_element_type=F32)


def nt(left, right):
    return lax.dot_general(left, right, (((1,), (1,)), ((), ())), preferred_element_type=F32)


def tn(left, right):
    return lax.dot_general(left, right, (((0,), (0,)), ((), ())), preferred_element_type=F32)


def vspec():
    return pl.BlockSpec(memory_space=VMEM)


def sspec():
    return pl.BlockSpec(memory_space=pltpu.SMEM)


def fixed(shape):
    return pl.BlockSpec(shape, lambda *_: (0,) * len(shape))


def shape_of(shape, dtype):
    return jax.ShapeDtypeStruct(shape, dtype)


def params(mib):
    return pltpu.CompilerParams(vmem_limit_bytes=mib * MIB)


def cost(flops, moved):
    return pl.CostEstimate(flops=int(flops), bytes_accessed=int(moved), transcendentals=0)


def windows(length):
    out, packed = [], 0
    for start in range(0, length, QB):
        low, high = max(0, start - MOST), min(length, start + QB + MOST)
        out.append((start, low, high, packed))
        packed += high - low
    return out, packed


def two_heads(pair):
    first = lax.broadcasted_iota(jnp.int32, pair.shape, 1) < HEAD_DIM
    zero = jnp.zeros((), pair.dtype)
    return jnp.concatenate([jnp.where(first, pair, zero), jnp.where(first, zero, pair)], axis=0)


def pick_heads(both):
    rows = both.shape[1] // 2
    return jnp.concatenate([both[:HEAD_DIM, :rows], both[HEAD_DIM:, rows:]], axis=0).T


def column_of(row):
    return jnp.broadcast_to(row, (8, row.shape[1])).T[:, :1]


def split_low(value):
    high = value.astype(BF16)
    return high, (value - high.astype(F32)).astype(BF16)


def normalise(value):
    middle = jnp.mean(value, axis=-1, keepdims=True)
    centered = value - middle
    spread = jnp.mean(centered * centered, axis=-1, keepdims=True)
    rstd = lax.rsqrt(spread + norm_epsilon)
    return centered * rstd, rstd


def forward_kernel(
    hid,
    seg,
    wqkv_h,
    bq,
    bv,
    wout_h,
    bout,
    g1,
    b1,
    win_h,
    bin_,
    wdown_h,
    bdown,
    g2,
    b2,
    qkv_o,
    p_o,
    ctx_o,
    n1_o,
    xh1_o,
    rs1_o,
    act_o,
    dg_o,
    xh2_o,
    rs2_o,
    unit_o,
    unitf_o,
    inv_o,
    wqkv,
    wout,
    win,
    wdown,
    bias_s,
    n1_s,
    sems,
):
    r = pl.program_id(0)
    length = hid.shape[0]
    blocks, _ = windows(length)
    pairs = ((wqkv_h, wqkv), (wout_h, wout), (win_h, win), (wdown_h, wdown))
    copies = [pltpu.make_async_copy(a, b, sems.at[i]) for i, (a, b) in enumerate(pairs)]

    @pl.when(r == 0)
    def _():
        for copy in copies:
            copy.start()

    seg_row = seg[pl.ds(r, 1), :].astype(F32)
    seg_col = column_of(seg_row)
    for start, low, high, packed in blocks:
        same = seg_col[low:high] == seg_row[:, start : start + QB]
        bias_s[packed : packed + high - low, :] = jnp.where(same, 0.0, masked_score)

    @pl.when(r == 0)
    def _():
        copies[0].wait()

    x = hid[...]
    for part in range(3):
        cols = slice(part * D, (part + 1) * D)
        value = nn(x, wqkv[:, cols])
        if part == 0:
            value = value + bq[...].astype(F32)
        if part == 2:
            value = value + bv[...].astype(F32)
        qkv_o[:, cols] = value.astype(BF16)

    def one_pair(h, carry):
        def lanes(part):
            return pl.ds(pl.multiple_of(part * D + h * PW, PW), PW)

        q_all = qkv_o[:, lanes(0)] * jnp.asarray(HEAD_DIM**-0.5, BF16)
        k_all = qkv_o[:, lanes(1)]
        v_turned = qkv_o[:, lanes(2)].T
        for start, low, high, packed in blocks:
            rows = slice(packed, packed + high - low)
            both = two_heads(q_all[start : start + QB])
            scores = nt(k_all[low:high], both)
            bias = bias_s[rows, :]
            parts = []
            for head in range(2):
                own = scores[:, head * QB : (head + 1) * QB] + bias
                top = jnp.max(own, axis=0, keepdims=True)
                weights = jnp.exp(own - top)
                total = jnp.sum(weights, axis=0, keepdims=True)
                parts.append((weights * (1.0 / total)).astype(BF16))
            p = jnp.concatenate(parts, axis=1)
            p_o[h, rows, :] = p
            out = nn(v_turned[:, low:high], p)
            ctx_o[start : start + QB, pl.ds(pl.multiple_of(h * PW, PW), PW)] = pick_heads(
                out.astype(BF16)
            )
        return carry

    lax.fori_loop(0, PAIRS, one_pair, 0)

    @pl.when(r == 0)
    def _():
        copies[1].wait()

    xhat, rstd = normalise(x.astype(F32) + (nn(ctx_o[...], wout[...]) + bout[...].astype(F32)))
    xh1_o[...] = xhat.astype(BF16)
    rs1_o[...] = jnp.broadcast_to(rstd, rs1_o.shape)
    n1 = xhat * g1[...].astype(F32) + b1[...].astype(F32)
    n1_s[...] = n1
    n1_o[...] = n1.astype(BF16)

    @pl.when(r == 0)
    def _():
        copies[2].wait()

    chunk = 512

    def one_chunk(c, carry):
        cols = pl.ds(pl.multiple_of(c * chunk, chunk), chunk)
        pre = nn(n1_o[...], win[:, cols]) + bin_[:, cols].astype(F32)
        half = 0.5 + 0.5 * lax.erf(pre * 0.5**0.5)
        act_o[:, cols] = (pre * half).astype(BF16)
        bell = jnp.exp(pre * pre * -0.5) * 0.3989422804014327
        dg_o[:, cols] = (half + pre * bell).astype(BF16)
        return carry

    lax.fori_loop(0, FF // chunk, one_chunk, 0)

    @pl.when(r == 0)
    def _():
        copies[3].wait()

    branch = nn(act_o[...], wdown[...]) + bdown[...].astype(F32)
    xhat, rstd = normalise(n1_s[...] + branch)
    xh2_o[...] = xhat.astype(BF16)
    rs2_o[...] = jnp.broadcast_to(rstd, rs2_o.shape)
    out = xhat * g2[...].astype(F32) + b2[...].astype(F32)
    member = (lax.broadcasted_iota(jnp.int32, (SEG, length), 0).astype(F32) == seg_row).astype(F32)
    counts = jnp.sum(member, axis=1, keepdims=True)
    high, low = split_low(out)
    member = member.astype(BF16)
    pooled = (nn(member, high) + nn(member, low)) / counts
    inv = lax.rsqrt(jnp.mean(pooled * pooled, axis=-1, keepdims=True) + unit_epsilon)
    unit = pooled * inv
    unitf_o[...] = unit
    unit_o[...] = unit.astype(BF16)
    inv_o[...] = jnp.broadcast_to(inv / counts, inv_o.shape)


def forward(hidden, seg, weights):
    rows, length, _ = hidden.shape
    tokens = rows * length
    _, packed = windows(length)
    wqkv, bq, bv, wout, bout, g1, b1, win, bin_, wdown, bdown, g2, b2 = weights

    def per_row(n):
        return pl.BlockSpec((length, n), lambda r: (r, 0))

    out_shape = [
        shape_of((tokens, 3 * D), BF16),
        shape_of((rows, PAIRS, packed, 2 * QB), BF16),
        shape_of((tokens, D), BF16),
        shape_of((tokens, D), BF16),
        shape_of((tokens, D), BF16),
        shape_of((tokens, 128), F32),
        shape_of((tokens, FF), BF16),
        shape_of((tokens, FF), BF16),
        shape_of((tokens, D), BF16),
        shape_of((tokens, 128), F32),
        shape_of((rows, SEG, D), BF16),
        shape_of((rows, SEG, D), F32),
        shape_of((rows, SEG, 128), F32),
    ]
    out_specs = [
        per_row(3 * D),
        pl.BlockSpec((None, PAIRS, packed, 2 * QB), lambda r: (r, 0, 0, 0)),
        per_row(D),
        per_row(D),
        per_row(D),
        per_row(128),
        per_row(FF),
        per_row(FF),
        per_row(D),
        per_row(128),
        pl.BlockSpec((None, SEG, D), lambda r: (r, 0, 0)),
        pl.BlockSpec((None, SEG, D), lambda r: (r, 0, 0)),
        pl.BlockSpec((None, SEG, 128), lambda r: (r, 0, 0)),
    ]
    hbm = pl.BlockSpec(memory_space=ANY)
    in_specs = [per_row(D), fixed(seg.shape)]
    in_specs += [hbm, fixed(bq.shape), fixed(bv.shape), hbm, fixed(bout.shape)]
    in_specs += [fixed(g1.shape), fixed(b1.shape), hbm, fixed(bin_.shape), hbm]
    in_specs += [fixed(bdown.shape), fixed(g2.shape), fixed(b2.shape)]
    return pl.pallas_call(
        forward_kernel,
        name="forward",
        grid=(rows,),
        in_specs=in_specs,
        out_specs=out_specs,
        out_shape=out_shape,
        scratch_shapes=[
            VMEM(wqkv.shape, BF16),
            VMEM(wout.shape, BF16),
            VMEM(win.shape, BF16),
            VMEM(wdown.shape, BF16),
            VMEM((packed, QB), F32),
            VMEM((length, D), F32),
            pltpu.SemaphoreType.DMA((4,)),
        ],
        cost_estimate=cost(1e9, 4e6),
        compiler_params=params(62),
    )(
        hidden.reshape(tokens, D),
        seg,
        wqkv,
        bq,
        bv,
        wout,
        bout,
        g1,
        b1,
        win,
        bin_,
        wdown,
        bdown,
        g2,
        b2,
    )


def loss_kernel(
    idx, units, targets, unitf, inv, seg, g2, xh2, rs2, loss_o, gb_o, vec_o, slope_s, rows_s
):
    twin, me = idx[0], idx[1]
    count = units.shape[0] // 2
    sentences = unitf.shape[0]
    rows, length = seg.shape
    step = min(count, 256)
    factor = cosine_scale / D
    positives = units.at[pl.ds(count, count)]
    own = pl.ds(pl.multiple_of(me * sentences, sentences), sentences)

    def one_block(i, carry):
        lanes = pl.ds(pl.multiple_of(i * step, step), step)
        sims = nt(positives[...], units[lanes, :]) * factor
        top = jnp.max(sims, axis=0, keepdims=True)
        weights = jnp.exp(sims - top)
        total = jnp.sum(weights, axis=0, keepdims=True)
        hit = lax.broadcasted_iota(jnp.int32, sims.shape, 0) == targets[:, lanes]
        picked = jnp.sum(jnp.where(hit, sims, 0.0), axis=0, keepdims=True)
        loss_o[:, lanes] = top + jnp.log(total) - picked
        slope = loss_scale * (weights * (1.0 / total) - hit.astype(F32))
        slope_s[:, lanes] = slope.astype(BF16)
        return carry

    if count == step:
        one_block(0, 0)
    else:
        lax.fori_loop(0, count // step, one_block, 0)

    @pl.when(twin == 0)
    def _():
        def part(i, carry):
            lanes = pl.ds(pl.multiple_of(i * step, step), step)
            rows_s[lanes, :] = tn(slope_s[:, lanes], positives[...])
            return carry

        lax.fori_loop(0, count // step, part, 0)
        rows_s[pl.ds(0, sentences), :] = rows_s[own, :]

    @pl.when(twin == 1)
    def _():
        rows_s[pl.ds(0, sentences), :] = nn(slope_s[own, :], units[pl.ds(0, count), :])

    gu = rows_s[pl.ds(0, sentences), :] * factor
    unit = unitf[...]
    gs = inv[:, :1] * (gu - unit * jnp.mean(gu * unit, axis=-1, keepdims=True))
    gy = gs * g2[...].astype(F32)
    u = gy - jnp.mean(gy, axis=-1, keepdims=True)
    gain = jnp.zeros((1, D), F32)
    shift = jnp.zeros((1, D), F32)
    summed = jnp.zeros((1, D), F32)
    for r in range(rows):
        part = slice(r * SEG, (r + 1) * SEG)
        tok = slice(r * length, (r + 1) * length)
        seg_row = seg[r : r + 1, :]
        hits = lax.broadcasted_iota(jnp.int32, (SEG, length), 0) == seg_row
        member = hits.astype(F32).astype(BF16)
        counts = jnp.sum(hits.astype(F32), axis=1, keepdims=True)
        xhat_low = xh2[tok, :]
        gain += jnp.sum(nn(member, xhat_low) * gs[part], axis=0, keepdims=True)
        shift += jnp.sum(counts * gs[part], axis=0, keepdims=True)
        xhat = xhat_low.astype(F32)
        high, low = split_low(u[part])
        spread = tn(member, high) + tn(member, low)
        inner = jnp.mean(spread * xhat, axis=-1, keepdims=True)
        grad = rs2[tok, :1] * (spread - xhat * inner)
        grad_low = grad.astype(BF16)
        gb_o[tok, :] = grad_low
        summed += jnp.sum(grad_low.astype(F32), axis=0, keepdims=True)
    vec_o[...] = jnp.concatenate([summed, gain, shift, jnp.zeros((5, D), F32)], axis=0)


def loss_stage(idx, units, targets, unitf, inv, seg, g2, xh2, rs2):
    tokens = xh2.shape[0]
    count = units.shape[0] // 2
    return pl.pallas_call(
        loss_kernel,
        name="loss",
        in_specs=[sspec()] + [vspec()] * 8,
        out_specs=[vspec()] * 3,
        out_shape=[
            shape_of((1, count), F32),
            shape_of((tokens, D), BF16),
            shape_of((8, D), F32),
        ],
        scratch_shapes=[VMEM((count, count), BF16), VMEM((count, D), F32)],
        cost_estimate=cost(1e8, 1e6),
        compiler_params=params(48),
    )(idx, units, targets, unitf, inv, seg, g2, xh2, rs2)


def pre_kernel(gb, wdown, dg, out):
    out[...] = (nt(gb[...], wdown[...]) * dg[...].astype(F32)).astype(BF16)


def pre_stage(gb, wdown, dg):
    tokens = gb.shape[0]
    n = 768
    return pl.pallas_call(
        pre_kernel,
        name="grad_pre",
        grid=(FF // n,),
        in_specs=[
            fixed(gb.shape),
            pl.BlockSpec((n, D), lambda j: (j, 0)),
            pl.BlockSpec((tokens, n), lambda j: (0, j)),
        ],
        out_specs=pl.BlockSpec((tokens, n), lambda j: (0, j)),
        out_shape=shape_of((tokens, FF), BF16),
        cost_estimate=cost(1e8, 1e6),
        compiler_params=params(40),
    )(gb, wdown, dg)


def normed_kernel(gp, win, gb, xh1, rs1, g1, wout, ga_o, gc_o, vec_o):
    grad = nt(gp[...], win[...]) + gb[...].astype(F32)
    xhat = xh1[...].astype(F32)
    gain = jnp.sum(grad * xhat, axis=0, keepdims=True)
    shift = jnp.sum(grad, axis=0, keepdims=True)
    gy = grad * g1[...].astype(F32)
    inner = jnp.mean(gy * xhat, axis=-1, keepdims=True)
    total = rs1[:, :1] * (gy - jnp.mean(gy, axis=-1, keepdims=True) - xhat * inner)
    low = total.astype(BF16)
    ga_o[...] = low
    summed = jnp.sum(low.astype(F32), axis=0, keepdims=True)
    gc_o[...] = nt(low, wout[...]).astype(BF16)
    rows = jnp.concatenate([summed, gain, shift, jnp.zeros((5, D), F32)], axis=0)

    @pl.when(pl.program_id(0) == 0)
    def _():
        vec_o[...] = rows

    @pl.when(pl.program_id(0) > 0)
    def _():
        vec_o[...] += rows


def normed_stage(gp, win, gb, xh1, rs1, g1, wout):
    tokens = gp.shape[0]
    m = 512

    def rows(n):
        return pl.BlockSpec((m, n), lambda i: (i, 0))

    return pl.pallas_call(
        normed_kernel,
        name="grad_normed",
        grid=(tokens // m,),
        in_specs=[
            rows(FF),
            fixed(win.shape),
            rows(D),
            rows(D),
            rows(128),
            fixed(g1.shape),
            fixed(wout.shape),
        ],
        out_specs=[rows(D), rows(D), fixed((8, D))],
        out_shape=[
            shape_of((tokens, D), BF16),
            shape_of((tokens, D), BF16),
            shape_of((8, D), F32),
        ],
        cost_estimate=cost(1e8, 1e6),
        compiler_params=params(48),
    )(gp, win, gb, xh1, rs1, g1, wout)


def attend_back_kernel(q_ref, k_ref, v_ref, g_ref, p_ref, out_ref, dk_acc, dv_acc):
    length = q_ref.shape[0]
    blocks, _ = windows(length)
    scale = HEAD_DIM**-0.5
    dk_acc[...] = jnp.zeros_like(dk_acc)
    dv_acc[...] = jnp.zeros_like(dv_acc)
    k_turned = k_ref[...].T
    for start, low, high, packed in blocks:
        q2 = two_heads(q_ref[start : start + QB, :])
        g2 = two_heads(g_ref[start : start + QB, :])
        p_low = p_ref[packed : packed + high - low, :]
        gp = nt(v_ref[low:high, :], g2)
        p = p_low.astype(F32)
        weighted = p * gp
        inner = jnp.sum(weighted, axis=0, keepdims=True)
        ds = (weighted - p * inner).astype(BF16)
        dv_acc[low:high, :] += nn(p_low, g2)
        dk_acc[low:high, :] += nn(ds, q2)
        dq = nn(k_turned[:, low:high], ds) * scale
        out_ref[0, start : start + QB, :] = pick_heads(dq.astype(BF16))
    out_ref[1] = (dk_acc[...] * scale).astype(BF16)
    out_ref[2] = dv_acc[...].astype(BF16)


def attend_back(qkv, grad_context, probs, rows, length):
    _, packed = windows(length)

    def block(part):
        return pl.BlockSpec((length, PW), lambda r, h: (r, part * PAIRS + h))

    return pl.pallas_call(
        attend_back_kernel,
        name="attend_back",
        grid=(rows, PAIRS),
        in_specs=[
            block(0),
            block(1),
            block(2),
            pl.BlockSpec((length, PW), lambda r, h: (r, h)),
            pl.BlockSpec((None, None, packed, 2 * QB), lambda r, h: (r, h, 0, 0)),
        ],
        out_specs=pl.BlockSpec((3, length, PW), lambda r, h: (0, r, h)),
        out_shape=shape_of((3, rows * length, D), BF16),
        scratch_shapes=[VMEM((length, PW), F32), VMEM((length, PW), F32)],
        cost_estimate=cost(1e8, 1e6),
        compiler_params=params(32),
    )(qkv, qkv, qkv, grad_context, probs)


def hidden_kernel(dqkv, wqkv, ga, out):
    total = ga[...].astype(F32)
    for part in range(3):
        total = total + nt(dqkv[part], wqkv[:, part * D : (part + 1) * D])
    out[...] = total.astype(BF16)


def hidden_stage(dqkv, wqkv, ga):
    tokens = ga.shape[0]
    m = 512
    return pl.pallas_call(
        hidden_kernel,
        name="hidden_grad",
        grid=(tokens // m,),
        in_specs=[
            pl.BlockSpec((3, m, D), lambda i: (0, i, 0)),
            fixed(wqkv.shape),
            pl.BlockSpec((m, D), lambda i: (i, 0)),
        ],
        out_specs=pl.BlockSpec((m, D), lambda i: (i, 0)),
        out_shape=shape_of((tokens, D), BF16),
        cost_estimate=cost(1e8, 1e6),
        compiler_params=params(40),
    )(dqkv, wqkv, ga)


HALF_A = (2, 8, 48, D)
HALF_B = (8, 48, 2 * D)


def place(core, value, keep, send):
    @pl.when(core == 0)
    def _():
        value(0, keep)
        value(1, send)

    @pl.when(core == 1)
    def _():
        value(1, keep)
        value(0, send)


def down_kernel(idx, act, gb, ka, kb, sa, sb):
    total = tn(act[...], gb[...]).astype(BF16)

    def store(parity, refs):
        a, b = refs
        for pair in range(2):
            base = (2 * pair + parity) * 192
            for q in range(4):
                piece = total[base + q * 48 : base + (q + 1) * 48]
                if q < 2:
                    a[q, pair] = piece
                else:
                    b[pair, :, (q - 2) * D : (q - 1) * D] = piece

    place(idx[2], store, (ka, kb), (sa, sb))


def down_stage(idx, act, gb):
    tokens = gb.shape[0]
    spec_a = pl.BlockSpec((2, 2, 48, D), lambda j: (0, j, 0, 0))
    spec_b = pl.BlockSpec((2, 48, 2 * D), lambda j: (j, 0, 0))
    return pl.pallas_call(
        down_kernel,
        name="grad_w_down",
        grid=(4,),
        in_specs=[sspec(), pl.BlockSpec((tokens, D), lambda j: (0, j)), fixed(gb.shape)],
        out_specs=[spec_a, spec_b] * 2,
        out_shape=[shape_of(HALF_A, BF16), shape_of(HALF_B, BF16)] * 2,
        cost_estimate=cost(1e8, 1e6),
        compiler_params=params(40),
    )(idx, act, gb)


def store_column(j, total, core, ka, kb, sa, sb):
    def store(parity, refs):
        a, b = refs

        @pl.when(j < 2)
        def _():
            for i in range(8):
                a[0, i] = total[(2 * i + parity) * 48 : (2 * i + parity + 1) * 48]

        @pl.when(j >= 2)
        def _():
            for i in range(8):
                b[i] = total[(2 * i + parity) * 48 : (2 * i + parity + 1) * 48]

    place(core, store, (ka, kb), (sa, sb))


SPEC_A = ((1, 8, 48, D), lambda j: (jnp.minimum(j, 1), 0, 0, 0))
SPEC_B = ((8, 48, D), lambda j: (0, 0, jnp.maximum(j - 2, 0)))


def in_kernel(idx, n1, gp, ka, kb, sa, sb, vec_o):
    j = pl.program_id(0)
    total = tn(n1[...], gp[...]).astype(BF16)
    store_column(j, total, idx[2], ka, kb, sa, sb)
    sums = tn(gp[...], jnp.ones((gp.shape[0], 128), BF16))
    lane = lax.broadcasted_iota(jnp.int32, (48, 128), 1)
    for block in range(4):
        acc = jnp.zeros((48, 128), F32)
        for q in range(4):
            base = block * 192 + q * 48
            acc = acc + jnp.where(lane == 8 + q, sums[base : base + 48], 0.0)
        vec_o[block] = acc


def in_stage(idx, n1, gp):
    tokens = gp.shape[0]
    return pl.pallas_call(
        in_kernel,
        name="grad_w_in",
        grid=(4,),
        in_specs=[sspec(), fixed(n1.shape), pl.BlockSpec((tokens, D), lambda j: (0, j))],
        out_specs=[pl.BlockSpec(*SPEC_A), pl.BlockSpec(*SPEC_B)] * 2
        + [pl.BlockSpec((4, 48, 128), lambda j: (j, 0, 0))],
        out_shape=[shape_of(HALF_A, BF16), shape_of(HALF_B, BF16)] * 2
        + [shape_of((16, 48, 128), F32)],
        cost_estimate=cost(1e8, 1e6),
        compiler_params=params(40),
    )(idx, n1, gp)


def last_kernel(idx, hid, dqkv, ctx, ga, vec2, vec1, vec_in, ka, kb, sa, sb, kv, sv, sums_s):
    j = pl.program_id(0)

    @pl.when(j < 3)
    def _():
        total = tn(hid[...], dqkv[...]).astype(BF16)
        store_column(j, total, idx[2], ka, kb, sa, sb)
        summed = jnp.sum(dqkv[...].astype(F32), axis=0, keepdims=True)

        @pl.when(j == 0)
        def _():
            sums_s[...] = jnp.zeros_like(sums_s)
            sums_s[0:1, :] = summed

        @pl.when(j == 2)
        def _():
            sums_s[1:2, :] = summed

    @pl.when(j == 3)
    def _():
        total = tn(ctx[...], ga[...]).astype(BF16)
        store_column(j, total, idx[2], ka, kb, sa, sb)
        sums_s[2:5, :] = vec1[0:3, :]
        sums_s[5:8, :] = vec2[0:3, :]
        turned = sums_s[...].T

        def store(parity, refs):
            (out,) = refs
            for i in range(8):
                block = 2 * i + parity
                out[i] = (turned[block * 48 : (block + 1) * 48] + vec_in[block]).astype(BF16)

        place(idx[2], store, (kv,), (sv,))


def last_stage(idx, hid, dqkv, ctx, ga, vec2, vec1, vec_in):
    tokens = ga.shape[0]
    return pl.pallas_call(
        last_kernel,
        name="grad_w_qkv",
        grid=(4,),
        in_specs=[
            sspec(),
            fixed(hid.shape),
            pl.BlockSpec((None, tokens, D), lambda j: (jnp.minimum(j, 2), 0, 0)),
            fixed(ctx.shape),
            fixed(ga.shape),
            fixed(vec2.shape),
            fixed(vec1.shape),
            fixed(vec_in.shape),
        ],
        out_specs=[pl.BlockSpec(*SPEC_A), pl.BlockSpec(*SPEC_B)] * 2 + [fixed((8, 48, 128))] * 2,
        out_shape=[shape_of(HALF_A, BF16), shape_of(HALF_B, BF16)] * 2
        + [shape_of((8, 48, 128), BF16)] * 2,
        scratch_shapes=[VMEM((128, D), F32)],
        cost_estimate=cost(1e8, 1e6),
        compiler_params=params(48),
    )(idx, hid, dqkv, ctx, ga, vec2, vec1, vec_in)


def swap_dp(value, flip):
    devices = lax.axis_size("dp")
    return lax.ppermute(value, "dp", [(i, i ^ flip) for i in range(devices)])


def swap_twin(value):
    return lax.ppermute(value, "twin", [(0, 1), (1, 0)])


def plus(*values):
    total = values[0].astype(F32)
    for value in values[1:]:
        total = total + value.astype(F32)
    return total.astype(BF16)


def call_small(kernel, name, idx, operands, outs):
    return pl.pallas_call(
        kernel,
        name=name,
        in_specs=[sspec()] + [vspec()] * len(operands),
        out_specs=[vspec()] * len(outs),
        out_shape=[shape_of(shape, dtype) for shape, dtype in outs],
        cost_estimate=cost(1e6, 1e5),
        compiler_params=params(32),
    )(idx, *operands)


def core_kernel(idx, ka, kb, ra, rb, as_o, ak_o, bs_o, bk_o):
    twin, y = idx[0], idx[3]
    as_o[...] = plus(ka[1 - twin], ra[1 - twin])
    ak_o[...] = plus(ka[twin], ra[twin])
    bs_o[0] = plus(kb[1 - y], rb[1 - y])
    bk_o[0] = plus(kb[y], rb[y])


def core_stage(idx, ka, kb, ra, rb):
    spec_a = pl.BlockSpec((2, 2, 48, D), lambda z: (0, z, 0, 0))
    spec_b = pl.BlockSpec((2, 48, 2 * D), lambda z: (z, 0, 0))
    out_a = pl.BlockSpec((2, 48, D), lambda z: (z, 0, 0))
    out_b = pl.BlockSpec((1, 48, 2 * D), lambda z: (z, 0, 0))
    return pl.pallas_call(
        core_kernel,
        name="core_sum",
        grid=(4,),
        in_specs=[sspec(), spec_a, spec_b, spec_a, spec_b],
        out_specs=[out_a, out_a, out_b, out_b],
        out_shape=[shape_of((8, 48, D), BF16)] * 2 + [shape_of((4, 48, 2 * D), BF16)] * 2,
        cost_estimate=cost(1e6, 1e5),
        compiler_params=params(32),
    )(idx, ka, kb, ra, rb)


def first_kernel(idx, ak, ar, bk, br, as_o, ak_o, b0, b1, b2, b3):
    y, z = idx[3], idx[4]
    for i in range(4):
        as_o[i] = plus(ak[2 * i + 1 - y], ar[2 * i + 1 - y])
        ak_o[i] = plus(ak[2 * i + y], ar[2 * i + y])
    for flip, out in enumerate((b0, b1, b2, b3)):
        out[...] = plus(bk[z ^ flip], br[z ^ flip])


def second_kernel(idx, ak, ar, b0, b1, b2, b3, a0, a1, a2, a3, b_o):
    z = idx[4]
    for flip, out in enumerate((a0, a1, a2, a3)):
        out[...] = plus(ak[z ^ flip], ar[z ^ flip])
    b_o[...] = plus(b0[...], b1[...], b2[...], b3[...])


def third_kernel(idx, a0, a1, a2, a3, a_o):
    a_o[...] = plus(a0[...], a1[...], a2[...], a3[...])


def fan_out(parts):
    return [swap_dp(part, flip * 4) for flip, part in enumerate(parts) if flip]


def exchange(idx, ka, kb, sa, sb):
    ra, rb = swap_dp(sa, 1), swap_dp(sb, 1)
    a_send, a_keep, b_send, b_keep = core_stage(idx, ka, kb, ra, rb)
    a_recv, b_recv = swap_twin(a_send), swap_dp(b_send, 2)
    quarter, wide = ((4, 48, D), BF16), ((48, 2 * D), BF16)
    a_send, a_keep, *b = call_small(
        first_kernel, "sum_x_y", idx, (a_keep, a_recv, b_keep, b_recv), [quarter] * 2 + [wide] * 4
    )
    a_recv, b_recv = swap_dp(a_send, 2), fan_out(b)
    *a, b_own = call_small(
        second_kernel,
        "sum_y_z",
        idx,
        (a_keep, a_recv, b[0], *b_recv),
        [((48, D), BF16)] * 4 + [wide],
    )
    a_recv, b_other = fan_out(a), swap_twin(b_own)
    (a_own,) = call_small(third_kernel, "sum_z", idx, (a[0], *a_recv), [((48, D), BF16)])
    return a_own, swap_twin(a_own), b_own, b_other


def vec_kernel(idx, keep, recv, s_o, k_o):
    y = idx[3]
    for i in range(4):
        s_o[i] = plus(keep[2 * i + 1 - y], recv[2 * i + 1 - y])
        k_o[i] = plus(keep[2 * i + y], recv[2 * i + y])


def vec_next_kernel(idx, keep, recv, o0, o1, o2, o3):
    z = idx[4]
    for flip, out in enumerate((o0, o1, o2, o3)):
        out[...] = plus(keep[z ^ flip], recv[z ^ flip])


def exchange_vec(idx, keep, send):
    recv = swap_dp(send, 1)
    send, keep = call_small(vec_kernel, "vec_core", idx, (keep, recv), [((4, 48, 128), BF16)] * 2)
    parts = call_small(
        vec_next_kernel, "vec_y", idx, (keep, swap_dp(send, 2)), [((48, 128), BF16)] * 4
    )
    recv = fan_out(parts)
    (own,) = call_small(third_kernel, "vec_z", idx, (parts[0], *recv), [((48, 128), BF16)])
    return own, swap_twin(own)


def final_kernel(idx, a, ao, b, bo, out):
    twin = idx[0]
    both = b[...].astype(F32) + bo[...].astype(F32)
    if out.shape[0] == 48:
        out[:, 2 * D :] = both

        @pl.when(twin == 0)
        def _():
            out[:, :D] = a[...].astype(F32)
            out[:, D : 2 * D] = ao[...].astype(F32)

        @pl.when(twin == 1)
        def _():
            out[:, :D] = ao[...].astype(F32)
            out[:, D : 2 * D] = a[...].astype(F32)
    else:
        out[96:144, :] = both[:, :D]
        out[144:, :] = both[:, D:]

        @pl.when(twin == 0)
        def _():
            out[:48, :] = a[...].astype(F32)
            out[48:96, :] = ao[...].astype(F32)

        @pl.when(twin == 1)
        def _():
            out[:48, :] = ao[...].astype(F32)
            out[48:96, :] = a[...].astype(F32)


def final_last_kernel(idx, a, ao, b, bo, v, vo, qkv_o, out_o, vec_o):
    twin = idx[0]
    both = b[...].astype(F32) + bo[...].astype(F32)
    qkv_o[:, 2 * D :] = both[:, :D]
    out_o[...] = both[:, D:]

    @pl.when(twin == 0)
    def _():
        qkv_o[:, :D] = a[...].astype(F32)
        qkv_o[:, D : 2 * D] = ao[...].astype(F32)

    @pl.when(twin == 1)
    def _():
        qkv_o[:, :D] = ao[...].astype(F32)
        qkv_o[:, D : 2 * D] = a[...].astype(F32)

    both = v[...].astype(F32) + vo[...].astype(F32)
    vec_o[...] = jnp.concatenate([both, jnp.zeros((80, 128), F32)], axis=0).T[:16]


def add_low(*parts):
    return lax.optimization_barrier(plus(*parts))


def digits_of(devices):
    out, rest = [], devices // 2
    while rest > 1:
        size = 4 if rest % 4 == 0 else 2
        out.append(size)
        rest //= size
    return out


def pick(value, index, axis):
    return lax.dynamic_index_in_dim(value, index, axis, keepdims=False)


def scatter(grad):
    devices = lax.axis_size("dp")
    me = lax.axis_index("dp")
    value = grad.reshape(devices, grad.shape[0] // devices, grad.shape[1])
    unit = 1
    for size in [2] + digits_of(devices):
        mine = (me // unit) % size
        view = value.reshape((value.shape[0] // size, size) + value.shape[1:])
        parts = [pick(view, mine, 1)]
        for flip in range(1, size):
            parts.append(swap_dp(pick(view, mine ^ flip, 1), flip * unit))
        value = add_low(*parts)
        unit *= size
    value = value[0]
    return value.astype(F32) + swap_twin(value).astype(F32)


def body(
    hidden,
    segment_ids,
    targets,
    w_qkv,
    b_query,
    b_value,
    w_out,
    b_out,
    ln1_gain,
    ln1_bias,
    w_in,
    b_in,
    w_down,
    b_down,
    ln2_gain,
    ln2_bias,
):
    row_count, length, width = hidden.shape
    tokens = row_count * length
    devices = lax.axis_size("dp")
    everyone = lax.axis_size(("twin", "dp"))
    me = lax.axis_index("dp")
    twin = lax.axis_index("twin")
    idx = jnp.stack([twin, me, me % 2, (me // 2) % 2, me // 4]).astype(jnp.int32)
    row = lambda v: v.reshape(1, -1)
    weights = (w_qkv, row(b_query), row(b_value), w_out, row(b_out), row(ln1_gain), row(ln1_bias))
    weights += (w_in, row(b_in), w_down, row(b_down), row(ln2_gain), row(ln2_bias))
    qkv, probs, ctx, n1, xh1, rs1, act, dg, xh2, rs2, unit, unitf, inv = forward(
        hidden, segment_ids, weights
    )
    sentences = row_count * SEG
    gathered = lax.all_gather(unit.reshape(sentences, width), ("twin", "dp"), axis=0, tiled=True)
    losses, gb, vec2 = loss_stage(
        idx,
        gathered,
        row(targets),
        unitf.reshape(sentences, width),
        inv.reshape(sentences, 128),
        segment_ids,
        row(ln2_gain),
        xh2,
        rs2,
    )
    share = losses.shape[1] // everyone
    losses = lax.dynamic_slice_in_dim(
        losses[0], lax.axis_index(("twin", "dp")) * share, share, 0
    )
    flat = hidden.reshape(tokens, width)
    if devices == 16 and width == D:
        down = exchange(idx, *down_stage(idx, act, gb))
        gp = pre_stage(gb, w_down, dg)
        *into, vec_in = in_stage(idx, n1, gp)
        into = exchange(idx, *into)
        ga, gc, vec1 = normed_stage(gp, w_in, gb, xh1, rs1, row(ln1_gain), w_out)
        dqkv = attend_back(qkv, gc, probs, row_count, length)
        *last, kv, sv = last_stage(idx, flat, dqkv, ctx, ga, vec2, vec1, vec_in)
        last = exchange(idx, *last)
        small = exchange_vec(idx, kv, sv)
        hidden_grad = hidden_stage(dqkv, w_qkv, ga)
        (grad_w_down,) = call_small(final_kernel, "final_down", idx, down, [((192, D), F32)])
        (grad_w_in,) = call_small(final_kernel, "final_in", idx, into, [((48, FF), F32)])
        grad_w_qkv, grad_w_out, vec = call_small(
            final_last_kernel,
            "final_qkv",
            idx,
            (*last, *small),
            [((48, 3 * D), F32), ((48, D), F32), ((16, 128), F32)],
        )
        vec = vec[:, :48]
        vecs = [vec[i] for i in range(8)]
        grad_b_in = vec[8:12].reshape(-1)
    else:
        gp = pre_stage(gb, w_down, dg)
        ga, gc, vec1 = normed_stage(gp, w_in, gb, xh1, rs1, row(ln1_gain), w_out)
        dqkv = attend_back(qkv, gc, probs, row_count, length)
        hidden_grad = hidden_stage(dqkv, w_qkv, ga)
        grad_w_down = scatter(tn(act, gb).astype(BF16))
        grad_w_in = scatter(tn(n1, gp).astype(BF16))
        wide = jnp.concatenate([dqkv[0], dqkv[1], dqkv[2]], axis=1)
        grad_w_qkv = scatter(tn(flat, wide).astype(BF16))
        grad_w_out = scatter(tn(ctx, ga).astype(BF16))
        sums = jnp.sum(dqkv, axis=1, dtype=F32)
        vec = jnp.concatenate([sums[0:1], sums[2:3], vec1[:3], vec2[:3]])
        vec = scatter(jnp.pad(vec, ((0, 120), (0, 0))).T.astype(BF16)).T
        vecs = [vec[i] for i in range(8)]
        bias = jnp.sum(gp, axis=0, dtype=F32)
        grad_b_in = scatter(jnp.broadcast_to(bias[:, None], (FF, 128)).astype(BF16))[:, 0]
    return (
        losses,
        hidden_grad.reshape(row_count, length, width),
        grad_w_qkv,
        vecs[0],
        vecs[1],
        grad_w_out,
        vecs[2],
        vecs[3],
        vecs[4],
        grad_w_in,
        grad_b_in,
        grad_w_down,
        vecs[5],
        vecs[6],
        vecs[7],
    )


def solution(mesh):
    whole = (P(),) * 14
    placed = (P(("twin", "dp"), None, None), P(("twin", "dp"), None)) + whole
    return jax.shard_map(
        body,
        mesh=mesh,
        in_specs=placed,
        out_specs=(
            P(("twin", "dp")),
            P(("twin", "dp"), None, None),
            P("dp", None),
            P("dp"),
            P("dp"),
            P("dp", None),
            P("dp"),
            P("dp"),
            P("dp"),
            P("dp", None),
            P("dp"),
            P("dp", None),
            P("dp"),
            P("dp"),
            P("dp"),
        ),
        check_vma=False,
    )
```

time: 678 us -> 350 us (0.52); the launches traced: 668 us -> 348 us
  waiting for transfers between devices: 228 us -> 53.6 us
  matrix products: 170 us -> 0 us
  Pallas kernels: 0 us -> 157 us
  blocking collectives: 113 us -> 45.7 us
  other arithmetic: 65.2 us -> 0.01 us
  starting transfers between devices: 0.2 us -> 48.1 us
  local copies, waits for them, and re-layouts: 75.5 us -> 42.7 us
  between operations: 16.2 us -> 1.21 us
    reduce_scatter x3 -> x0, waiting for transfers between devices: 189 us -> none  [the longest x1 114 us: body(): lax.psum_scatter(grad_w_down, 'dp', scatter_dimension=0, tiled=True)]
    dot_general x31 -> x0, matrix products: 170 us -> none  [the longest x5 38.7 us: contract_cols(): lax.dot_general(left, right, (((1,), (1,)), ((), ())), preferred_element_...]
    pallas_call x0 -> x27, Pallas kernels: none -> 157 us  [the longest x1 52 us: forward(): pl.pallas_call(forward_kernel, name='forward', grid=(rows,), in_specs=in_...]
    unnamed x1 -> x0, blocking collectives: 61.8 us -> none
    ppermute x0 -> x45, waiting for transfers between devices: none -> 53.6 us  [the longest x35 44.8 us: swap_dp(): return lax.ppermute(value, 'dp', [(i, i ^ flip) for i in range(devices)])]
    ppermute x0 -> x45, starting transfers between devices: none -> 48.1 us  [the longest x35 37.6 us: swap_dp(): return lax.ppermute(value, 'dp', [(i, i ^ flip) for i in range(devices)])]
    psum x1 -> x0, waiting for transfers between devices: 38.7 us -> none  [body(): lax.psum(grad_w_qkv.astype(jnp.bfloat16), 'twin').astype(jnp.float32)]
    convert_element_type x28 -> x0, other arithmetic: 37.6 us -> none  [the longest x2 14.2 us: attend_backward(): grad_scores = (prob_rows * (grad_prob - inner)).astype(jnp.bfloat16)]
  transfers between devices with their start and end apart: 5 -> 45, of which waited for: 3 -> 6; matrix products, arithmetic and copies ran while one was open for 25% -> 1% of each run, Pallas kernels for 0% -> 22%
where the time goes in v2:
time: 350 us; the launch traced here: 348 us
  Pallas kernels  157 us (45%)
  waiting for transfers between devices  53.6 us (15%)
  starting transfers between devices  48.1 us (14%)
  blocking collectives  45.7 us (13%)
  local copies, waits for them, and re-layouts  42.7 us (12%)
    pallas_call x1, Pallas kernels, forward(): pl.pallas_call(forward_kernel, name='forward', grid=(rows,), in_specs=in_...  52 us
    all_gather x1, blocking collectives, body(): lax.all_gather(unit.reshape(sentences, width), ('twin', 'dp'), axis=0, ti...  45.7 us
    ppermute x35, waiting for transfers between devices, swap_dp(): return lax.ppermute(value, 'dp', [(i, i ^ flip) for i in range(devices)])  44.8 us
    ppermute x35, starting transfers between devices, swap_dp(): return lax.ppermute(value, 'dp', [(i, i ^ flip) for i in range(devices)])  37.6 us
    unnamed x104, local copies, waits for them, and re-layouts  28.7 us
    pallas_call x1, Pallas kernels, attend_back(): pl.pallas_call(attend_back_kernel, name='attend_back', grid=(rows, PAIRS)...  20.2 us
    pallas_call x15, Pallas kernels, call_small(): pl.pallas_call(kernel, name=name, in_specs=[sspec()] + [vspec()] * len(op...  16 us
    pallas_call x1, Pallas kernels, normed_stage(): pl.pallas_call(normed_kernel, name='grad_normed', grid=(tokens // m,), in...  13.9 us
  transfers between devices with their start and end apart: 45, of which 6 were waited for; matrix products, arithmetic and copies ran while one was open for 1% of the time, Pallas kernels for 22%

profile of v2, /device:TPU:0, one launch (start us, length us, event | category | flops | bytes accessed | tf_op | source)
XLA Modules:
  0.0 348.4 jit_solution(11422116179986889977)
XLA Ops:
  0.7 1.3 reshape.86.g1
  1.9 1.3 reshape.90.g2
  3.2 1.3 reshape.83.bq
  4.5 1.3 reshape.84.bv
  5.8 1.3 reshape.85.bout
  7.0 1.3 reshape.87.b1
  8.3 1.3 reshape.89.bdown
  9.6 1.3 reshape.91.b2
  10.9 1.3 reshape.88.bin_
  12.1 52.0 %forward.1 = (bf16[1024,2304]{1,0:T(8,128)(2,1)}, bf16[2,6,1280,256]{3,2,1,0:T(8,128)(2,1)}, bf16[1024,768]{1,0:T(8,128)(2,1)}, bf16[1024,768]{1,0:T(8,128)(2,1)...) custom-call(bf16[1024,768]{1,0:T(8,128)(2,1)} %bitcast.36, ...), custom_call_target="tpu_custom_call" | custom-call | flops 1000000000 | bytes 4000000 | tf_op jit(solution)/shard_map/forward/pallas_call | solution.py:296
  64.2 45.7 %all_gather.3.units = bf16[512,768]{1,0:T(8,128)(2,1)S(1)} all-gather(bf16[16,768]{1,0:T(8,128)(2,1)} %bitcast.39), channel_id=1, replica_groups=mesh['twin'=2,'dp'=16] {'twin','dp'}, dimensions={0}, use_global_device_ids=true | all-gather | bytes 811008 | tf_op jit(solution)/shard_map/all_gather | solution.py:975
  110.0 1.4 copy-done.11
  112.9 3.5 loss.1
  116.4 2.9 copy-done.3
  119.3 7.7 %grad_pre.1.gp = bf16[1024,3072]{1,0:T(8,128)(2,1)S(1)} custom-call(bf16[1024,768]{1,0:T(8,128)(2,1)S(1)} %get-tuple-element.110.gb, bf16[3072,768]{1,0:T(8,128)(2,1)S(1)} %copy-done.3, bf16[1024,3072]{1,0:T(8,128)(2,1)} %get-tuple-element.111.dg), custom_call_target="tpu_custom_call" | custom-call | flops 100000000 | bytes 1000000 | tf_op jit(solution)/shard_map/grad_pre/pallas_call | solution.py:432
  127.1 13.8 %grad_w_in.1 = (bf16[2,8,48,768]{3,2,1,0:T(8,128)(2,1)S(1)}, bf16[8,48,1536]{2,1,0:T(8,128)(2,1)S(1)}, bf16[2,8,48,768]{3,2,1,0:T(8,128)(2,1)}, bf16[8,48,1536]{2,1,0:T(8,128)(2,1)}, f32[16,48,128]{2,1,0:T(8,128)S(1)}) custom-call(s32[5]{0:T(128)S(1)} %stack.23.idx, bf16[1024,768]{1,0:T(8,128)(2,1)S(1)} %copy-done.12, bf16[1024,3072]{1,0:T(8,128)(2,1)S(1)} %grad_pre.1.gp), custom_call_target="tpu_custom_call" | custom-call | flops 100000000 | bytes 1000000 | tf_op jit(solution)/shard_map/grad_w_in/pallas_call | solution.py:663
  141.0 1.0 copy-done.15
  142.0 1.0 copy-done.17
  143.6 13.9 %grad_normed.1 = (bf16[1024,768]{1,0:T(8,128)(2,1)S(1)}, bf16[1024,768]{1,0:T(8,128)(2,1)S(1)}, f32[8,768]{1,0:T(8,128)S(1)}) custom-call(bf16[1024,3072]{1,0:T(8,128)(2,1)} %copy-done, bf16[768,3072]{1,0:T(8,128)(2,1)} %win.1, bf16[1024,768]{1,0:T(8,128)(2,1)} %copy-done.5, bf16[1024,768]{1,0:T(8,128)(2,1)} %get-tuple-element.112.xh1, ...), custom_call_target="tpu_custom_call" | custom-call | flops 100000000 | bytes 1000000 | tf_op jit(solution)/shard_map/grad_normed/pallas_call | solution.py:478
  157.5 3.8 %copy-done.7 = bf16[2,6,1280,256]{3,2,1,0:T(8,128)(2,1)S(1)} copy-done((bf16[2,6,1280,256]{3,2,1,0:T(8,128)(2,1)S(1)}, bf16[2,6,1280,256]{3,2,1,0:T(8,128)(2,1)}, u32[]{:S(2)}) %copy-start.7) | copy-done | bytes 7864344
  161.3 20.2 %attend_back.1.dqkv = bf16[3,1024,768]{2,1,0:T(8,128)(2,1)S(1)} custom-call(bf16[1024,2304]{1,0:T(8,128)(2,1)S(1)} %bitcast.30, bf16[1024,2304]{1,0:T(8,128)(2,1)S(1)} %bitcast.30, bf16[1024,2304]{1,0:T(8,128)(2,1)S(1)} %bitcast.30, bf16[1024,768]{1,0:T(8,128)(2,1)S(1)} %get-tuple-element.114.g_ref, bf16[2,6,1280,256]{3,2,1,0:T(8,128)(2,1)S(1)} %copy-done.7), custom_call_target="tpu_custom_call" | custom-call | flops 100000000 | bytes 1000000 | tf_op jit(solution)/shard_map/attend_back/pallas_call | solution.py:532
  181.6 2.2 copy-done.1
  183.8 11.7 %grad_w_qkv.1 = (bf16[2,8,48,768]{3,2,1,0:T(8,128)(2,1)S(1)}, bf16[8,48,1536]{2,1,0:T(8,128)(2,1)S(1)}, bf16[2,8,48,768]{3,2,1,0:T(8,128)(2,1)}, bf16[8,48,1536]...) custom-call(s32[5]{0:T(128)S(1)} %stack.23.idx, bf16[1024,768]{1,0:T(8,128)(2,1)} %bitcast.37, ...), custom_call_target="tpu_custom_call" | custom-call | flops 100000000 | bytes 1000000 | tf_op jit(solution)/shard_map/grad_w_qkv/pallas_call | solution.py:714
  197.0 7.3 %grad_w_down.1 = (bf16[2,8,48,768]{3,2,1,0:T(8,128)(2,1)S(1)}, bf16[8,48,1536]{2,1,0:T(8,128)(2,1)S(1)}, bf16[2,8,48,768]{3,2,1,0:T(8,128)(2,1)S(1)}, bf16[8,48,1536]{2,1,0:T(8,128)(2,1)S(1)}) custom-call(s32[5]{0:T(128)S(1)} %stack.23.idx, bf16[1024,3072]{1,0:T(8,128)(2,1)S(1)} %bitcast.32, bf16[1024,768]{1,0:T(8,128)(2,1)S(1)} %copy-done.6), custom_call_target="tpu_custom_call" | custom-call | flops 100000000 | bytes 1000000 | tf_op jit(solution)/shard_map/grad_w_down/pallas_call | solution.py:614
  205.0 2.8 core_sum.4
  208.4 1.3 core_sum.3
  209.8 1.7 collective-permute-start.2
  211.5 1.9 collective-permute-start.3
  213.4 1.3 core_sum.5
  215.2 8.8 %collective-permute-done.21.ar = bf16[8,48,768]{2,1,0:T(8,128)(2,1)S(1)} collective-permute-done((bf16[8,48,768]{2,1,0:T(8,128)(2,1)S(1)}, bf16[8,48,768]{2,1,0:T(8,128)(2,1)S(1)}, u32[]{:S(2)}, u32[]{:S(2)}) %collective-permute-start.21) | collective-permute-done | bytes 589856 | tf_op jit(solution)/shard_map/ppermute | solution.py:743
  224.7 2.1 collective-permute-start.14
  227.6 22.3 %collective-permute-done.14.recv = bf16[4,48,128]{2,1,0:T(8,128)(2,1)S(1)} collective-permute-done((bf16[4,48,128]{2,1,0:T(8,128)(2,1)S(1)}, bf16[4,48,128]{2,1,0:T(8,128)(2,1)S(1)}, u32[]{:S(2)}, u32[]{:S(2)}) %collective-permute-start.14) | collective-permute-done | bytes 49184 | tf_op jit(solution)/shard_map/ppermute | solution.py:739
  250.5 2.1 collective-permute-start.15
  253.4 3.3 collective-permute-done.15.a1
  257.6 2.0 collective-permute-start.26
  259.8 2.2 collective-permute-start.6
  262.0 2.0 collective-permute-start.7
  264.8 1.5 collective-permute-done.26.b3
  266.3 1.7 collective-permute-start.23
  268.5 8.5 %collective-permute-done.6.b2 = bf16[48,1536]{1,0:T(8,128)(2,1)S(1)} collective-permute-done((bf16[48,1536]{1,0:T(8,128)(2,1)S(1)}, bf16[48,1536]{1,0:T(8,128)(2,1)S(1)}, u32[]{:S(2)}, u32[]{:S(2)}) %collective-permute-start.6) | collective-permute-done | bytes 147488 | tf_op jit(solution)/shard_map/ppermute | solution.py:739
  277.0 2.6 collective-permute-start.38
  279.6 2.6 collective-permute-start.39
  282.3 1.3 sum_y_z.3
  283.6 9.0 %collective-permute-done.38.b2 = bf16[48,1536]{1,0:T(8,128)(2,1)S(1)} collective-permute-done((bf16[48,1536]{1,0:T(8,128)(2,1)S(1)}, bf16[48,1536]{1,0:T(8,128)(2,1)S(1)}, u32[]{:S(2)}, u32[]{:S(2)}) %collective-permute-start.38) | collective-permute-done | bytes 147488 | tf_op jit(solution)/shard_map/ppermute | solution.py:739
  292.6 1.4 collective-permute-start.10
  294.1 3.0 collective-permute-start.16
  297.1 2.4 collective-permute-start.17
  299.5 1.3 sum_y_z.4
  300.8 1.3 sum_y_z.5
  304.0 2.0 collective-permute-start.28
  306.6 2.4 collective-permute-start.29
  310.3 1.6 collective-permute-start.12
  319.3 2.0 collective-permute-start.41
  321.2 2.4 collective-permute-start.42
  323.6 1.6 collective-permute-start.11
  325.3 1.2 dynamic-slice_bitcast_fusion
  326.5 2.3 copy-done.2
  328.9 1.4 copy-done.9
  330.3 5.3 %hidden_grad.1 = bf16[1024,768]{1,0:T(8,128)(2,1)} custom-call(bf16[3,1024,768]{2,1,0:T(8,128)(2,1)S(1)} %copy-done.2, bf16[768,2304]{1,0:T(8,128)(2,1)S(1)} %copy-done.4, bf16[1024,768]{1,0:T(8,128)(2,1)S(1)} %copy-done.9), custom_call_target="tpu_custom_call" | custom-call | flops 100000000 | bytes 1000000 | tf_op jit(solution)/shard_map/hidden_grad/pallas_call | solution.py:561
  337.0 1.6 collective-permute-start.44
  340.1 1.6 collective-permute-start.43
  341.7 1.9 final_qkv.1
  344.8 1.8 final_in.1
  346.6 1.8 final_down.1
  (174 shorter events, 25.7 us)
Async XLA Ops:
  12.1 97.9 %copy-start.35 = (bf16[1,768]{1,0:T(2,128)(2,1)S(1)}, bf16[1,768]{1,0:T(2,128)(2,1)}, u32[]{:S(2)}) copy-start(bf16[1,768]{1,0:T(2,128)(2,1)} %reshape.90.g2) | copy-start | bytes 4612
  12.1 97.9 %copy-start.36 = (s32[2,512]{1,0:T(2,128)S(1)}, s32[2,512]{1,0:T(2,128)}, u32[]{:S(2)}) copy-start(s32[2,512]{1,0:T(2,128)} %seg.3) | copy-start | bytes 12292
  12.1 97.9 %copy-start.44 = (s32[256]{0:T(256)S(1)}, s32[256]{0:T(256)}, u32[]{:S(2)}) copy-start(s32[256]{0:T(256)} %param.18) | copy-start | bytes 3076
  64.2 45.8 %copy-start.20 = (f32[1024,128]{1,0:T(8,128)S(1)}, f32[1024,128]{1,0:T(8,128)}, u32[]{:S(2)}) copy-start(f32[1024,128]{1,0:T(8,128)} %get-tuple-element.107.rs2) | copy-start | bytes 1572868
  116.4 10.7 %copy-start.5 = (bf16[1024,768]{1,0:T(8,128)(2,1)}, bf16[1024,768]{1,0:T(8,128)(2,1)S(1)}, u32[]{:S(2)}) copy-start(bf16[1024,768]{1,0:T(8,128)(2,1)S(1)} %get-tuple-element.110.gb) | copy-start | bytes 4718596
  116.4 10.7 %copy-start.47 = (f32[1,256]{1,0:T(1,128)}, f32[1,256]{1,0:T(1,128)S(1)}, u32[]{:S(2)}) copy-start(f32[1,256]{1,0:T(1,128)S(1)} %get-tuple-element.108) | copy-start | bytes 3076
  127.1 13.9 %copy-start = (bf16[1024,3072]{1,0:T(8,128)(2,1)}, bf16[1024,3072]{1,0:T(8,128)(2,1)S(1)}, u32[]{:S(2)}) copy-start(bf16[1024,3072]{1,0:T(8,128)(2,1)S(1)} %grad_pre.1.gp) | copy-start | bytes 18874372
  127.1 16.5 %copy-start.10 = (bf16[768,768]{1,0:T(8,128)(2,1)S(1)}, bf16[768,768]{1,0:T(8,128)(2,1)}, u32[]{:S(2)}) copy-start(bf16[768,768]{1,0:T(8,128)(2,1)} %wout.1) | copy-start | bytes 3538948
  127.1 16.4 %copy-start.19 = (f32[1024,128]{1,0:T(8,128)S(1)}, f32[1024,128]{1,0:T(8,128)}, u32[]{:S(2)}) copy-start(f32[1024,128]{1,0:T(8,128)} %get-tuple-element.113.rs1) | copy-start | bytes 1572868
  127.1 16.4 %copy-start.34 = (bf16[1,768]{1,0:T(2,128)(2,1)S(1)}, bf16[1,768]{1,0:T(2,128)(2,1)}, u32[]{:S(2)}) copy-start(bf16[1,768]{1,0:T(2,128)(2,1)} %reshape.86.g1) | copy-start | bytes 4612
  143.0 61.7 %collective-permute-start.19 = (bf16[2,8,48,768]{3,2,1,0:T(8,128)(2,1)}, bf16[2,8,48,768]{3,2,1,0:T(8,128)(2,1)}, u32[]{:S(2)}, u32[]{:S(2)}) collective-permute-start(bf16[2,8,48,768]{3,2,1,0:T(8,128)(2,1)} %get-tuple-element.154), channel_id=1, source_target_pairs={{0,1},{1,0},{2,3},{3,2},{4,5},{5,4},{6,7},{7,6},{8,9},{9,8},{10,11... | collective-permute-start | bytes 3538952 | tf_op jit(solution)/shard_map/ppermute | solution.py:739
  143.4 61.6 %collective-permute-start.20 = (bf16[8,48,1536]{2,1,0:T(8,128)(2,1)}, bf16[8,48,1536]{2,1,0:T(8,128)(2,1)}, u32[]{:S(2)}, u32[]{:S(2)}) collective-permute-start(bf16[8,48,1536]{2,1,0:T(8,128)(2,1)} %get-tuple-element.155), channel_id=1, source_target_pairs={{0,1},{1,0},{2,3},{3,2},{4,5},{5,4},{6,7},{7,6},{8,9},{9,8},{10,11... | collective-permute-start | bytes 3538952 | tf_op jit(solution)/shard_map/ppermute | solution.py:739
  143.5 13.9 %slice-start = ((s8[4718592]{0:T(1024)(128)(4,1)}), s8[4194304]{0:T(1024)(128)(4,1)S(1)}, s32[]{:S(2)}) async-start(s8[4718592]{0:T(1024)(128)(4,1)} %bitcast.29), calls=%async_computation | async-start | bytes 8388608
  143.6 13.9 %slice-start.1 = ((s8[4718592]{0:T(1024)(128)(4,1)}), s8[524288]{0:T(1024)(128)(4,1)S(1)}, s32[]{:S(2)}) async-start(s8[4718592]{0:T(1024)(128)(4,1)} %bitcast.29), calls=%async_computation.1 | async-start | bytes 1048576
  143.6 53.4 %slice-start.2 = ((s8[6291456]{0:T(1024)(128)(4,1)}), s8[4194304]{0:T(1024)(128)(4,1)S(1)}, s32[]{:S(2)}) async-start(s8[6291456]{0:T(1024)(128)(4,1)} %bitcast.31), calls=%async_computation.2 | async-start | bytes 8388608
  157.5 24.1 %copy-start.8 = (bf16[1024,768]{1,0:T(8,128)(2,1)}, bf16[1024,768]{1,0:T(8,128)(2,1)S(1)}, u32[]{:S(2)}) copy-start(bf16[1024,768]{1,0:T(8,128)(2,1)S(1)} %get-tuple-element.116.ga) | copy-start | bytes 4718596
  161.3 35.7 %slice-start.3 = ((s8[6291456]{0:T(1024)(128)(4,1)}), s8[2097152]{0:T(1024)(128)(4,1)S(1)}, s32[]{:S(2)}) async-start(s8[6291456]{0:T(1024)(128)(4,1)} %bitcast.31), calls=%async_computation.3 | async-start | bytes 4194304
  183.7 13.3 %copy-start.6 = (bf16[1024,768]{1,0:T(8,128)(2,1)S(1)}, bf16[1024,768]{1,0:T(8,128)(2,1)}, u32[]{:S(2)}) copy-start(bf16[1024,768]{1,0:T(8,128)(2,1)} %copy-done.5) | copy-start | bytes 4718596
  196.5 11.8 %collective-permute-start = (bf16[2,8,48,768]{3,2,1,0:T(8,128)(2,1)}, bf16[2,8,48,768]{3,2,1,0:T(8,128)(2,1)S(1)}, u32[]{:S(2)}, u32[]{:S(2)}) collective-permute-start(bf16[2,8,48,768]{3,2,1,0:T(8,128)(2,1)} %get-tuple-element.124), channel_id=1, source_target_pairs={{0,1},{1,0},{2,3},{3,2},{4,5},{5,4},{6,7},{7,6},{8,9},{9,8},{10,11... | collective-permute-start | bytes 3538952 | tf_op jit(solution)/shard_map/ppermute | solution.py:739
  196.8 11.5 %collective-permute-start.1 = (bf16[8,48,1536]{2,1,0:T(8,128)(2,1)}, bf16[8,48,1536]{2,1,0:T(8,128)(2,1)S(1)}, u32[]{:S(2)}, u32[]{:S(2)}) collective-permute-start(bf16[8,48,1536]{2,1,0:T(8,128)(2,1)} %get-tuple-element.125), channel_id=1, source_target_pairs={{0,1},{1,0},{2,3},{3,2},{4,5},{5,4},{6,7},{7,6},{8,9},{9,8},{10,11... | collective-permute-start | bytes 3538952 | tf_op jit(solution)/shard_map/ppermute | solution.py:739
  204.4 5.4 %collective-permute-start.32 = (bf16[2,8,48,768]{3,2,1,0:T(8,128)(2,1)S(1)}, bf16[2,8,48,768]{3,2,1,0:T(8,128)(2,1)S(1)}, u32[]{:S(2)}, u32[]{:S(2)}) collective-permute-start(bf16[2,8,48,768]{3,2,1,0:T(8,128)(2,1)S(1)} %get-tuple-element.174), channel_id=1, source_target_pairs={{0,1},{1,0},{2,3},{3,2},{4,5},{5,4},{6,7},{7,6},{8,9},{9,8},{10,11... | collective-permute-start | bytes 3538952 | tf_op jit(solution)/shard_map/ppermute | solution.py:739
  204.8 6.7 %collective-permute-start.33 = (bf16[8,48,1536]{2,1,0:T(8,128)(2,1)S(1)}, bf16[8,48,1536]{2,1,0:T(8,128)(2,1)S(1)}, u32[]{:S(2)}, u32[]{:S(2)}) collective-permute-start(bf16[8,48,1536]{2,1,0:T(8,128)(2,1)S(1)} %get-tuple-element.175), channel_id=1, source_target_pairs={{0,1},{1,0},{2,3},{3,2},{4,5},{5,4},{6,7},{7,6},{8,9},{9,8},{10,11... | collective-permute-start | bytes 3538952 | tf_op jit(solution)/shard_map/ppermute | solution.py:739
  207.8 16.2 %collective-permute-start.21 = (bf16[8,48,768]{2,1,0:T(8,128)(2,1)S(1)}, bf16[8,48,768]{2,1,0:T(8,128)(2,1)S(1)}, u32[]{:S(2)}, u32[]{:S(2)}) collective-permute-start(bf16[8,48,768]{2,1,0:T(8,128)(2,1)S(1)} %get-tuple-element.157), channel_id=1, source_target_pairs={{0,16},{16,0},{1,17},{17,1},{2,18},{18,2},{3,19},{19,3},{4,20},{20... | collective-permute-start | bytes 1769480 | tf_op jit(solution)/shard_map/ppermute | solution.py:743
  208.3 16.3 %collective-permute-start.22 = (bf16[4,48,1536]{2,1,0:T(8,128)(2,1)S(1)}, bf16[4,48,1536]{2,1,0:T(8,128)(2,1)S(1)}, u32[]{:S(2)}, u32[]{:S(2)}) collective-permute-start(bf16[4,48,1536]{2,1,0:T(8,128)(2,1)S(1)} %get-tuple-element.159), channel_id=1, source_target_pairs={{0,2},{1,3},{2,0},{3,1},{4,6},{5,7},{6,4},{7,5},{8,10},{9,11},{10,... | collective-permute-start | bytes 1769480 | tf_op jit(solution)/shard_map/ppermute | solution.py:739
  208.3 6.4 %collective-permute-start.13 = (bf16[8,48,128]{2,1,0:T(8,128)(2,1)S(1)}, bf16[8,48,128]{2,1,0:T(8,128)(2,1)S(1)}, u32[]{:S(2)}, u32[]{:S(2)}) collective-permute-start(bf16[8,48,128]{2,1,0:T(8,128)(2,1)S(1)} %get-tuple-element.142), channel_id=1, source_target_pairs={{0,1},{1,0},{2,3},{3,2},{4,5},{5,4},{6,7},{7,6},{8,9},{9,8},{10,11... | collective-permute-start | bytes 294920 | tf_op jit(solution)/shard_map/ppermute | solution.py:739
  209.8 40.1 %collective-permute-start.2 = (bf16[8,48,768]{2,1,0:T(8,128)(2,1)S(1)}, bf16[8,48,768]{2,1,0:T(8,128)(2,1)S(1)}, u32[]{:S(2)}, u32[]{:S(2)}) collective-permute-start(bf16[8,48,768]{2,1,0:T(8,128)(2,1)S(1)} %get-tuple-element.127), channel_id=1, source_target_pairs={{0,16},{16,0},{1,17},{17,1},{2,18},{18,2},{3,19},{19,3},{4,20},{20... | collective-permute-start | bytes 1769480 | tf_op jit(solution)/shard_map/ppermute | solution.py:743
  211.5 39.0 %collective-permute-start.3 = (bf16[4,48,1536]{2,1,0:T(8,128)(2,1)S(1)}, bf16[4,48,1536]{2,1,0:T(8,128)(2,1)S(1)}, u32[]{:S(2)}, u32[]{:S(2)}) collective-permute-start(bf16[4,48,1536]{2,1,0:T(8,128)(2,1)S(1)} %get-tuple-element.129), channel_id=1, source_target_pairs={{0,2},{1,3},{2,0},{3,1},{4,6},{5,7},{6,4},{7,5},{8,10},{9,11},{10,... | collective-permute-start | bytes 1769480 | tf_op jit(solution)/shard_map/ppermute | solution.py:739
  214.8 42.8 %collective-permute-start.34 = (bf16[8,48,768]{2,1,0:T(8,128)(2,1)S(1)}, bf16[8,48,768]{2,1,0:T(8,128)(2,1)S(1)}, u32[]{:S(2)}, u32[]{:S(2)}) collective-permute-start(bf16[8,48,768]{2,1,0:T(8,128)(2,1)S(1)} %get-tuple-element.177), channel_id=1, source_target_pairs={{0,16},{16,0},{1,17},{17,1},{2,18},{18,2},{3,19},{19,3},{4,20},{20... | collective-permute-start | bytes 1769480 | tf_op jit(solution)/shard_map/ppermute | solution.py:743
  224.1 35.5 %collective-permute-start.35 = (bf16[4,48,1536]{2,1,0:T(8,128)(2,1)S(1)}, bf16[4,48,1536]{2,1,0:T(8,128)(2,1)S(1)}, u32[]{:S(2)}, u32[]{:S(2)}) collective-permute-start(bf16[4,48,1536]{2,1,0:T(8,128)(2,1)S(1)} %get-tuple-element.179), channel_id=1, source_target_pairs={{0,2},{1,3},{2,0},{3,1},{4,6},{5,7},{6,4},{7,5},{8,10},{9,11},{10,... | collective-permute-start | bytes 1769480 | tf_op jit(solution)/shard_map/ppermute | solution.py:739
  224.7 25.2 %collective-permute-start.14 = (bf16[4,48,128]{2,1,0:T(8,128)(2,1)S(1)}, bf16[4,48,128]{2,1,0:T(8,128)(2,1)S(1)}, u32[]{:S(2)}, u32[]{:S(2)}) collective-permute-start(bf16[4,48,128]{2,1,0:T(8,128)(2,1)S(1)} %get-tuple-element.144), channel_id=1, source_target_pairs={{0,2},{1,3},{2,0},{3,1},{4,6},{5,7},{6,4},{7,5},{8,10},{9,11},{10,... | collective-permute-start | bytes 147464 | tf_op jit(solution)/shard_map/ppermute | solution.py:739
  249.9 9.9 %collective-permute-start.24 = (bf16[48,1536]{1,0:T(8,128)(2,1)S(1)}, bf16[48,1536]{1,0:T(8,128)(2,1)S(1)}, u32[]{:S(2)}, u32[]{:S(2)}) collective-permute-start(bf16[48,1536]{1,0:T(8,128)(2,1)S(1)} %get-tuple-element.163), channel_id=1, source_target_pairs={{0,4},{1,5},{2,6},{3,7},{4,0},{5,1},{6,2},{7,3},{8,12},{9,13},{10,... | collective-permute-start | bytes 442376 | tf_op jit(solution)/shard_map/ppermute | solution.py:739
  249.9 12.1 %collective-permute-start.25 = (bf16[48,1536]{1,0:T(8,128)(2,1)S(1)}, bf16[48,1536]{1,0:T(8,128)(2,1)S(1)}, u32[]{:S(2)}, u32[]{:S(2)}) collective-permute-start(bf16[48,1536]{1,0:T(8,128)(2,1)S(1)} %get-tuple-element.164), channel_id=1, source_target_pairs={{0,8},{1,9},{2,10},{3,11},{4,12},{5,13},{6,14},{7,15},{8,0},{9,1},... | collective-permute-start | bytes 442376 | tf_op jit(solution)/shard_map/ppermute | solution.py:739
  250.5 6.2 %collective-permute-start.15 = (bf16[48,128]{1,0:T(8,128)(2,1)S(1)}, bf16[48,128]{1,0:T(8,128)(2,1)S(1)}, u32[]{:S(2)}, u32[]{:S(2)}) collective-permute-start(bf16[48,128]{1,0:T(8,128)(2,1)S(1)} %get-tuple-element.146), channel_id=1, source_target_pairs={{0,4},{1,5},{2,6},{3,7},{4,0},{5,1},{6,2},{7,3},{8,12},{9,13},{10,... | collective-permute-start | bytes 36872 | tf_op jit(solution)/shard_map/ppermute | solution.py:739
  257.3 22.3 %collective-permute-start.4 = (bf16[4,48,768]{2,1,0:T(8,128)(2,1)S(1)}, bf16[4,48,768]{2,1,0:T(8,128)(2,1)S(1)}, u32[]{:S(2)}, u32[]{:S(2)}) collective-permute-start(bf16[4,48,768]{2,1,0:T(8,128)(2,1)S(1)} %get-tuple-element.131), channel_id=1, source_target_pairs={{0,2},{1,3},{2,0},{3,1},{4,6},{5,7},{6,4},{7,5},{8,10},{9,11},{10,... | collective-permute-start | bytes 884744 | tf_op jit(solution)/shard_map/ppermute | solution.py:739
  257.6 8.7 %collective-permute-start.26 = (bf16[48,1536]{1,0:T(8,128)(2,1)S(1)}, bf16[48,1536]{1,0:T(8,128)(2,1)S(1)}, u32[]{:S(2)}, u32[]{:S(2)}) collective-permute-start(bf16[48,1536]{1,0:T(8,128)(2,1)S(1)} %get-tuple-element.165), channel_id=1, source_target_pairs={{0,12},{1,13},{2,14},{3,15},{4,8},{5,9},{6,10},{7,11},{8,4},{9,5},... | collective-permute-start | bytes 442376 | tf_op jit(solution)/shard_map/ppermute | solution.py:739
  259.6 8.5 %collective-permute-start.5 = (bf16[48,1536]{1,0:T(8,128)(2,1)S(1)}, bf16[48,1536]{1,0:T(8,128)(2,1)S(1)}, u32[]{:S(2)}, u32[]{:S(2)}) collective-permute-start(bf16[48,1536]{1,0:T(8,128)(2,1)S(1)} %get-tuple-element.133), channel_id=1, source_target_pairs={{0,4},{1,5},{2,6},{3,7},{4,0},{5,1},{6,2},{7,3},{8,12},{9,13},{10,... | collective-permute-start | bytes 442376 | tf_op jit(solution)/shard_map/ppermute | solution.py:739
  259.8 17.2 %collective-permute-start.6 = (bf16[48,1536]{1,0:T(8,128)(2,1)S(1)}, bf16[48,1536]{1,0:T(8,128)(2,1)S(1)}, u32[]{:S(2)}, u32[]{:S(2)}) collective-permute-start(bf16[48,1536]{1,0:T(8,128)(2,1)S(1)} %get-tuple-element.134), channel_id=1, source_target_pairs={{0,8},{1,9},{2,10},{3,11},{4,12},{5,13},{6,14},{7,15},{8,0},{9,1},... | collective-permute-start | bytes 442376 | tf_op jit(solution)/shard_map/ppermute | solution.py:739
  262.0 15.0 %collective-permute-start.7 = (bf16[48,1536]{1,0:T(8,128)(2,1)S(1)}, bf16[48,1536]{1,0:T(8,128)(2,1)S(1)}, u32[]{:S(2)}, u32[]{:S(2)}) collective-permute-start(bf16[48,1536]{1,0:T(8,128)(2,1)S(1)} %get-tuple-element.135), channel_id=1, source_target_pairs={{0,12},{1,13},{2,14},{3,15},{4,8},{5,9},{6,10},{7,11},{8,4},{9,5},... | collective-permute-start | bytes 442376 | tf_op jit(solution)/shard_map/ppermute | solution.py:739
  266.3 27.8 %collective-permute-start.23 = (bf16[4,48,768]{2,1,0:T(8,128)(2,1)S(1)}, bf16[4,48,768]{2,1,0:T(8,128)(2,1)S(1)}, u32[]{:S(2)}, u32[]{:S(2)}) collective-permute-start(bf16[4,48,768]{2,1,0:T(8,128)(2,1)S(1)} %get-tuple-element.161), channel_id=1, source_target_pairs={{0,2},{1,3},{2,0},{3,1},{4,6},{5,7},{6,4},{7,5},{8,10},{9,11},{10,... | collective-permute-start | bytes 884744 | tf_op jit(solution)/shard_map/ppermute | solution.py:739
  268.0 29.1 %collective-permute-start.36 = (bf16[4,48,768]{2,1,0:T(8,128)(2,1)S(1)}, bf16[4,48,768]{2,1,0:T(8,128)(2,1)S(1)}, u32[]{:S(2)}, u32[]{:S(2)}) collective-permute-start(bf16[4,48,768]{2,1,0:T(8,128)(2,1)S(1)} %get-tuple-element.181), channel_id=1, source_target_pairs={{0,2},{1,3},{2,0},{3,1},{4,6},{5,7},{6,4},{7,5},{8,10},{9,11},{10,... | collective-permute-start | bytes 884744 | tf_op jit(solution)/shard_map/ppermute | solution.py:739
  277.0 6.5 %collective-permute-start.37 = (bf16[48,1536]{1,0:T(8,128)(2,1)S(1)}, bf16[48,1536]{1,0:T(8,128)(2,1)S(1)}, u32[]{:S(2)}, u32[]{:S(2)}) collective-permute-start(bf16[48,1536]{1,0:T(8,128)(2,1)S(1)} %get-tuple-element.183), channel_id=1, source_target_pairs={{0,4},{1,5},{2,6},{3,7},{4,0},{5,1},{6,2},{7,3},{8,12},{9,13},{10,... | collective-permute-start | bytes 442376 | tf_op jit(solution)/shard_map/ppermute | solution.py:739
  277.0 15.6 %collective-permute-start.38 = (bf16[48,1536]{1,0:T(8,128)(2,1)S(1)}, bf16[48,1536]{1,0:T(8,128)(2,1)S(1)}, u32[]{:S(2)}, u32[]{:S(2)}) collective-permute-start(bf16[48,1536]{1,0:T(8,128)(2,1)S(1)} %get-tuple-element.184), channel_id=1, source_target_pairs={{0,8},{1,9},{2,10},{3,11},{4,12},{5,13},{6,14},{7,15},{8,0},{9,1},... | collective-permute-start | bytes 442376 | tf_op jit(solution)/shard_map/ppermute | solution.py:739
  279.6 13.0 %collective-permute-start.39 = (bf16[48,1536]{1,0:T(8,128)(2,1)S(1)}, bf16[48,1536]{1,0:T(8,128)(2,1)S(1)}, u32[]{:S(2)}, u32[]{:S(2)}) collective-permute-start(bf16[48,1536]{1,0:T(8,128)(2,1)S(1)} %get-tuple-element.185), channel_id=1, source_target_pairs={{0,12},{1,13},{2,14},{3,15},{4,8},{5,9},{6,10},{7,11},{8,4},{9,5},... | collective-permute-start | bytes 442376 | tf_op jit(solution)/shard_map/ppermute | solution.py:739
  282.3 44.2 %copy-start.4 = (bf16[768,2304]{1,0:T(8,128)(2,1)S(1)}, bf16[768,2304]{1,0:T(8,128)(2,1)}, u32[]{:S(2)}) copy-start(bf16[768,2304]{1,0:T(8,128)(2,1)} %wqkv.1) | copy-start | bytes 10616836
  283.6 18.6 %copy-start.23 = (bf16[48,768]{1,0:T(8,128)(2,1)}, bf16[48,768]{1,0:T(8,128)(2,1)S(1)}, u32[]{:S(2)}) copy-start(bf16[48,768]{1,0:T(8,128)(2,1)S(1)} %get-tuple-element.136.a0) | copy-start | bytes 221188
  283.6 22.4 %collective-permute-start.8 = (bf16[48,768]{1,0:T(8,128)(2,1)S(1)}, bf16[48,768]{1,0:T(8,128)(2,1)S(1)}, u32[]{:S(2)}, u32[]{:S(2)}) collective-permute-start(bf16[48,768]{1,0:T(8,128)(2,1)S(1)} %get-tuple-element.137), channel_id=1, source_target_pairs={{0,4},{1,5},{2,6},{3,7},{4,0},{5,1},{6,2},{7,3},{8,12},{9,13},{10,... | collective-permute-start | bytes 221192 | tf_op jit(solution)/shard_map/ppermute | solution.py:739
  292.6 16.5 %collective-permute-start.9 = (bf16[48,768]{1,0:T(8,128)(2,1)S(1)}, bf16[48,768]{1,0:T(8,128)(2,1)S(1)}, u32[]{:S(2)}, u32[]{:S(2)}) collective-permute-start(bf16[48,768]{1,0:T(8,128)(2,1)S(1)} %get-tuple-element.138), channel_id=1, source_target_pairs={{0,8},{1,9},{2,10},{3,11},{4,12},{5,13},{6,14},{7,15},{8,0},{9,1},... | collective-permute-start | bytes 221192 | tf_op jit(solution)/shard_map/ppermute | solution.py:739
  292.6 17.1 %collective-permute-start.10 = (bf16[48,768]{1,0:T(8,128)(2,1)S(1)}, bf16[48,768]{1,0:T(8,128)(2,1)S(1)}, u32[]{:S(2)}, u32[]{:S(2)}) collective-permute-start(bf16[48,768]{1,0:T(8,128)(2,1)S(1)} %get-tuple-element.139), channel_id=1, source_target_pairs={{0,12},{1,13},{2,14},{3,15},{4,8},{5,9},{6,10},{7,11},{8,4},{9,5},... | collective-permute-start | bytes 221192 | tf_op jit(solution)/shard_map/ppermute | solution.py:739
  294.1 8.7 %collective-permute-start.16 = (bf16[48,128]{1,0:T(8,128)(2,1)S(1)}, bf16[48,128]{1,0:T(8,128)(2,1)S(1)}, u32[]{:S(2)}, u32[]{:S(2)}) collective-permute-start(bf16[48,128]{1,0:T(8,128)(2,1)S(1)} %get-tuple-element.147), channel_id=1, source_target_pairs={{0,8},{1,9},{2,10},{3,11},{4,12},{5,13},{6,14},{7,15},{8,0},{9,1},... | collective-permute-start | bytes 36872 | tf_op jit(solution)/shard_map/ppermute | solution.py:739
  297.1 6.3 %collective-permute-start.17 = (bf16[48,128]{1,0:T(8,128)(2,1)S(1)}, bf16[48,128]{1,0:T(8,128)(2,1)S(1)}, u32[]{:S(2)}, u32[]{:S(2)}) collective-permute-start(bf16[48,128]{1,0:T(8,128)(2,1)S(1)} %get-tuple-element.148), channel_id=1, source_target_pairs={{0,12},{1,13},{2,14},{3,15},{4,8},{5,9},{6,10},{7,11},{8,4},{9,5},... | collective-permute-start | bytes 36872 | tf_op jit(solution)/shard_map/ppermute | solution.py:739
  303.4 15.4 %collective-permute-start.27 = (bf16[48,768]{1,0:T(8,128)(2,1)}, bf16[48,768]{1,0:T(8,128)(2,1)}, u32[]{:S(2)}, u32[]{:S(2)}) collective-permute-start(bf16[48,768]{1,0:T(8,128)(2,1)} %get-tuple-element.167), channel_id=1, source_target_pairs={{0,4},{1,5},{2,6},{3,7},{4,0},{5,1},{6,2},{7,3},{8,12},{9,13},{10,... | collective-permute-start | bytes 221192 | tf_op jit(solution)/shard_map/ppermute | solution.py:739
  304.0 15.2 %collective-permute-start.28 = (bf16[48,768]{1,0:T(8,128)(2,1)}, bf16[48,768]{1,0:T(8,128)(2,1)}, u32[]{:S(2)}, u32[]{:S(2)}) collective-permute-start(bf16[48,768]{1,0:T(8,128)(2,1)} %get-tuple-element.168), channel_id=1, source_target_pairs={{0,8},{1,9},{2,10},{3,11},{4,12},{5,13},{6,14},{7,15},{8,0},{9,1},... | collective-permute-start | bytes 221192 | tf_op jit(solution)/shard_map/ppermute | solution.py:739
  306.6 14.6 %collective-permute-start.29 = (bf16[48,768]{1,0:T(8,128)(2,1)}, bf16[48,768]{1,0:T(8,128)(2,1)}, u32[]{:S(2)}, u32[]{:S(2)}) collective-permute-start(bf16[48,768]{1,0:T(8,128)(2,1)} %get-tuple-element.169), channel_id=1, source_target_pairs={{0,12},{1,13},{2,14},{3,15},{4,8},{5,9},{6,10},{7,11},{8,4},{9,5},... | collective-permute-start | bytes 221192 | tf_op jit(solution)/shard_map/ppermute | solution.py:739
  309.7 13.9 %collective-permute-start.40 = (bf16[48,768]{1,0:T(8,128)(2,1)}, bf16[48,768]{1,0:T(8,128)(2,1)}, u32[]{:S(2)}, u32[]{:S(2)}) collective-permute-start(bf16[48,768]{1,0:T(8,128)(2,1)} %get-tuple-element.187), channel_id=1, source_target_pairs={{0,4},{1,5},{2,6},{3,7},{4,0},{5,1},{6,2},{7,3},{8,12},{9,13},{10,... | collective-permute-start | bytes 221192 | tf_op jit(solution)/shard_map/ppermute | solution.py:739
  310.3 31.4 %collective-permute-start.12 = (bf16[48,1536]{1,0:T(8,128)(2,1)}, bf16[48,1536]{1,0:T(8,128)(2,1)}, u32[]{:S(2)}, u32[]{:S(2)}) collective-permute-start(bf16[48,1536]{1,0:T(8,128)(2,1)} %get-tuple-element.140.b), channel_id=1, source_target_pairs={{0,16},{16,0},{1,17},{17,1},{2,18},{18,2},{3,19},{19,3},{4,20},{20... | collective-permute-start | bytes 442376 | tf_op jit(solution)/shard_map/ppermute | solution.py:743
  318.8 20.8 %collective-permute-start.18 = (bf16[48,128]{1,0:T(8,128)(2,1)S(1)}, bf16[48,128]{1,0:T(8,128)(2,1)S(1)}, u32[]{:S(2)}, u32[]{:S(2)}) collective-permute-start(bf16[48,128]{1,0:T(8,128)(2,1)S(1)} %vec_z.1.v), channel_id=1, source_target_pairs={{0,16},{16,0},{1,17},{17,1},{2,18},{18,2},{3,19},{19,3},{4,20},{20... | collective-permute-start | bytes 36872 | tf_op jit(solution)/shard_map/ppermute | solution.py:743
  319.3 17.3 %collective-permute-start.41 = (bf16[48,768]{1,0:T(8,128)(2,1)}, bf16[48,768]{1,0:T(8,128)(2,1)S(1)}, u32[]{:S(2)}, u32[]{:S(2)}) collective-permute-start(bf16[48,768]{1,0:T(8,128)(2,1)} %copy-done.46), channel_id=1, source_target_pairs={{0,8},{1,9},{2,10},{3,11},{4,12},{5,13},{6,14},{7,15},{8,0},{9,1},... | collective-permute-start | bytes 221192 | tf_op jit(solution)/shard_map/ppermute | solution.py:739
  321.2 15.8 %collective-permute-start.42 = (bf16[48,768]{1,0:T(8,128)(2,1)}, bf16[48,768]{1,0:T(8,128)(2,1)S(1)}, u32[]{:S(2)}, u32[]{:S(2)}) collective-permute-start(bf16[48,768]{1,0:T(8,128)(2,1)} %copy-done.45), channel_id=1, source_target_pairs={{0,12},{1,13},{2,14},{3,15},{4,8},{5,9},{6,10},{7,11},{8,4},{9,5},... | collective-permute-start | bytes 221192 | tf_op jit(solution)/shard_map/ppermute | solution.py:739
  323.6 16.4 %collective-permute-start.11 = (bf16[48,768]{1,0:T(8,128)(2,1)S(1)}, bf16[48,768]{1,0:T(8,128)(2,1)S(1)}, u32[]{:S(2)}, u32[]{:S(2)}) collective-permute-start(bf16[48,768]{1,0:T(8,128)(2,1)S(1)} %sum_z.3.a), channel_id=1, source_target_pairs={{0,16},{16,0},{1,17},{17,1},{2,18},{18,2},{3,19},{19,3},{4,20},{20... | collective-permute-start | bytes 221192 | tf_op jit(solution)/shard_map/ppermute | solution.py:743
  330.3 8.4 %copy-start.22 = (bf16[48,768]{1,0:T(8,128)(2,1)S(1)}, bf16[48,768]{1,0:T(8,128)(2,1)}, u32[]{:S(2)}) copy-start(bf16[48,768]{1,0:T(8,128)(2,1)} %copy-done.21) | copy-start | bytes 221188
  336.6 8.2 %collective-permute-start.31 = (bf16[48,1536]{1,0:T(8,128)(2,1)}, bf16[48,1536]{1,0:T(8,128)(2,1)S(1)}, u32[]{:S(2)}, u32[]{:S(2)}) collective-permute-start(bf16[48,1536]{1,0:T(8,128)(2,1)} %get-tuple-element.170.b), channel_id=1, source_target_pairs={{0,16},{16,0},{1,17},{17,1},{2,18},{18,2},{3,19},{19,3},{4,20},{20... | collective-permute-start | bytes 442376 | tf_op jit(solution)/shard_map/ppermute | solution.py:743
  337.0 9.5 %collective-permute-start.44 = (bf16[48,1536]{1,0:T(8,128)(2,1)}, bf16[48,1536]{1,0:T(8,128)(2,1)S(1)}, u32[]{:S(2)}, u32[]{:S(2)}) collective-permute-start(bf16[48,1536]{1,0:T(8,128)(2,1)} %get-tuple-element.190.b), channel_id=1, source_target_pairs={{0,16},{16,0},{1,17},{17,1},{2,18},{18,2},{3,19},{19,3},{4,20},{20... | collective-permute-start | bytes 442376 | tf_op jit(solution)/shard_map/ppermute | solution.py:743
  339.6 5.1 %collective-permute-start.30 = (bf16[48,768]{1,0:T(8,128)(2,1)S(1)}, bf16[48,768]{1,0:T(8,128)(2,1)S(1)}, u32[]{:S(2)}, u32[]{:S(2)}) collective-permute-start(bf16[48,768]{1,0:T(8,128)(2,1)S(1)} %sum_z.4.a), channel_id=1, source_target_pairs={{0,16},{16,0},{1,17},{17,1},{2,18},{18,2},{3,19},{19,3},{4,20},{20... | collective-permute-start | bytes 221192 | tf_op jit(solution)/shard_map/ppermute | solution.py:743
  340.1 6.5 %collective-permute-start.43 = (bf16[48,768]{1,0:T(8,128)(2,1)S(1)}, bf16[48,768]{1,0:T(8,128)(2,1)S(1)}, u32[]{:S(2)}, u32[]{:S(2)}) collective-permute-start(bf16[48,768]{1,0:T(8,128)(2,1)S(1)} %sum_z.5.a), channel_id=1, source_target_pairs={{0,16},{16,0},{1,17},{17,1},{2,18},{18,2},{3,19},{19,3},{4,20},{20... | collective-permute-start | bytes 221192 | tf_op jit(solution)/shard_map/ppermute | solution.py:743
  (33 other events, 77.5 us)
